TPU v7x, 512 devices: a whole 4x4x16 slice. The times are simulated.
512 devices in a mesh: section: 2 (over x_hi), dp: 8 (over y, core), tensor: 32 (over x_lo, z).
Axes of the slice: x: 4 (x_hi: 2, x_lo: 2; x = x_hi * 2 + x_lo), y: 4, z: 16, core: 2. Of those that a mesh axis runs over, the one named last changes fastest.
Arguments:
- tokens_in: bfloat16 [2, 7168, 2048], P(None, 'tensor', 'dp'), may hold values from -47 to 47
- section_proj: bfloat16 [2, 7168, 7168], P('section', 'tensor'), may hold values from -0.0625 to 0.0625
- section_gain: bfloat16 [2, 7168], P('section', 'tensor'), may hold values from 0.099609375 to 1.8984375
- final_gain: bfloat16 [7168], P('tensor'), may hold values from 0.099609375 to 1.8984375
- score_weight: bfloat16 [7168], P('tensor'), may hold values from -0.0625 to 0.0625
- labels: int32 [2, 2048], P(None, 'dp'), may hold values from 0 to 2
- loss_mask: int32 [2, 2048], P(None, 'dp'), may hold values 0 or 1
- segment_ids: int32 [2, 2048], P(None, 'dp'), may hold values from 0 to 15, never falling along the last dimension, each value on 1 to 512 neighbouring positions
Outputs:
- section_out: bfloat16 [2, 2, 7168, 2048], P('section', None, 'tensor', 'dp')
- segment_loss: float32 [2, 16], replicated
Inputs may be any that keep to these rules, and one draw needn't show every extreme that they name: `segment_ids`: within a micro-batch segment numbers never fall along the tokens; each segment has 1 to 512 tokens.
All inputs are finite; a program needn't handle non-finite values. No bound on the sum of `loss_mask` on one device may be relied on, other than what follows from the above.
Results may differ from a plain program's by a relative error of at most 0.0045.
Values may be sent and summed in bfloat16 or wider, within the bound.
No kernel may reach another device: no remote copies, remote signals or barrier semaphores. Data moves between devices by JAX's collectives and lax.ppermute only.
A program may use at most 64 MiB of HBM per device.

v0:
```python
import jax
import jax.numpy as jnp
from jax import lax
from jax.sharding import PartitionSpec as P

D = 7168
SEGS = 16


epsilon = 1e-05


def passed_along(shard, axis, by):
    count = lax.axis_size(axis)
    pairs = [(i, i + by) for i in range(count) if 0 <= i + by < count]
    return lax.ppermute(shard, axis, pairs)


def body(
    tokens_in, section_proj, section_gain, final_gain, score_weight, labels, loss_mask, segment_ids
):
    section_index = lax.axis_index("section")
    weight_local = section_proj[0]
    gain_local = section_gain[0]
    head_vector = final_gain.astype(jnp.float32) * score_weight.astype(jnp.float32)
    micro_count = tokens_in.shape[0]
    received = jnp.zeros_like(tokens_in[0])
    produced = []
    score_list = []
    for moment in range(micro_count + 1):
        if moment < micro_count:
            fresh_rows = tokens_in[moment]
        else:
            fresh_rows = jnp.zeros_like(tokens_in[0])
        incoming = jnp.where(section_index == 0, fresh_rows, received)
        apply_as_float = incoming.astype(jnp.float32)
        apply_squares = lax.psum(jnp.sum(apply_as_float * apply_as_float, axis=0), "tensor")
        apply_inv_root = lax.rsqrt(apply_squares / D + epsilon)[None, :]
        normed = (apply_as_float * apply_inv_root * gain_local.astype(jnp.float32)[:, None]).astype(
            jnp.bfloat16
        )
        mixed = jnp.dot(
            weight_local,
            lax.all_gather(normed, "tensor", axis=0, tiled=True),
            preferred_element_type=jnp.float32,
        )
        result_rows = (apply_as_float + jax.nn.silu(mixed)).astype(jnp.bfloat16)
        produced.append(result_rows)
        if moment < micro_count:
            received = passed_along(result_rows, "section", 1)
        if moment >= 1:
            as_float = result_rows.astype(jnp.float32)
            squares_part = jnp.sum(as_float * as_float, axis=0)
            squares = lax.psum(squares_part, "tensor")
            inv_root = lax.rsqrt(squares / D + epsilon)
            partial_score = jnp.sum(as_float * inv_root[None, :] * head_vector[:, None], axis=0)
            score_list.append(lax.psum(partial_score, "tensor"))
    section_out = jnp.where(
        section_index == 0, jnp.stack(produced[:micro_count]), jnp.stack(produced[1:])
    )[None]
    segment_range = lax.broadcasted_iota(jnp.int32, (1, SEGS), 1)
    sum_rows = []
    count_rows = []
    for micro in range(micro_count):
        target = labels[micro].astype(jnp.float32) - 1.0
        weight_mask = loss_mask[micro].astype(jnp.float32)
        offset_err = score_list[micro] - target
        squared = weight_mask * offset_err * offset_err
        member = (segment_ids[micro][:, None] == segment_range).astype(jnp.float32)
        sum_rows.append(jnp.dot(squared, member, precision=lax.Precision.HIGHEST))
        count_rows.append(jnp.dot(weight_mask, member, precision=lax.Precision.HIGHEST))
    live_section = (section_index == 1).astype(jnp.float32)
    loss_sums, counted = lax.psum(
        (jnp.stack(sum_rows) * live_section, jnp.stack(count_rows) * live_section),
        ("section", "dp"),
    )
    segment_loss = loss_sums / jnp.maximum(counted, 1.0)
    return (section_out, segment_loss)


def solution(mesh):
    in_specs = (
        P(None, "tensor", "dp"),
        P("section", "tensor", None),
        P("section", "tensor"),
        P("tensor"),
        P("tensor"),
        P(None, "dp"),
        P(None, "dp"),
        P(None, "dp"),
    )
    out_specs = (P("section", None, "tensor", "dp"), P())
    return jax.shard_map(body, mesh=mesh, in_specs=in_specs, out_specs=out_specs, check_vma=False)
```

profile of v0, /device:TPU:1, one launch (start us, length us, event | category | flops | bytes accessed | tf_op | source)
XLA Modules:
  0.0 791.1 jit_solution(1438535462206001825)
XLA Ops:
  7.2 1.1 fusion.29
  8.3 57.2 %psum.63 = f32[256]{0:T(256)S(1)} all-reduce(f32[256]{0:T(256)S(1)} %fusion.29), channel_id=1, replica_groups=mesh['section'=2,'dp'=8,'tensor'=32] {'tensor'}, use_global_device_ids=true, to_apply=%region_1.2 | all-reduce | flops 256 | bytes 2048 | tf_op jit(solution)/shard_map/psum | solution.py:37
  66.8 1.6 fusion.31
  68.5 124.1 %all-gather.4.cloned.1.call-done = bf16[7168,256]{1,0:T(8,128)(2,1)} async-done(((bf16[224,256]{1,0:T(8,128)(2,1)}), bf16[7168,256]{1,0:T(8,128)(2,1)}) %all-gather.4.cloned.1.call-update) | async-done | bytes 3670032 | tf_op jit(solution)/shard_map/all_gather | solution.py:44
  192.6 3.1 fusion.32
  195.7 3.6 collective-permute-start
  199.3 2.0 collective-permute-done
  201.9 49.3 %psum.64 = f32[256]{0:T(256)S(1)} all-reduce(f32[256]{0:T(256)} %get-tuple-element.10), channel_id=1, replica_groups=mesh['section'=2,'dp'=8,'tensor'=32] {'tensor'}, use_global_device_ids=true, to_apply=%region_3.4 | all-reduce | flops 256 | bytes 2048 | tf_op jit(solution)/shard_map/psum | solution.py:37
  251.2 1.4 fusion.23
  252.7 144.1 %all-gather.6.cloned.1.call-done = bf16[7168,256]{1,0:T(8,128)(2,1)} async-done(((bf16[224,256]{1,0:T(8,128)(2,1)}), bf16[7168,256]{1,0:T(8,128)(2,1)}) %all-gather.6.cloned.1.call-update) | async-done | bytes 3670032 | tf_op jit(solution)/shard_map/all_gather | solution.py:44
  396.8 3.6 fusion.15
  400.5 3.6 collective-permute-start.1
  404.1 2.0 collective-permute-done.1
  406.1 49.3 %psum.65 = f32[256]{0:T(256)S(1)} all-reduce(f32[256]{0:T(256)S(1)} %fusion.25), channel_id=1, replica_groups=mesh['section'=2,'dp'=8,'tensor'=32] {'tensor'}, use_global_device_ids=true, to_apply=%region_5.6 | all-reduce | flops 256 | bytes 2048 | tf_op jit(solution)/shard_map/psum | solution.py:37
  455.4 1.4 fusion.27
  456.8 0.8 fusion.49
  458.1 0.9 fusion.39
  459.0 0.9 fusion.41
  460.5 1.2 convert_multiply_fusion.10
  461.7 1.4 slice_convert_fusion.1
  463.1 1.4 convert_add_fusion.4
  464.5 136.4 %all-gather.8.cloned.1.call-done = bf16[7168,256]{1,0:T(8,128)(2,1)} async-done(((bf16[224,256]{1,0:T(8,128)(2,1)}), bf16[7168,256]{1,0:T(8,128)(2,1)}) %all-gather.8.cloned.1.call-update) | async-done | bytes 3670032 | tf_op jit(solution)/shard_map/all_gather | solution.py:44
  600.9 3.6 fusion.18
  604.5 48.4 %all-reduce.1 = (f32[256]{0:T(256)S(1)}, f32[256]{0:T(256)S(1)}) all-reduce(f32[256]{0:T(256)} %get-tuple-element.18, f32[256]{0:T(256)} %get-tuple-element.20), channel_id=1, replica_groups=mesh['section'=2,'dp'=8,'tensor'=32] {'tensor'}, use_global_device_ids=true, to_apply=%region_7.8 | all-reduce | flops 512 | bytes 4096 | tf_op jit(solution)/shard_map/psum | solution.py:54
  653.0 0.7 fusion.17
  653.7 46.4 %all-reduce = (f32[256]{0:T(256)S(1)}, f32[256]{0:T(256)S(1)}) all-reduce(f32[256]{0:T(256)S(1)} %get-tuple-element.3, f32[256]{0:T(256)S(1)} %get-tuple-element.2), channel_id=1, replica_groups=mesh['section'=2,'dp'=8,'tensor'=32] {'tensor'}, use_global_device_ids=true, to_apply=%region_13.14 | all-reduce | flops 512 | bytes 4096 | tf_op jit(solution)/shard_map/psum | solution.py:57
  700.1 0.7 multiply_multiply_fusion.1
  700.8 0.9 fusion.42
  701.6 0.7 multiply_multiply_fusion
  702.3 0.8 fusion.40
  703.2 79.2 %all-reduce.2 = (f32[2,16]{1,0:T(2,128)S(1)}, f32[2,16]{1,0:T(2,128)S(1)}) all-reduce(f32[2,16]{1,0:T(2,128)S(1)} %maximum_multiply_fusion, f32[2,16]{1,0:T(2,128)} %maximum_multiply_fusion.1), channel_id=1, replica_groups=mesh['section'=2,'dp'=8,'tensor'=32] {'section','dp'}, use_global_device_ids=true, to_apply=%region_14.15 | all-reduce | flops 64 | bytes 512 | tf_op jit(solution)/shard_map/psum | solution.py:73
  782.9 1.6 maximum_select_fusion
  (28 shorter events, 3.8 us)
Async XLA Ops:
  7.2 185.4 %copy-start = (bf16[1,224,7168]{2,1,0:T(8,128)(2,1)S(1)}, bf16[1,224,7168]{2,1,0:T(8,128)(2,1)}, u32[]{:S(2)}) copy-start(bf16[1,224,7168]{2,1,0:T(8,128)(2,1)} %param.9) | copy-start | bytes 9633796
  7.2 185.4 %all-gather.4.cloned.1.call-start = ((), (), s32[]{:S(2)}) async-start(), calls=%async_computation | async-start | bytes 3784704 | tf_op jit(solution)/shard_map/all_gather | solution.py:44
  66.2 0.5 copy-start.3
  68.4 132.9 %copy-start.1 = (bf16[2,224,256]{2,1,0:T(8,128)(2,1)S(1)}, bf16[2,224,256]{2,1,0:T(8,128)(2,1)}, u32[]{:S(2)}) copy-start(bf16[2,224,256]{2,1,0:T(8,128)(2,1)} %param.8) | copy-start | bytes 688132
  68.5 328.4 %all-gather.6.cloned.1.call-start = ((), (), s32[]{:S(2)}) async-start(), calls=%async_computation.1 | async-start | bytes 3784704 | tf_op jit(solution)/shard_map/all_gather | solution.py:44
  195.7 6.3 copy-start.2
  195.7 5.6 collective-permute-start
  252.6 348.3 %all-gather.8.cloned.1.call-start = ((), (), s32[]{:S(2)}) async-start(), calls=%async_computation.2 | async-start | bytes 3784704 | tf_op jit(solution)/shard_map/all_gather | solution.py:44
  400.5 5.6 collective-permute-start.1
  457.6 0.5 copy-start.4
  457.6 1.4 copy-start.5
Sparse Core Ops, SparseCore 0:
  68.6 123.9 all-gather.3
  252.7 144.0 all-gather.5
  456.9 143.8 all-gather.7
where the time goes:
time: 792 us; the launch traced here: 791 us
  waiting for transfers between devices  409 us (52%)
  blocking collectives  330 us (42%)
  other arithmetic  15.7 us (2%)
  matrix products  13.9 us (2%)
  between operations  13.8 us (2%)
    all_gather x3, waiting for transfers between devices, body(): lax.all_gather(normed, 'tensor', axis=0, tiled=True)  405 us
    psum x3, blocking collectives, body(): lax.psum(jnp.sum(apply_as_float * apply_as_float, axis=0), 'tensor')  156 us
    psum x1, blocking collectives, body(): lax.psum((jnp.stack(sum_rows) * live_section, jnp.stack(count_rows) * liv...  79.2 us
    psum x1, blocking collectives, body(): squares = lax.psum(squares_part, 'tensor')  48.4 us
    psum x1, blocking collectives, body(): score_list.append(lax.psum(partial_score, 'tensor'))  46.4 us
  transfers between devices with their start and end apart: 5, of which 5 were waited for; matrix products, arithmetic and copies ran while one was open for 1% of the time, Pallas kernels for 0%

commit v1 on v0

v1 whole, which is shorter than its diff:
```python
import jax
import jax.numpy as jnp
from jax import lax
from jax.experimental import pallas as pl
from jax.experimental.pallas import tpu as pltpu
from jax.sharding import Mesh
from jax.sharding import PartitionSpec as P

D = 7168
SEGS = 16
EPS = 1e-05
F = 224
T = 256
KH = D // 2
R = 240
HALF = F // 2
F32 = jnp.float32
BF16 = jnp.bfloat16
Z = ("h", "p")
VMEM_LIMIT = 40 * 1024 * 1024


def vmem():
    return pl.BlockSpec(memory_space=pltpu.VMEM)


def smem():
    return pl.BlockSpec(memory_space=pltpu.SMEM)


def anywhere():
    return pl.BlockSpec(memory_space=pl.ANY)


def pack_block(rows, gain, block_ref):
    block_ref[0:F, :] = (rows * gain).astype(BF16)
    squares = jnp.sum(rows * rows, axis=0, keepdims=True)
    first = squares.astype(BF16)
    rest = squares - first.astype(F32)
    second = rest.astype(BF16)
    third = (rest - second.astype(F32)).astype(BF16)
    at = lax.broadcasted_iota(jnp.int32, (R - F, T), 0)
    tail = jnp.where(at == 0, first.astype(F32), 0.0)
    tail = jnp.where(at == 1, second.astype(F32), tail)
    tail = jnp.where(at == 2, third.astype(F32), tail)
    block_ref[F:R, :] = tail.astype(BF16)


def pack_kernel(rows_ref, gain_ref, block_ref):
    pack_block(rows_ref[...].astype(F32), gain_ref[...].astype(F32), block_ref)


def pack(rows, gain):
    return pl.pallas_call(
        pack_kernel,
        out_shape=jax.ShapeDtypeStruct((R, T), BF16),
        in_specs=[vmem(), vmem()],
        out_specs=vmem(),
        name="pack",
    )(rows, gain)


def product_kernel(
    local_block, at_ref, same_ref, below_ref, above_ref, weight_ref, side_ref, side2_ref,
    over_ref, over2_ref, cross_ref, cross2_ref, own_ref, send_ref, held, values, sems,
):
    section, x, core, parity = at_ref[0], at_ref[1], at_ref[2], at_ref[3]
    columns = pl.ds(pl.multiple_of(x * KH, 128), KH)
    mine = pl.ds(pl.multiple_of(core * HALF, 16), HALF)
    theirs = pl.ds(pl.multiple_of((1 - core) * HALF, 16), HALF)
    far = pl.ds(pl.multiple_of(F + core * HALF, 16), HALF)
    far2 = pl.ds(pl.multiple_of(F + (1 - core) * HALF, 16), HALF)

    def near_copies():
        return [
            pltpu.make_async_copy(weight_ref.at[:, columns], held.at[0:F, :], sems.at[0]),
            pltpu.make_async_copy(side_ref, held.at[far, :], sems.at[1]),
            pltpu.make_async_copy(side2_ref, held.at[far2, :], sems.at[2]),
        ]

    def away_copies():
        return [
            pltpu.make_async_copy(over_ref, held.at[mine, :], sems.at[0]),
            pltpu.make_async_copy(over2_ref, held.at[theirs, :], sems.at[1]),
            pltpu.make_async_copy(cross_ref, held.at[far, :], sems.at[2]),
            pltpu.make_async_copy(cross2_ref, held.at[far2, :], sems.at[3]),
        ]

    @pl.when(section == local_block)
    def _():
        for copy in near_copies():
            copy.start()

    @pl.when(section != local_block)
    def _():
        for copy in away_copies():
            copy.start()

    squares = jnp.zeros((1, T), F32)
    for i in range(8):
        got = same_ref[i]
        here = pl.ds(pl.multiple_of((2 * i + parity) * F, 16), F)
        values[here, :] = got[0:F]
        squares += jnp.sum(got[F:R].astype(F32), axis=0, keepdims=True)
        other = below_ref[i] if i < 4 else above_ref[i - 4]
        there = pl.ds(pl.multiple_of((2 * i + 1 - parity) * F, 16), F)
        values[there, :] = other[0:F]
        squares += jnp.sum(other[F:R].astype(F32), axis=0, keepdims=True)

    @pl.when(section == local_block)
    def _():
        for copy in near_copies():
            copy.wait()

    @pl.when(section != local_block)
    def _():
        for copy in away_copies():
            copy.wait()

    product = jnp.dot(held[...], values[...], preferred_element_type=F32)
    rows = jnp.broadcast_to(squares, (8, T))
    own_ref[0:F, :] = product[0:F]
    own_ref[F:F + 8, :] = rows
    send_ref[0:F, :] = product[F:2 * F]
    send_ref[F:F + 8, :] = rows


def product(local_block, at, same, below, above, weight, received):
    import functools
    out = jax.ShapeDtypeStruct((F + 8, T), F32)
    return pl.pallas_call(
        functools.partial(product_kernel, local_block),
        out_shape=(out, out),
        in_specs=[smem(), vmem(), vmem(), vmem()] + [anywhere()] * 7,
        out_specs=(vmem(), vmem()),
        scratch_shapes=[
            pltpu.VMEM((2 * F, KH), BF16),
            pltpu.VMEM((KH, T), BF16),
            pltpu.SemaphoreType.DMA((4,)),
        ],
        compiler_params=pltpu.CompilerParams(vmem_limit_bytes=VMEM_LIMIT),
        name="product",
    )(at, same, below, above, weight, *received)


def block_rows(own_ref, other_ref, rows_ref):
    squares = own_ref[F:F + 1, :] + other_ref[F:F + 1, :]
    inv_root = lax.rsqrt(squares / D + EPS)
    mixed = (own_ref[0:F, :] + other_ref[0:F, :]) * inv_root
    gated = mixed / (1.0 + jnp.exp(-mixed))
    return (rows_ref[...].astype(F32) + gated).astype(BF16)


def middle_kernel(own_ref, other_ref, rows_ref, gain_ref, out_ref, block_ref):
    out = block_rows(own_ref, other_ref, rows_ref)
    out_ref[...] = out
    pack_block(out.astype(F32), gain_ref[...].astype(F32), block_ref)


def middle(own, other, rows, gain):
    return pl.pallas_call(
        middle_kernel,
        out_shape=(jax.ShapeDtypeStruct((F, T), BF16), jax.ShapeDtypeStruct((R, T), BF16)),
        in_specs=[vmem()] * 4,
        out_specs=(vmem(), vmem()),
        name="middle",
    )(own, other, rows, gain)


def last_kernel(at_ref, own_ref, other_ref, rows_ref, head_ref, out_ref, swap_ref, stats_ref):
    out = block_rows(own_ref, other_ref, rows_ref)
    out_ref[...] = out
    @pl.when(at_ref[0] == 0)
    def _():
        swap_ref[...] = out

    @pl.when(at_ref[0] != 0)
    def _():
        swap_ref[...] = rows_ref[...]

    as_float = out.astype(F32)
    head = head_ref[...]
    squares = jnp.sum(as_float * as_float, axis=0, keepdims=True)
    scores = jnp.sum(as_float * head, axis=0, keepdims=True)
    stats = jnp.concatenate([squares, scores], axis=0)
    for i in range(32):
        stats_ref[i] = stats


def last(at, own, other, rows, head):
    out = jax.ShapeDtypeStruct((F, T), BF16)
    return pl.pallas_call(
        last_kernel,
        out_shape=(out, out, jax.ShapeDtypeStruct((32, 2, T), F32)),
        in_specs=[smem()] + [vmem()] * 4,
        out_specs=(vmem(), vmem(), vmem()),
        name="last",
    )(at, own, other, rows, head)


def loss_kernel(stats_ref, label_ref, mask_ref, segment_ref, sums_ref):
    total = jnp.sum(stats_ref[...], axis=0)
    inv_root = lax.rsqrt(total[0:1] / D + EPS)
    score = total[1:2] * inv_root
    target = label_ref[...].astype(F32) - 1.0
    mask = mask_ref[...].astype(F32)
    err = score - target
    squared = mask * err * err
    member = segment_ref[...] == lax.broadcasted_iota(jnp.int32, (SEGS, T), 0)
    sums = jnp.sum(jnp.where(member, squared, 0.0), axis=1, keepdims=True)
    counts = jnp.sum(jnp.where(member, mask, 0.0), axis=1, keepdims=True)
    lane = lax.broadcasted_iota(jnp.int32, (SEGS, 128), 1)
    sums_ref[...] = jnp.where(lane == 0, sums, jnp.where(lane == 1, counts, 0.0))


def loss_parts(stats, label, mask, segment):
    return pl.pallas_call(
        loss_kernel,
        out_shape=jax.ShapeDtypeStruct((SEGS, 128), F32),
        in_specs=[vmem()] * 4,
        out_specs=vmem(),
        name="loss_parts",
    )(stats, label, mask, segment)


def swapped(value, *axes):
    count = 2 ** len(axes)
    name = axes if len(axes) > 1 else axes[0]
    return lax.ppermute(value, name, [(i, i ^ (count - 1)) for i in range(count)])


def shifted(value, by):
    return lax.ppermute(value, Z, [(i, (i + by) % 16) for i in range(16)])


def gathered(block):
    same = lax.all_gather(block, "h", axis=0, tiled=False)
    return same, shifted(same[0:4], 1), shifted(same[4:8], -1)


def body(
    tokens_in, section_proj, section_gain, final_gain, score_weight, labels, loss_mask, segment_ids
):
    section = lax.axis_index("s")
    x = lax.axis_index("x")
    core = lax.axis_index("c")
    at = jnp.stack([section, x, core, lax.axis_index("p")]).astype(jnp.int32)
    weight = section_proj[0]

    gain = section_gain[0][:, None]
    gain_away = swapped(gain, "s")
    gain0 = jnp.where(section == 0, gain, gain_away)
    gain1 = jnp.where(section == 0, gain_away, gain)

    half = lax.dynamic_slice(weight, (core * HALF, 0), (HALF, D))
    near = lax.dynamic_slice(half, (0, x * KH), (HALF, KH))
    far = lax.dynamic_slice(half, (0, (1 - x) * KH), (HALF, KH))
    side = swapped(far, "x")
    over = swapped(near, "s")
    cross = swapped(far, "s", "x")

    rows = lax.dynamic_index_in_dim(tokens_in, section, 0, keepdims=False)
    same, below, above = gathered(pack(rows, gain0))

    side, over, cross, same = lax.optimization_barrier((side, over, cross, same))
    received = (
        side, swapped(side, "c"), over, swapped(over, "c"), cross, swapped(cross, "c")
    )
    own, send = product(0, at, same, below, above, weight, received)
    first, block = middle(own, swapped(send, "x"), rows, gain1)

    same, below, above = gathered(block)
    own, send = product(1, at, same, below, above, weight, received)
    head = (final_gain.astype(F32) * score_weight.astype(F32))[:, None]
    second, handed, stats = last(at, own, swapped(send, "x"), first, head)
    handed = swapped(handed, "s")

    stats = lax.all_to_all(stats, ("x", "h", "p"), 0, 0, tiled=True)
    pick = lambda value: lax.dynamic_slice(value, (section, 0), (1, T))
    parts = loss_parts(stats, pick(labels), pick(loss_mask), pick(segment_ids))
    parts = jnp.broadcast_to(parts[None, :, 0:2], (16, SEGS, 2))
    parts = lax.all_to_all(parts, ("s", "y", "c"), 0, 0, tiled=True)
    parts = jnp.sum(parts.reshape(2, 8, SEGS, 2), axis=1)
    segment_loss = parts[..., 0] / jnp.maximum(parts[..., 1], 1.0)

    section_out = jnp.where(section == 0, jnp.stack([first, handed]), jnp.stack([handed, second]))
    return section_out[None], segment_loss


def solution(mesh):
    finer = Mesh(mesh.devices.reshape(2, 4, 2, 2, 8, 2), ("s", "y", "c", "x", "h", "p"))
    tensor = ("x", "h", "p")
    dp = ("y", "c")
    in_specs = (
        P(None, tensor, dp),
        P("s", tensor, None),
        P("s", tensor),
        P(tensor),
        P(tensor),
        P(None, dp),
        P(None, dp),
        P(None, dp),
    )
    out_specs = (P("s", None, tensor, dp), P())
    return jax.shard_map(body, mesh=finer, in_specs=in_specs, out_specs=out_specs, check_vma=False)
```

time: 792 us -> 239 us (0.30)
  waiting for transfers between devices: 409 us -> 69.4 us
  blocking collectives: 330 us -> 63.9 us
  starting transfers between devices: 7.31 us -> 71.1 us
  Pallas kernels: 0 us -> 15.1 us
  matrix products: 13.9 us -> 0 us
  between operations: 13.8 us -> 0.97 us
  other arithmetic: 15.7 us -> 3.01 us
  local copies, waits for them, and re-layouts: 1.85 us -> 14.3 us
    all_gather x3 -> x0, waiting for transfers between devices: 405 us -> none  [body(): lax.all_gather(normed, 'tensor', axis=0, tiled=True)]
    psum x6 -> x0, blocking collectives: 330 us -> none  [the longest x3 156 us: body(): lax.psum(jnp.sum(apply_as_float * apply_as_float, axis=0), 'tensor')]
    all_gather x0 -> x2, blocking collectives: none -> 63.9 us  [gathered(): same = lax.all_gather(block, 'h', axis=0, tiled=False)]
    ppermute x2 -> x14, waiting for transfers between devices: 4.04 us -> 55.4 us  [the longest x10 36.9 us: swapped(): return lax.ppermute(value, name, [(i, i ^ count - 1) for i in range(count)])]
    ppermute x2 -> x14, starting transfers between devices: 7.19 us -> 48.4 us  [the longest x10 34.7 us: swapped(): return lax.ppermute(value, name, [(i, i ^ count - 1) for i in range(count)])]
    all_to_all x0 -> x2, starting transfers between devices: none -> 22.7 us  [the longest x1 16.8 us: body(): parts = lax.all_to_all(parts, ('s', 'y', 'c'), 0, 0, tiled=True)]
    pallas_call x0 -> x6, Pallas kernels: none -> 15.1 us  [the longest x2 7.9 us: product(): pl.pallas_call(functools.partial(product_kernel, local_block), out_shape=...]
    all_to_all x0 -> x2, waiting for transfers between devices: none -> 14 us  [the longest x1 8.43 us: body(): stats = lax.all_to_all(stats, ('x', 'h', 'p'), 0, 0, tiled=True)]
  transfers between devices with their start and end apart: 5 -> 16, of which waited for: 5 -> 9; matrix products, arithmetic and copies ran while one was open for 1% -> 3% of each run, Pallas kernels for 0% -> 1%
where the time goes in v1:
time: 239 us; the launch traced here: 238 us
  starting transfers between devices  71.1 us (30%)
  waiting for transfers between devices  69.4 us (29%)
  blocking collectives  63.9 us (27%)
  Pallas kernels  15.1 us (6%)
  local copies, waits for them, and re-layouts  14.3 us (6%)
  other arithmetic  3.01 us (1%)
    all_gather x2, blocking collectives, gathered(): same = lax.all_gather(block, 'h', axis=0, tiled=False)  63.9 us
    ppermute x10, waiting for transfers between devices, swapped(): return lax.ppermute(value, name, [(i, i ^ count - 1) for i in range(count)])  36.9 us
    ppermute x10, starting transfers between devices, swapped(): return lax.ppermute(value, name, [(i, i ^ count - 1) for i in range(count)])  34.7 us
    ppermute x4, waiting for transfers between devices, shifted(): return lax.ppermute(value, Z, [(i, (i + by) % 16) for i in range(16)])  18.5 us
    all_to_all x1, starting transfers between devices, body(): parts = lax.all_to_all(parts, ('s', 'y', 'c'), 0, 0, tiled=True)  16.8 us
    ppermute x4, starting transfers between devices, shifted(): return lax.ppermute(value, Z, [(i, (i + by) % 16) for i in range(16)])  13.7 us
    all_to_all x1, waiting for transfers between devices, body(): stats = lax.all_to_all(stats, ('x', 'h', 'p'), 0, 0, tiled=True)  8.43 us
    pallas_call x2, Pallas kernels, product(): pl.pallas_call(functools.partial(product_kernel, local_block), out_shape=...  7.9 us
  transfers between devices with their start and end apart: 16, of which 9 were waited for; matrix products, arithmetic and copies ran while one was open for 3% of the time, Pallas kernels for 1%

profile of v1, /device:TPU:1, one launch (start us, length us, event | category | flops | bytes accessed | tf_op | source)
XLA Modules:
  0.0 237.8 jit_solution(14881614137796562172)
XLA Ops:
  0.7 3.5 %dynamic-slice_bitcast_fusion = (bf16[112,3584]{1,0:T(8,128)(2,1)}, bf16[112,3584]{1,0:T(8,128)(2,1)}) fusion(bf16[1,224,7168]{2,1,0:T(8,128)(2,1)} %param.9, s32[]{:T(128)S(6)} %select_n.51, s32[]{:T(128)S(6)} %select_n.55, s32[]{:T(128)S(6)} %select_n.53), kind=kLoop, calls=%fused_computation | loop fusion | bytes 3211276 | tf_op jit(solution)/shard_map/dynamic_slice | solution.py:256
  4.2 3.9 %collective-permute-start = (bf16[112,3584]{1,0:T(8,128)(2,1)}, bf16[112,3584]{1,0:T(8,128)(2,1)}, u32[]{:S(2)}, u32[]{:S(2)}) collective-permute-start(bf16[112,3584]{1,0:T(8,128)(2,1)} %get-tuple-element.29), channel_id=1, source_target_pairs={{0,16},{16,0},{1,17},{17,1},{2,18},{18,2},{3,19},{19,3},{4,20},{20... | collective-permute-start | bytes 2408456 | tf_op jit(solution)/shard_map/ppermute | solution.py:229
  8.1 4.4 %collective-permute-start.1 = (bf16[112,3584]{1,0:T(8,128)(2,1)}, bf16[112,3584]{1,0:T(8,128)(2,1)}, u32[]{:S(2)}, u32[]{:S(2)}) collective-permute-start(bf16[112,3584]{1,0:T(8,128)(2,1)} %get-tuple-element.28), channel_id=1, source_target_pairs={{0,256},{256,0},{1,257},{257,1},{2,258},{258,2},{3,259},{259,3},{4... | collective-permute-start | bytes 2408456 | tf_op jit(solution)/shard_map/ppermute | solution.py:229
  12.5 1.9 collective-permute-start.2
  14.6 3.6 %collective-permute-start.3 = (bf16[224,1]{1,0:T(8,128)(2,1)S(1)}, bf16[224,1]{1,0:T(8,128)(2,1)S(1)}, u32[]{:S(2)}, u32[]{:S(2)}) collective-permute-start(bf16[224,1]{1,0:T(8,128)(2,1)S(1)} %copy.20), channel_id=1, source_target_pairs={{0,256},{256,0},{1,257},{257,1},{2,258},{258,2},{3,259},{259,3},{4... | collective-permute-start | bytes 1352 | tf_op jit(solution)/shard_map/ppermute | solution.py:229
  18.9 27.7 %collective-permute-done.3 = bf16[224,1]{1,0:T(8,128)(2,1)S(1)} collective-permute-done((bf16[224,1]{1,0:T(8,128)(2,1)S(1)}, bf16[224,1]{1,0:T(8,128)(2,1)S(1)}, u32[]{:S(2)}, u32[]{:S(2)}) %collective-permute-start.3) | collective-permute-done | bytes 480 | tf_op jit(solution)/shard_map/ppermute | solution.py:229
  48.9 36.4 %all-gather = bf16[1920,256]{1,0:T(8,128)(2,1)S(1)} all-gather(bf16[240,256]{1,0:T(8,128)(2,1)} %pack.1), channel_id=2, replica_groups=mesh['s'=2,'y'=4,'c'=2,'x'=2,'h'=8,'p'=2] {'h'}, dimensions={0}, use_global_device_ids=true | all-gather | bytes 1105920 | tf_op jit(solution)/shard_map/all_gather | solution.py:237
  85.3 7.8 %collective-permute-start.6 = (bf16[112,3584]{1,0:T(8,128)(2,1)}, bf16[112,3584]{1,0:T(8,128)(2,1)}, u32[]{:S(2)}, u32[]{:S(2)}) collective-permute-start(bf16[112,3584]{1,0:T(8,128)(2,1)} %collective-permute-done.side_ref), channel_id=1, source_target_pairs={{0,32},{32,0},{1,33},{33,1},{2,34},{34,2},{3,35},{35,3},{4,36},{36... | collective-permute-start | bytes 2408456 | tf_op jit(solution)/shard_map/ppermute | solution.py:229
  93.1 1.9 collective-permute-start.7
  95.0 2.4 %collective-permute-start.8 = (bf16[112,3584]{1,0:T(8,128)(2,1)}, bf16[112,3584]{1,0:T(8,128)(2,1)}, u32[]{:S(2)}, u32[]{:S(2)}) collective-permute-start(bf16[112,3584]{1,0:T(8,128)(2,1)} %collective-permute-done.2.cross_ref), channel_id=1, source_target_pairs={{0,32},{32,0},{1,33},{33,1},{2,34},{34,2},{3,35},{35,3},{4,36},{36... | collective-permute-start | bytes 2408456 | tf_op jit(solution)/shard_map/ppermute | solution.py:229
  99.4 2.4 %collective-permute-start.4 = (bf16[4,240,256]{2,1,0:T(8,128)(2,1)}, bf16[4,240,256]{2,1,0:T(8,128)(2,1)}, u32[]{:S(2)}, u32[]{:S(2)}) collective-permute-start(bf16[4,240,256]{2,1,0:T(8,128)(2,1)} %bitcast.9), channel_id=1, source_target_pairs={{0,1},{1,2},{2,3},{3,4},{4,5},{5,6},{6,7},{7,8},{8,9},{9,10},{10,1... | collective-permute-start | bytes 1474568 | tf_op jit(solution)/shard_map/ppermute | solution.py:233
  101.8 4.1 %collective-permute-start.5 = (bf16[4,240,256]{2,1,0:T(8,128)(2,1)}, bf16[4,240,256]{2,1,0:T(8,128)(2,1)}, u32[]{:S(2)}, u32[]{:S(2)}) collective-permute-start(bf16[4,240,256]{2,1,0:T(8,128)(2,1)} %bitcast.10), channel_id=1, source_target_pairs={{0,15},{1,0},{2,1},{3,2},{4,3},{5,4},{6,5},{7,6},{8,7},{9,8},{10,9... | collective-permute-start | bytes 1474568 | tf_op jit(solution)/shard_map/ppermute | solution.py:233
  106.0 9.7 %collective-permute-done.4.below_ref = bf16[4,240,256]{2,1,0:T(8,128)(2,1)} collective-permute-done((bf16[4,240,256]{2,1,0:T(8,128)(2,1)}, bf16[4,240,256]{2,1,0:T(8,128)(2,1)}, u32[]{:S(2)}, u32[]{:S(2)}) %collective-permute-start.4) | collective-permute-done | bytes 491552 | tf_op jit(solution)/shard_map/ppermute | solution.py:233
  117.8 3.7 %product.2 = (f32[232,256]{1,0:T(8,128)S(1)}, f32[232,256]{1,0:T(8,128)S(1)}) custom-call(s32[4]{0:T(128)S(1)} %pad_add_fusion.at_ref, bf16[8,240,256]{2,1,0:T(8,128)(2,1)S(1)} %bitcast.28, bf16[4,240,256]{2,1,0:T(8,128)(2,1)} %collective-permute-done.4.below_ref, bf16[4,240,256]{2,1,0:T(8,128)(2,1)} %collective-permute-done.5.above_ref, ...), custom_call_target="tpu_custom_call" | custom-call | tf_op jit(solution)/shard_map/product/pallas_call | solution.py:131
  122.2 1.9 collective-permute-start.9
  124.2 6.1 %collective-permute-done.9.other_ref = f32[232,256]{1,0:T(8,128)S(1)} collective-permute-done((f32[232,256]{1,0:T(8,128)S(1)}, f32[232,256]{1,0:T(8,128)S(1)}, u32[]{:S(2)}, u32[]{:S(2)}) %collective-permute-start.9) | collective-permute-done | bytes 237600 | tf_op jit(solution)/shard_map/ppermute | solution.py:229
  131.0 2.0 middle.1
  132.9 27.6 %all-gather.1 = bf16[1920,256]{1,0:T(8,128)(2,1)S(1)} all-gather(bf16[240,256]{1,0:T(8,128)(2,1)} %get-tuple-element.22), channel_id=3, replica_groups=mesh['s'=2,'y'=4,'c'=2,'x'=2,'h'=8,'p'=2] {'h'}, dimensions={0}, use_global_device_ids=true | all-gather | bytes 1105920 | tf_op jit(solution)/shard_map/all_gather | solution.py:237
  160.5 5.3 %collective-permute-start.10 = (bf16[4,240,256]{2,1,0:T(8,128)(2,1)S(1)}, bf16[4,240,256]{2,1,0:T(8,128)(2,1)S(1)}, u32[]{:S(2)}, u32[]{:S(2)}) collective-permute-start(bf16[4,240,256]{2,1,0:T(8,128)(2,1)S(1)} %bitcast.31), channel_id=1, source_target_pairs={{0,1},{1,2},{2,3},{3,4},{4,5},{5,6},{6,7},{7,8},{8,9},{9,10},{10,1... | collective-permute-start | bytes 1474568 | tf_op jit(solution)/shard_map/ppermute | solution.py:233
  165.8 1.9 collective-permute-start.11
  167.8 4.8 %collective-permute-done.10.below_ref = bf16[4,240,256]{2,1,0:T(8,128)(2,1)S(1)} collective-permute-done((bf16[4,240,256]{2,1,0:T(8,128)(2,1)S(1)}, bf16[4,240,256]{2,1,0:T(8,128)(2,1)S(1)}, u32[]{:S(2)}, u32[]{:S(2)}) %collective-permute-start.10) | collective-permute-done | bytes 491552 | tf_op jit(solution)/shard_map/ppermute | solution.py:233
  172.6 3.1 %collective-permute-done.11.above_ref = bf16[4,240,256]{2,1,0:T(8,128)(2,1)S(1)} collective-permute-done((bf16[4,240,256]{2,1,0:T(8,128)(2,1)S(1)}, bf16[4,240,256]{2,1,0:T(8,128)(2,1)S(1)}, u32[]{:S(2)}, u32[]{:S(2)}) %collective-permute-start.11) | collective-permute-done | bytes 491552 | tf_op jit(solution)/shard_map/ppermute | solution.py:233
  175.8 4.2 %product.3 = (f32[232,256]{1,0:T(8,128)S(1)}, f32[232,256]{1,0:T(8,128)}) custom-call(s32[4]{0:T(128)S(1)} %pad_add_fusion.at_ref, bf16[8,240,256]{2,1,0:T(8,128)(2,1)S(1)} %bitcast.29, bf16[4,240,256]{2,1,0:T(8,128)(2,1)S(1)} %collective-permute-done.10.below_ref, bf16[4,240,256]{2,1,0:T(8,128)(2,1)S(1)} %collective-permute-done.11.above_ref, ...), custom_call_target="tpu_custom_call" | custom-call | tf_op jit(solution)/shard_map/product/pallas_call | solution.py:131
  180.6 3.2 %collective-permute-start.12 = (f32[232,256]{1,0:T(8,128)}, f32[232,256]{1,0:T(8,128)S(1)}, u32[]{:S(2)}, u32[]{:S(2)}) collective-permute-start(f32[232,256]{1,0:T(8,128)} %get-tuple-element.24), channel_id=1, source_target_pairs={{0,16},{16,0},{1,17},{17,1},{2,18},{18,2},{3,19},{19,3},{4,20},{20... | collective-permute-start | bytes 712712 | tf_op jit(solution)/shard_map/ppermute | solution.py:229
  184.6 3.1 %collective-permute-done.12.other_ref = f32[232,256]{1,0:T(8,128)S(1)} collective-permute-done((f32[232,256]{1,0:T(8,128)}, f32[232,256]{1,0:T(8,128)S(1)}, u32[]{:S(2)}, u32[]{:S(2)}) %collective-permute-start.12) | collective-permute-done | bytes 237600 | tf_op jit(solution)/shard_map/ppermute | solution.py:229
  188.4 2.0 last.1
  190.4 5.9 %all-to-all-start = ((f32[32,2,256]{2,1,0:T(2,128)}), f32[32,2,256]{2,1,0:T(2,128)S(1)}, u32[]{:S(2)}, u32[]{:S(2)}) async-start(f32[32,2,256]{2,1,0:T(2,128)} %get-tuple-element.27), calls=%async_computation | async-start | bytes 131072 | tf_op jit(solution)/shard_map/all_to_all | solution.py:278
  196.3 3.6 %collective-permute-start.13 = (bf16[224,256]{1,0:T(8,128)(2,1)}, bf16[224,256]{1,0:T(8,128)(2,1)S(1)}, u32[]{:S(2)}, u32[]{:S(2)}) collective-permute-start(bf16[224,256]{1,0:T(8,128)(2,1)} %get-tuple-element.25), channel_id=1, source_target_pairs={{0,256},{256,0},{1,257},{257,1},{2,258},{258,2},{3,259},{259,3},{4... | collective-permute-start | bytes 344072 | tf_op jit(solution)/shard_map/ppermute | solution.py:229
  201.1 8.4 %all-to-all-done.stats_ref = f32[32,2,256]{2,1,0:T(2,128)S(1)} async-done(((f32[32,2,256]{2,1,0:T(2,128)}), f32[32,2,256]{2,1,0:T(2,128)S(1)}, u32[]{:S(2)}, u32[]{:S(2)}) %all-to-all-start) | async-done | bytes 65568 | tf_op jit(solution)/shard_map/all_to_all | solution.py:278
  213.1 16.8 %all-to-all-start.1 = ((f32[16,16,2]{1,2,0:T(2,128)}), f32[16,16,2]{1,2,0:T(2,128)S(1)}, u32[]{:S(2)}, u32[]{:S(2)}) async-start(f32[16,16,2]{1,2,0:T(2,128)} %broadcast_in_dim.5), calls=%async_computation.1 | async-start | bytes 32768 | tf_op jit(solution)/shard_map/all_to_all | solution.py:282
  229.9 1.7 maximum_select_fusion
  231.6 5.6 %all-to-all-done.1 = f32[16,16,2]{1,2,0:T(2,128)S(1)} async-done(((f32[16,16,2]{1,2,0:T(2,128)}), f32[16,16,2]{1,2,0:T(2,128)S(1)}, u32[]{:S(2)}, u32[]{:S(2)}) %all-to-all-start.1) | async-done | bytes 2080 | tf_op jit(solution)/shard_map/all_to_all | solution.py:282
  (56 shorter events, 16.3 us)
Async XLA Ops:
  0.6 17.6 %copy-start = (bf16[2,224,256]{2,1,0:T(8,128)(2,1)S(1)}, bf16[2,224,256]{2,1,0:T(8,128)(2,1)}, u32[]{:S(2)}) copy-start(bf16[2,224,256]{2,1,0:T(8,128)(2,1)} %param.8) | copy-start | bytes 688132
  0.6 13.8 %copy-start.10 = (bf16[1,224]{1,0:T(2,128)(2,1)S(1)}, bf16[1,224]{1,0:T(2,128)(2,1)}, u32[]{:S(2)}) copy-start(bf16[1,224]{1,0:T(2,128)(2,1)} %param.10) | copy-start | bytes 1348
  0.7 115.9 %copy-start.1 = (bf16[1,224,7168]{2,1,0:T(8,128)(2,1)S(1)}, bf16[1,224,7168]{2,1,0:T(8,128)(2,1)}, u32[]{:S(2)}) copy-start(bf16[1,224,7168]{2,1,0:T(8,128)(2,1)} %param.9) | copy-start | bytes 9633796
  4.2 81.1 %collective-permute-start = (bf16[112,3584]{1,0:T(8,128)(2,1)}, bf16[112,3584]{1,0:T(8,128)(2,1)}, u32[]{:S(2)}, u32[]{:S(2)}) collective-permute-start(bf16[112,3584]{1,0:T(8,128)(2,1)} %get-tuple-element.29), channel_id=1, source_target_pairs={{0,16},{16,0},{1,17},{17,1},{2,18},{18,2},{3,19},{19,3},{4,20},{20... | collective-permute-start | bytes 2408456 | tf_op jit(solution)/shard_map/ppermute | solution.py:229
  8.1 77.1 %collective-permute-start.1 = (bf16[112,3584]{1,0:T(8,128)(2,1)}, bf16[112,3584]{1,0:T(8,128)(2,1)}, u32[]{:S(2)}, u32[]{:S(2)}) collective-permute-start(bf16[112,3584]{1,0:T(8,128)(2,1)} %get-tuple-element.28), channel_id=1, source_target_pairs={{0,256},{256,0},{1,257},{257,1},{2,258},{258,2},{3,259},{259,3},{4... | collective-permute-start | bytes 2408456 | tf_op jit(solution)/shard_map/ppermute | solution.py:229
  12.5 72.8 %collective-permute-start.2 = (bf16[112,3584]{1,0:T(8,128)(2,1)}, bf16[112,3584]{1,0:T(8,128)(2,1)}, u32[]{:S(2)}, u32[]{:S(2)}) collective-permute-start(bf16[112,3584]{1,0:T(8,128)(2,1)} %get-tuple-element.29), channel_id=1, source_target_pairs={{0,272},{16,256},{256,16},{272,0},{1,273},{17,257},{257,17},{273,1... | collective-permute-start | bytes 2408456 | tf_op jit(solution)/shard_map/ppermute | solution.py:229
  14.6 32.0 %collective-permute-start.3 = (bf16[224,1]{1,0:T(8,128)(2,1)S(1)}, bf16[224,1]{1,0:T(8,128)(2,1)S(1)}, u32[]{:S(2)}, u32[]{:S(2)}) collective-permute-start(bf16[224,1]{1,0:T(8,128)(2,1)S(1)} %copy.20), channel_id=1, source_target_pairs={{0,256},{256,0},{1,257},{257,1},{2,258},{258,2},{3,259},{259,3},{4... | collective-permute-start | bytes 1352 | tf_op jit(solution)/shard_map/ppermute | solution.py:229
  85.3 31.3 %collective-permute-start.6 = (bf16[112,3584]{1,0:T(8,128)(2,1)}, bf16[112,3584]{1,0:T(8,128)(2,1)}, u32[]{:S(2)}, u32[]{:S(2)}) collective-permute-start(bf16[112,3584]{1,0:T(8,128)(2,1)} %collective-permute-done.side_ref), channel_id=1, source_target_pairs={{0,32},{32,0},{1,33},{33,1},{2,34},{34,2},{3,35},{35,3},{4,36},{36... | collective-permute-start | bytes 2408456 | tf_op jit(solution)/shard_map/ppermute | solution.py:229
  93.1 23.5 %collective-permute-start.7 = (bf16[112,3584]{1,0:T(8,128)(2,1)}, bf16[112,3584]{1,0:T(8,128)(2,1)}, u32[]{:S(2)}, u32[]{:S(2)}) collective-permute-start(bf16[112,3584]{1,0:T(8,128)(2,1)} %collective-permute-done.1.over_ref), channel_id=1, source_target_pairs={{0,32},{32,0},{1,33},{33,1},{2,34},{34,2},{3,35},{35,3},{4,36},{36... | collective-permute-start | bytes 2408456 | tf_op jit(solution)/shard_map/ppermute | solution.py:229
  95.0 21.6 %collective-permute-start.8 = (bf16[112,3584]{1,0:T(8,128)(2,1)}, bf16[112,3584]{1,0:T(8,128)(2,1)}, u32[]{:S(2)}, u32[]{:S(2)}) collective-permute-start(bf16[112,3584]{1,0:T(8,128)(2,1)} %collective-permute-done.2.cross_ref), channel_id=1, source_target_pairs={{0,32},{32,0},{1,33},{33,1},{2,34},{34,2},{3,35},{35,3},{4,36},{36... | collective-permute-start | bytes 2408456 | tf_op jit(solution)/shard_map/ppermute | solution.py:229
  98.5 1.0 copy-start.2
  99.4 16.3 %collective-permute-start.4 = (bf16[4,240,256]{2,1,0:T(8,128)(2,1)}, bf16[4,240,256]{2,1,0:T(8,128)(2,1)}, u32[]{:S(2)}, u32[]{:S(2)}) collective-permute-start(bf16[4,240,256]{2,1,0:T(8,128)(2,1)} %bitcast.9), channel_id=1, source_target_pairs={{0,1},{1,2},{2,3},{3,4},{4,5},{5,6},{6,7},{7,8},{8,9},{9,10},{10,1... | collective-permute-start | bytes 1474568 | tf_op jit(solution)/shard_map/ppermute | solution.py:233
  101.8 14.7 %collective-permute-start.5 = (bf16[4,240,256]{2,1,0:T(8,128)(2,1)}, bf16[4,240,256]{2,1,0:T(8,128)(2,1)}, u32[]{:S(2)}, u32[]{:S(2)}) collective-permute-start(bf16[4,240,256]{2,1,0:T(8,128)(2,1)} %bitcast.10), channel_id=1, source_target_pairs={{0,15},{1,0},{2,1},{3,2},{4,3},{5,4},{6,5},{7,6},{8,7},{9,8},{10,9... | collective-permute-start | bytes 1474568 | tf_op jit(solution)/shard_map/ppermute | solution.py:233
  106.0 69.7 %copy-start.6 = (s32[4]{0:T(128)}, s32[4]{0:T(128)S(1)}, u32[]{:S(2)}) copy-start(s32[4]{0:T(128)S(1)} %pad_add_fusion.at_ref) | copy-start | bytes 52
  116.6 1.2 copy-start.3
  121.5 0.7 copy-start.5
  122.2 8.0 %collective-permute-start.9 = (f32[232,256]{1,0:T(8,128)S(1)}, f32[232,256]{1,0:T(8,128)S(1)}, u32[]{:S(2)}, u32[]{:S(2)}) collective-permute-start(f32[232,256]{1,0:T(8,128)S(1)} %get-tuple-element.20), channel_id=1, source_target_pairs={{0,16},{16,0},{1,17},{17,1},{2,18},{18,2},{3,19},{19,3},{4,20},{20... | collective-permute-start | bytes 712712 | tf_op jit(solution)/shard_map/ppermute | solution.py:229
  130.3 0.7 copy-start.9
  160.5 12.0 %collective-permute-start.10 = (bf16[4,240,256]{2,1,0:T(8,128)(2,1)S(1)}, bf16[4,240,256]{2,1,0:T(8,128)(2,1)S(1)}, u32[]{:S(2)}, u32[]{:S(2)}) collective-permute-start(bf16[4,240,256]{2,1,0:T(8,128)(2,1)S(1)} %bitcast.31), channel_id=1, source_target_pairs={{0,1},{1,2},{2,3},{3,4},{4,5},{5,6},{6,7},{7,8},{8,9},{9,10},{10,1... | collective-permute-start | bytes 1474568 | tf_op jit(solution)/shard_map/ppermute | solution.py:233
  165.8 9.9 %collective-permute-start.11 = (bf16[4,240,256]{2,1,0:T(8,128)(2,1)S(1)}, bf16[4,240,256]{2,1,0:T(8,128)(2,1)S(1)}, u32[]{:S(2)}, u32[]{:S(2)}) collective-permute-start(bf16[4,240,256]{2,1,0:T(8,128)(2,1)S(1)} %bitcast.30), channel_id=1, source_target_pairs={{0,15},{1,0},{2,1},{3,2},{4,3},{5,4},{6,5},{7,6},{8,7},{9,8},{10,9... | collective-permute-start | bytes 1474568 | tf_op jit(solution)/shard_map/ppermute | solution.py:233
  175.7 8.1 %copy-start.14 = (bf16[224]{0:T(256)(128)(2,1)S(1)}, bf16[224]{0:T(256)(128)(2,1)}, u32[]{:S(2)}) copy-start(bf16[224]{0:T(256)(128)(2,1)} %param.12) | copy-start | bytes 1348
  175.7 8.1 %copy-start.15 = (bf16[224]{0:T(256)(128)(2,1)S(1)}, bf16[224]{0:T(256)(128)(2,1)}, u32[]{:S(2)}) copy-start(bf16[224]{0:T(256)(128)(2,1)} %param.11) | copy-start | bytes 1348
  175.7 24.2 %copy-start.11 = (s32[2,256]{1,0:T(2,128)S(1)}, s32[2,256]{1,0:T(2,128)}, u32[]{:S(2)}) copy-start(s32[2,256]{1,0:T(2,128)} %param.13) | copy-start | bytes 6148
  175.7 24.8 %copy-start.12 = (s32[2,256]{1,0:T(2,128)S(1)}, s32[2,256]{1,0:T(2,128)}, u32[]{:S(2)}) copy-start(s32[2,256]{1,0:T(2,128)} %param.15) | copy-start | bytes 6148
  175.7 24.8 %copy-start.13 = (s32[2,256]{1,0:T(2,128)S(1)}, s32[2,256]{1,0:T(2,128)}, u32[]{:S(2)}) copy-start(s32[2,256]{1,0:T(2,128)} %param.14) | copy-start | bytes 6148
  179.9 0.7 copy-start.4
  180.6 7.1 %collective-permute-start.12 = (f32[232,256]{1,0:T(8,128)}, f32[232,256]{1,0:T(8,128)S(1)}, u32[]{:S(2)}, u32[]{:S(2)}) collective-permute-start(f32[232,256]{1,0:T(8,128)} %get-tuple-element.24), channel_id=1, source_target_pairs={{0,16},{16,0},{1,17},{17,1},{2,18},{18,2},{3,19},{19,3},{4,20},{20... | collective-permute-start | bytes 712712 | tf_op jit(solution)/shard_map/ppermute | solution.py:229
  187.7 0.7 copy-start.8
  190.4 19.1 %all-to-all-start = ((f32[32,2,256]{2,1,0:T(2,128)}), f32[32,2,256]{2,1,0:T(2,128)S(1)}, u32[]{:S(2)}, u32[]{:S(2)}) async-start(f32[32,2,256]{2,1,0:T(2,128)} %get-tuple-element.27), calls=%async_computation | async-start | bytes 131072 | tf_op jit(solution)/shard_map/all_to_all | solution.py:278
  196.3 33.6 %collective-permute-start.13 = (bf16[224,256]{1,0:T(8,128)(2,1)}, bf16[224,256]{1,0:T(8,128)(2,1)S(1)}, u32[]{:S(2)}, u32[]{:S(2)}) collective-permute-start(bf16[224,256]{1,0:T(8,128)(2,1)} %get-tuple-element.25), channel_id=1, source_target_pairs={{0,256},{256,0},{1,257},{257,1},{2,258},{258,2},{3,259},{259,3},{4... | collective-permute-start | bytes 344072 | tf_op jit(solution)/shard_map/ppermute | solution.py:229
  209.5 0.6 copy-start.7
  213.1 24.1 %all-to-all-start.1 = ((f32[16,16,2]{1,2,0:T(2,128)}), f32[16,16,2]{1,2,0:T(2,128)S(1)}, u32[]{:S(2)}, u32[]{:S(2)}) async-start(f32[16,16,2]{1,2,0:T(2,128)} %broadcast_in_dim.5), calls=%async_computation.1 | async-start | bytes 32768 | tf_op jit(solution)/shard_map/all_to_all | solution.py:282

commit v2 on v1

--- a/solution.py
+++ b/solution.py
@@ -1,3 +1,5 @@
+import functools
+
 import jax
 import jax.numpy as jnp
 from jax import lax
@@ -13,11 +15,11 @@
 T = 256
 KH = D // 2
 R = 240
-HALF = F // 2
 F32 = jnp.float32
 BF16 = jnp.bfloat16
 Z = ("h", "p")
-VMEM_LIMIT = 40 * 1024 * 1024
+SMALL = pltpu.CompilerParams(vmem_limit_bytes=4 * 1024 * 1024)
+LARGE = pltpu.CompilerParams(vmem_limit_bytes=16 * 1024 * 1024)
 
 
 def vmem():
@@ -56,44 +58,59 @@
         out_shape=jax.ShapeDtypeStruct((R, T), BF16),
         in_specs=[vmem(), vmem()],
         out_specs=vmem(),
+        compiler_params=SMALL,
         name="pack",
     )(rows, gain)
 
 
+def split_kernel(at_ref, weight_ref, near_ref, far_ref, sems):
+    x = at_ref[1]
+    near = pl.ds(pl.multiple_of(x * KH, 128), KH)
+    far = pl.ds(pl.multiple_of((1 - x) * KH, 128), KH)
+    copies = [
+        pltpu.make_async_copy(weight_ref.at[:, near], near_ref, sems.at[0]),
+        pltpu.make_async_copy(weight_ref.at[:, far], far_ref, sems.at[1]),
+    ]
+    for copy in copies:
+        copy.start()
+    for copy in copies:
+        copy.wait()
+
+
+def split(at, weight):
+    out = jax.ShapeDtypeStruct((F, KH), BF16)
+    return pl.pallas_call(
+        split_kernel,
+        out_shape=(out, out),
+        in_specs=[smem(), anywhere()],
+        out_specs=(anywhere(), anywhere()),
+        scratch_shapes=[pltpu.SemaphoreType.DMA((2,))],
+        compiler_params=SMALL,
+        name="split",
+    )(at, weight)
+
+
 def product_kernel(
-    local_block, at_ref, same_ref, below_ref, above_ref, weight_ref, side_ref, side2_ref,
-    over_ref, over2_ref, cross_ref, cross2_ref, own_ref, send_ref, held, values, sems,
+    local_block, at_ref, same_ref, below_ref, above_ref, near_ref, side_ref, over_ref, cross_ref,
+    own_ref, send_ref, held, values, sems,
 ):
-    section, x, core, parity = at_ref[0], at_ref[1], at_ref[2], at_ref[3]
-    columns = pl.ds(pl.multiple_of(x * KH, 128), KH)
-    mine = pl.ds(pl.multiple_of(core * HALF, 16), HALF)
-    theirs = pl.ds(pl.multiple_of((1 - core) * HALF, 16), HALF)
-    far = pl.ds(pl.multiple_of(F + core * HALF, 16), HALF)
-    far2 = pl.ds(pl.multiple_of(F + (1 - core) * HALF, 16), HALF)
-
-    def near_copies():
+    local = at_ref[0] == local_block
+    parity = at_ref[3]
+
+    def copies(first, second):
         return [
-            pltpu.make_async_copy(weight_ref.at[:, columns], held.at[0:F, :], sems.at[0]),
-            pltpu.make_async_copy(side_ref, held.at[far, :], sems.at[1]),
-            pltpu.make_async_copy(side2_ref, held.at[far2, :], sems.at[2]),
+            pltpu.make_async_copy(first, held.at[0:F, :], sems.at[0]),
+            pltpu.make_async_copy(second, held.at[F:2 * F, :], sems.at[1]),
         ]
 
-    def away_copies():
-        return [
-            pltpu.make_async_copy(over_ref, held.at[mine, :], sems.at[0]),
-            pltpu.make_async_copy(over2_ref, held.at[theirs, :], sems.at[1]),
-            pltpu.make_async_copy(cross_ref, held.at[far, :], sems.at[2]),
-            pltpu.make_async_copy(cross2_ref, held.at[far2, :], sems.at[3]),
-        ]
-
-    @pl.when(section == local_block)
-    def _():
-        for copy in near_copies():
+    @pl.when(local)
+    def _():
+        for copy in copies(near_ref, side_ref):
             copy.start()
 
-    @pl.when(section != local_block)
-    def _():
-        for copy in away_copies():
+    @pl.when(jnp.logical_not(local))
+    def _():
+        for copy in copies(over_ref, cross_ref):
             copy.start()
 
     squares = jnp.zeros((1, T), F32)
@@ -107,14 +124,14 @@
         values[there, :] = other[0:F]
         squares += jnp.sum(other[F:R].astype(F32), axis=0, keepdims=True)
 
-    @pl.when(section == local_block)
-    def _():
-        for copy in near_copies():
+    @pl.when(local)
+    def _():
+        for copy in copies(near_ref, side_ref):
             copy.wait()
 
-    @pl.when(section != local_block)
-    def _():
-        for copy in away_copies():
+    @pl.when(jnp.logical_not(local))
+    def _():
+        for copy in copies(over_ref, cross_ref):
             copy.wait()
 
     product = jnp.dot(held[...], values[...], preferred_element_type=F32)
@@ -125,22 +142,21 @@
     send_ref[F:F + 8, :] = rows
 
 
-def product(local_block, at, same, below, above, weight, received):
-    import functools
+def product(local_block, at, same, below, above, blocks):
     out = jax.ShapeDtypeStruct((F + 8, T), F32)
     return pl.pallas_call(
         functools.partial(product_kernel, local_block),
         out_shape=(out, out),
-        in_specs=[smem(), vmem(), vmem(), vmem()] + [anywhere()] * 7,
+        in_specs=[smem(), vmem(), vmem(), vmem()] + [anywhere()] * 4,
         out_specs=(vmem(), vmem()),
         scratch_shapes=[
             pltpu.VMEM((2 * F, KH), BF16),
             pltpu.VMEM((KH, T), BF16),
-            pltpu.SemaphoreType.DMA((4,)),
+            pltpu.SemaphoreType.DMA((2,)),
         ],
-        compiler_params=pltpu.CompilerParams(vmem_limit_bytes=VMEM_LIMIT),
+        compiler_params=LARGE,
         name="product",
-    )(at, same, below, above, weight, *received)
+    )(at, same, below, above, *blocks)
 
 
 def block_rows(own_ref, other_ref, rows_ref):
@@ -163,6 +179,7 @@
         out_shape=(jax.ShapeDtypeStruct((F, T), BF16), jax.ShapeDtypeStruct((R, T), BF16)),
         in_specs=[vmem()] * 4,
         out_specs=(vmem(), vmem()),
+        compiler_params=SMALL,
         name="middle",
     )(own, other, rows, gain)
 
@@ -194,6 +211,7 @@
         out_shape=(out, out, jax.ShapeDtypeStruct((32, 2, T), F32)),
         in_specs=[smem()] + [vmem()] * 4,
         out_specs=(vmem(), vmem(), vmem()),
+        compiler_params=SMALL,
         name="last",
     )(at, own, other, rows, head)
 
@@ -210,15 +228,21 @@
     sums = jnp.sum(jnp.where(member, squared, 0.0), axis=1, keepdims=True)
     counts = jnp.sum(jnp.where(member, mask, 0.0), axis=1, keepdims=True)
     lane = lax.broadcasted_iota(jnp.int32, (SEGS, 128), 1)
-    sums_ref[...] = jnp.where(lane == 0, sums, jnp.where(lane == 1, counts, 0.0))
+    diagonal = lane == lax.broadcasted_iota(jnp.int32, (SEGS, 128), 0)
+    sums = jnp.sum(jnp.where(diagonal, sums, 0.0), axis=0, keepdims=True)
+    counts = jnp.sum(jnp.where(diagonal, counts, 0.0), axis=0, keepdims=True)
+    both = jnp.concatenate([sums, counts], axis=0)
+    for i in range(16):
+        sums_ref[i] = both
 
 
 def loss_parts(stats, label, mask, segment):
     return pl.pallas_call(
         loss_kernel,
-        out_shape=jax.ShapeDtypeStruct((SEGS, 128), F32),
+        out_shape=jax.ShapeDtypeStruct((16, 2, 128), F32),
         in_specs=[vmem()] * 4,
         out_specs=vmem(),
+        compiler_params=SMALL,
         name="loss_parts",
     )(stats, label, mask, segment)
 
@@ -243,8 +267,7 @@
 ):
     section = lax.axis_index("s")
     x = lax.axis_index("x")
-    core = lax.axis_index("c")
-    at = jnp.stack([section, x, core, lax.axis_index("p")]).astype(jnp.int32)
+    at = jnp.stack([section, x, x, lax.axis_index("p")]).astype(jnp.int32)
     weight = section_proj[0]
 
     gain = section_gain[0][:, None]
@@ -252,25 +275,18 @@
     gain0 = jnp.where(section == 0, gain, gain_away)
     gain1 = jnp.where(section == 0, gain_away, gain)
 
-    half = lax.dynamic_slice(weight, (core * HALF, 0), (HALF, D))
-    near = lax.dynamic_slice(half, (0, x * KH), (HALF, KH))
-    far = lax.dynamic_slice(half, (0, (1 - x) * KH), (HALF, KH))
-    side = swapped(far, "x")
-    over = swapped(near, "s")
-    cross = swapped(far, "s", "x")
+    near, far = split(at, weight)
+    near, far, gain0, gain1 = lax.optimization_barrier((near, far, gain0, gain1))
+    blocks = (near, swapped(far, "x"), swapped(near, "s"), swapped(far, "s", "x"))
 
     rows = lax.dynamic_index_in_dim(tokens_in, section, 0, keepdims=False)
     same, below, above = gathered(pack(rows, gain0))
 
-    side, over, cross, same = lax.optimization_barrier((side, over, cross, same))
-    received = (
-        side, swapped(side, "c"), over, swapped(over, "c"), cross, swapped(cross, "c")
-    )
-    own, send = product(0, at, same, below, above, weight, received)
+    own, send = product(0, at, same, below, above, blocks)
     first, block = middle(own, swapped(send, "x"), rows, gain1)
 
     same, below, above = gathered(block)
-    own, send = product(1, at, same, below, above, weight, received)
+    own, send = product(1, at, same, below, above, blocks)
     head = (final_gain.astype(F32) * score_weight.astype(F32))[:, None]
     second, handed, stats = last(at, own, swapped(send, "x"), first, head)
     handed = swapped(handed, "s")
@@ -278,10 +294,9 @@
     stats = lax.all_to_all(stats, ("x", "h", "p"), 0, 0, tiled=True)
     pick = lambda value: lax.dynamic_slice(value, (section, 0), (1, T))
     parts = loss_parts(stats, pick(labels), pick(loss_mask), pick(segment_ids))
-    parts = jnp.broadcast_to(parts[None, :, 0:2], (16, SEGS, 2))
     parts = lax.all_to_all(parts, ("s", "y", "c"), 0, 0, tiled=True)
-    parts = jnp.sum(parts.reshape(2, 8, SEGS, 2), axis=1)
-    segment_loss = parts[..., 0] / jnp.maximum(parts[..., 1], 1.0)
+    parts = jnp.sum(parts.reshape(2, 8, 2, 128), axis=1)[:, :, :SEGS]
+    segment_loss = parts[:, 0] / jnp.maximum(parts[:, 1], 1.0)
 
     section_out = jnp.where(section == 0, jnp.stack([first, handed]), jnp.stack([handed, second]))
     return section_out[None], segment_loss

time: 239 us -> 209 us (0.87)
  waiting for transfers between devices: 69.4 us -> 51.1 us
  blocking collectives: 63.9 us -> 74.1 us
  starting transfers between devices: 71.1 us -> 62.5 us
  local copies, waits for them, and re-layouts: 14.3 us -> 6.75 us
  Pallas kernels: 15.1 us -> 11.1 us
    ppermute x10 -> x7, waiting for transfers between devices: 36.9 us -> 22.9 us  [swapped(): return lax.ppermute(value, name, [(i, i ^ count - 1) for i in range(count)])]
    all_gather x2, blocking collectives: 63.9 us -> 74.1 us  [gathered(): same = lax.all_gather(block, 'h', axis=0, tiled=False)]
    ppermute x10 -> x7, starting transfers between devices: 34.7 us -> 25.2 us  [swapped(): return lax.ppermute(value, name, [(i, i ^ count - 1) for i in range(count)])]
    ppermute x4, waiting for transfers between devices: 18.5 us -> 12.3 us  [shifted(): return lax.ppermute(value, Z, [(i, (i + by) % 16) for i in range(16)])]
    dynamic_slice x1 -> x0, local copies, waits for them, and re-layouts: 3.51 us -> none  [body(): near = lax.dynamic_slice(half, (0, x * KH), (HALF, KH))]
    unnamed x32 -> x20, local copies, waits for them, and re-layouts: 5.6 us -> 4.22 us
  transfers between devices with their start and end apart: 16 -> 13, of which waited for: 9 -> 9; matrix products, arithmetic and copies ran while one was open for 3% -> 1% of each run, Pallas kernels for 1% -> 1%
where the time goes in v2:
time: 209 us
  blocking collectives  74.1 us (35%)
  starting transfers between devices  62.5 us (30%)
  waiting for transfers between devices  51.1 us (24%)
  Pallas kernels  11.1 us (5%)
  local copies, waits for them, and re-layouts  6.75 us (3%)
    all_gather x2, blocking collectives, gathered(): same = lax.all_gather(block, 'h', axis=0, tiled=False)  74.1 us
    ppermute x7, starting transfers between devices, swapped(): return lax.ppermute(value, name, [(i, i ^ count - 1) for i in range(count)])  25.2 us
    ppermute x7, waiting for transfers between devices, swapped(): return lax.ppermute(value, name, [(i, i ^ count - 1) for i in range(count)])  22.9 us
    all_to_all x1, starting transfers between devices, body(): parts = lax.all_to_all(parts, ('s', 'y', 'c'), 0, 0, tiled=True)  17.6 us
    ppermute x4, starting transfers between devices, shifted(): return lax.ppermute(value, Z, [(i, (i + by) % 16) for i in range(16)])  13 us
    ppermute x4, waiting for transfers between devices, shifted(): return lax.ppermute(value, Z, [(i, (i + by) % 16) for i in range(16)])  12.3 us
    all_to_all x1, waiting for transfers between devices, body(): stats = lax.all_to_all(stats, ('x', 'h', 'p'), 0, 0, tiled=True)  9.4 us
    pallas_call x2, Pallas kernels, product(): pl.pallas_call(functools.partial(product_kernel, local_block), out_shape=...  6.8 us
  transfers between devices with their start and end apart: 13, of which 9 were waited for; matrix products, arithmetic and copies ran while one was open for 1% of the time, Pallas kernels for 1%

profile of v2, /device:TPU:1, one launch (start us, length us, event | category | flops | bytes accessed | tf_op | source)
XLA Modules:
  0.0 208.5 jit_solution(12999953727463223013)
XLA Ops:
  0.6 0.9 copy.15
  1.5 5.5 %collective-permute-start = (bf16[224,1]{1,0:T(8,128)(2,1)S(1)}, bf16[224,1]{1,0:T(8,128)(2,1)S(1)}, u32[]{:S(2)}, u32[]{:S(2)}) collective-permute-start(bf16[224,1]{1,0:T(8,128)(2,1)S(1)} %copy.15), channel_id=1, source_target_pairs={{0,256},{256,0},{1,257},{257,1},{2,258},{258,2},{3,259},{259,3},{4... | collective-permute-start | bytes 1352 | tf_op jit(solution)/shard_map/ppermute | solution.py:253
  7.1 1.9 copy-done.1
  9.0 1.8 split.1
  11.5 2.8 %collective-permute-start.5 = (bf16[224,3584]{1,0:T(8,128)(2,1)}, bf16[224,3584]{1,0:T(8,128)(2,1)S(1)}, u32[]{:S(2)}, u32[]{:S(2)}) collective-permute-start(bf16[224,3584]{1,0:T(8,128)(2,1)} %get-tuple-element.21), channel_id=1, source_target_pairs={{0,272},{16,256},{256,16},{272,0},{1,273},{17,257},{257,17},{273,1... | collective-permute-start | bytes 4816904 | tf_op jit(solution)/shard_map/ppermute | solution.py:253
  14.3 1.9 collective-permute-start.3
  16.2 4.9 %collective-permute-start.4 = (bf16[224,3584]{1,0:T(8,128)(2,1)S(1)}, bf16[224,3584]{1,0:T(8,128)(2,1)}, u32[]{:S(2)}, u32[]{:S(2)}) collective-permute-start(bf16[224,3584]{1,0:T(8,128)(2,1)S(1)} %get-tuple-element.20.near_ref), channel_id=1, source_target_pairs={{0,256},{256,0},{1,257},{257,1},{2,258},{258,2},{3,259},{259,3},{4... | collective-permute-start | bytes 4816904 | tf_op jit(solution)/shard_map/ppermute | solution.py:253
  21.2 35.1 %all-gather = bf16[1920,256]{1,0:T(8,128)(2,1)S(1)} all-gather(bf16[240,256]{1,0:T(8,128)(2,1)S(1)} %pack.1), channel_id=2, replica_groups=mesh['s'=2,'y'=4,'c'=2,'x'=2,'h'=8,'p'=2] {'h'}, dimensions={0}, use_global_device_ids=true | all-gather | bytes 1105920 | tf_op jit(solution)/shard_map/all_gather | solution.py:261
  56.4 2.9 %collective-permute-start.1 = (bf16[4,240,256]{2,1,0:T(8,128)(2,1)S(1)}, bf16[4,240,256]{2,1,0:T(8,128)(2,1)S(1)}, u32[]{:S(2)}, u32[]{:S(2)}) collective-permute-start(bf16[4,240,256]{2,1,0:T(8,128)(2,1)S(1)} %bitcast.27), channel_id=1, source_target_pairs={{0,1},{1,2},{2,3},{3,4},{4,5},{5,6},{6,7},{7,8},{8,9},{9,10},{10,1... | collective-permute-start | bytes 1474568 | tf_op jit(solution)/shard_map/ppermute | solution.py:257
  59.3 3.6 %collective-permute-start.2 = (bf16[4,240,256]{2,1,0:T(8,128)(2,1)S(1)}, bf16[4,240,256]{2,1,0:T(8,128)(2,1)S(1)}, u32[]{:S(2)}, u32[]{:S(2)}) collective-permute-start(bf16[4,240,256]{2,1,0:T(8,128)(2,1)S(1)} %bitcast.25), channel_id=1, source_target_pairs={{0,15},{1,0},{2,1},{3,2},{4,3},{5,4},{6,5},{7,6},{8,7},{9,8},{10,9... | collective-permute-start | bytes 1474568 | tf_op jit(solution)/shard_map/ppermute | solution.py:257
  62.9 4.9 %collective-permute-done.1.below_ref = bf16[4,240,256]{2,1,0:T(8,128)(2,1)S(1)} collective-permute-done((bf16[4,240,256]{2,1,0:T(8,128)(2,1)S(1)}, bf16[4,240,256]{2,1,0:T(8,128)(2,1)S(1)}, u32[]{:S(2)}, u32[]{:S(2)}) %collective-permute-start.1) | collective-permute-done | bytes 491552 | tf_op jit(solution)/shard_map/ppermute | solution.py:257
  67.8 1.5 collective-permute-done.2.above_ref
  69.2 14.4 %collective-permute-done.4.over_ref = bf16[224,3584]{1,0:T(8,128)(2,1)} collective-permute-done((bf16[224,3584]{1,0:T(8,128)(2,1)S(1)}, bf16[224,3584]{1,0:T(8,128)(2,1)}, u32[]{:S(2)}, u32[]{:S(2)}) %collective-permute-start.4) | collective-permute-done | bytes 1605664 | tf_op jit(solution)/shard_map/ppermute | solution.py:253
  83.6 3.1 %product.2 = (f32[232,256]{1,0:T(8,128)S(1)}, f32[232,256]{1,0:T(8,128)S(1)}) custom-call(s32[4]{0:T(128)S(1)} %pad_add_fusion.at_ref, bf16[8,240,256]{2,1,0:T(8,128)(2,1)S(1)} %bitcast.20, bf16[4,240,256]{2,1,0:T(8,128)(2,1)S(1)} %collective-permute-done.1.below_ref, bf16[4,240,256]{2,1,0:T(8,128)(2,1)S(1)} %collective-permute-done.2.above_ref, ...), custom_call_target="tpu_custom_call" | custom-call | tf_op jit(solution)/shard_map/product/pallas_call | solution.py:147
  86.8 1.9 collective-permute-start.6
  88.7 4.9 %collective-permute-done.6.other_ref = f32[232,256]{1,0:T(8,128)S(1)} collective-permute-done((f32[232,256]{1,0:T(8,128)S(1)}, f32[232,256]{1,0:T(8,128)S(1)}, u32[]{:S(2)}, u32[]{:S(2)}) %collective-permute-start.6) | collective-permute-done | bytes 237600 | tf_op jit(solution)/shard_map/ppermute | solution.py:253
  93.8 39.1 %all-gather.1 = bf16[1920,256]{1,0:T(8,128)(2,1)S(1)} all-gather(bf16[240,256]{1,0:T(8,128)(2,1)S(1)} %get-tuple-element.26), channel_id=3, replica_groups=mesh['s'=2,'y'=4,'c'=2,'x'=2,'h'=8,'p'=2] {'h'}, dimensions={0}, use_global_device_ids=true | all-gather | bytes 1105920 | tf_op jit(solution)/shard_map/all_gather | solution.py:261
  133.0 2.5 %collective-permute-start.7 = (bf16[4,240,256]{2,1,0:T(8,128)(2,1)S(1)}, bf16[4,240,256]{2,1,0:T(8,128)(2,1)S(1)}, u32[]{:S(2)}, u32[]{:S(2)}) collective-permute-start(bf16[4,240,256]{2,1,0:T(8,128)(2,1)S(1)} %bitcast.28), channel_id=1, source_target_pairs={{0,1},{1,2},{2,3},{3,4},{4,5},{5,6},{6,7},{7,8},{8,9},{9,10},{10,1... | collective-permute-start | bytes 1474568 | tf_op jit(solution)/shard_map/ppermute | solution.py:257
  135.5 4.0 %collective-permute-start.8 = (bf16[4,240,256]{2,1,0:T(8,128)(2,1)S(1)}, bf16[4,240,256]{2,1,0:T(8,128)(2,1)S(1)}, u32[]{:S(2)}, u32[]{:S(2)}) collective-permute-start(bf16[4,240,256]{2,1,0:T(8,128)(2,1)S(1)} %bitcast.26), channel_id=1, source_target_pairs={{0,15},{1,0},{2,1},{3,2},{4,3},{5,4},{6,5},{7,6},{8,7},{9,8},{10,9... | collective-permute-start | bytes 1474568 | tf_op jit(solution)/shard_map/ppermute | solution.py:257
  139.5 5.1 %collective-permute-done.7.below_ref = bf16[4,240,256]{2,1,0:T(8,128)(2,1)S(1)} collective-permute-done((bf16[4,240,256]{2,1,0:T(8,128)(2,1)S(1)}, bf16[4,240,256]{2,1,0:T(8,128)(2,1)S(1)}, u32[]{:S(2)}, u32[]{:S(2)}) %collective-permute-start.7) | collective-permute-done | bytes 491552 | tf_op jit(solution)/shard_map/ppermute | solution.py:257
  144.6 0.9 collective-permute-done.8.above_ref
  145.4 3.7 %product.3 = (f32[232,256]{1,0:T(8,128)S(1)}, f32[232,256]{1,0:T(8,128)}) custom-call(s32[4]{0:T(128)S(1)} %copy-done.6, bf16[8,240,256]{2,1,0:T(8,128)(2,1)S(1)} %bitcast.21, bf16[4,240,256]{2,1,0:T(8,128)(2,1)S(1)} %collective-permute-done.7.below_ref, bf16[4,240,256]{2,1,0:T(8,128)(2,1)S(1)} %collective-permute-done.8.above_ref, ...), custom_call_target="tpu_custom_call" | custom-call | tf_op jit(solution)/shard_map/product/pallas_call | solution.py:147
  149.8 5.8 %collective-permute-start.9 = (f32[232,256]{1,0:T(8,128)}, f32[232,256]{1,0:T(8,128)S(1)}, u32[]{:S(2)}, u32[]{:S(2)}) collective-permute-start(f32[232,256]{1,0:T(8,128)} %get-tuple-element.28), channel_id=1, source_target_pairs={{0,16},{16,0},{1,17},{17,1},{2,18},{18,2},{3,19},{19,3},{4,20},{20... | collective-permute-start | bytes 712712 | tf_op jit(solution)/shard_map/ppermute | solution.py:253
  155.8 3.5 %collective-permute-done.9.other_ref = f32[232,256]{1,0:T(8,128)S(1)} collective-permute-done((f32[232,256]{1,0:T(8,128)}, f32[232,256]{1,0:T(8,128)S(1)}, u32[]{:S(2)}, u32[]{:S(2)}) %collective-permute-start.9) | collective-permute-done | bytes 237600 | tf_op jit(solution)/shard_map/ppermute | solution.py:253
  159.3 0.9 copy-done.3
  160.9 1.4 last.1
  162.3 6.8 %all-to-all-start = ((f32[32,2,256]{2,1,0:T(2,128)}), f32[32,2,256]{2,1,0:T(2,128)S(1)}, u32[]{:S(2)}, u32[]{:S(2)}) async-start(f32[32,2,256]{2,1,0:T(2,128)} %get-tuple-element.31), calls=%async_computation | async-start | bytes 131072 | tf_op jit(solution)/shard_map/all_to_all | solution.py:294
  169.1 2.4 %collective-permute-start.10 = (bf16[224,256]{1,0:T(8,128)(2,1)S(1)}, bf16[224,256]{1,0:T(8,128)(2,1)S(1)}, u32[]{:S(2)}, u32[]{:S(2)}) collective-permute-start(bf16[224,256]{1,0:T(8,128)(2,1)S(1)} %get-tuple-element.29), channel_id=1, source_target_pairs={{0,256},{256,0},{1,257},{257,1},{2,258},{258,2},{3,259},{259,3},{4... | collective-permute-start | bytes 344072 | tf_op jit(solution)/shard_map/ppermute | solution.py:253
  172.9 9.4 %all-to-all-done.stats_ref = f32[32,2,256]{2,1,0:T(2,128)S(1)} async-done(((f32[32,2,256]{2,1,0:T(2,128)}), f32[32,2,256]{2,1,0:T(2,128)S(1)}, u32[]{:S(2)}, u32[]{:S(2)}) %all-to-all-start) | async-done | bytes 65568 | tf_op jit(solution)/shard_map/all_to_all | solution.py:294
  182.3 0.7 loss_parts.1
  183.0 17.6 %all-to-all-start.1 = ((f32[16,2,128]{2,1,0:T(2,128)}), f32[16,2,128]{2,1,0:T(2,128)S(1)}, u32[]{:S(2)}, u32[]{:S(2)}) async-start(f32[16,2,128]{2,1,0:T(2,128)} %loss_parts.1), calls=%async_computation.1 | async-start | bytes 32768 | tf_op jit(solution)/shard_map/all_to_all | solution.py:297
  201.4 6.6 %all-to-all-done.1 = f32[16,2,128]{2,1,0:T(2,128)S(1)} async-done(((f32[16,2,128]{2,1,0:T(2,128)}), f32[16,2,128]{2,1,0:T(2,128)S(1)}, u32[]{:S(2)}, u32[]{:S(2)}) %all-to-all-start.1) | async-done | bytes 16416 | tf_op jit(solution)/shard_map/all_to_all | solution.py:297
  (36 shorter events, 5.3 us)
Async XLA Ops:
  0.6 20.5 %copy-start = (bf16[2,224,256]{2,1,0:T(8,128)(2,1)S(1)}, bf16[2,224,256]{2,1,0:T(8,128)(2,1)}, u32[]{:S(2)}) copy-start(bf16[2,224,256]{2,1,0:T(8,128)(2,1)} %param.8) | copy-start | bytes 688132
  1.5 9.3 %collective-permute-start = (bf16[224,1]{1,0:T(8,128)(2,1)S(1)}, bf16[224,1]{1,0:T(8,128)(2,1)S(1)}, u32[]{:S(2)}, u32[]{:S(2)}) collective-permute-start(bf16[224,1]{1,0:T(8,128)(2,1)S(1)} %copy.15), channel_id=1, source_target_pairs={{0,256},{256,0},{1,257},{257,1},{2,258},{258,2},{3,259},{259,3},{4... | collective-permute-start | bytes 1352 | tf_op jit(solution)/shard_map/ppermute | solution.py:253
  7.1 76.5 %copy-start.5 = (s32[4]{0:T(128)}, s32[4]{0:T(128)S(1)}, u32[]{:S(2)}) copy-start(s32[4]{0:T(128)S(1)} %pad_add_fusion.at_ref) | copy-start | bytes 52
  7.1 1.9 copy-start.1
  11.5 57.7 %collective-permute-start.5 = (bf16[224,3584]{1,0:T(8,128)(2,1)}, bf16[224,3584]{1,0:T(8,128)(2,1)S(1)}, u32[]{:S(2)}, u32[]{:S(2)}) collective-permute-start(bf16[224,3584]{1,0:T(8,128)(2,1)} %get-tuple-element.21), channel_id=1, source_target_pairs={{0,272},{16,256},{256,16},{272,0},{1,273},{17,257},{257,17},{273,1... | collective-permute-start | bytes 4816904 | tf_op jit(solution)/shard_map/ppermute | solution.py:253
  14.3 55.0 %collective-permute-start.3 = (bf16[224,3584]{1,0:T(8,128)(2,1)}, bf16[224,3584]{1,0:T(8,128)(2,1)}, u32[]{:S(2)}, u32[]{:S(2)}) collective-permute-start(bf16[224,3584]{1,0:T(8,128)(2,1)} %get-tuple-element.21), channel_id=1, source_target_pairs={{0,16},{16,0},{1,17},{17,1},{2,18},{18,2},{3,19},{19,3},{4,20},{20... | collective-permute-start | bytes 4816904 | tf_op jit(solution)/shard_map/ppermute | solution.py:253
  16.2 67.4 %collective-permute-start.4 = (bf16[224,3584]{1,0:T(8,128)(2,1)S(1)}, bf16[224,3584]{1,0:T(8,128)(2,1)}, u32[]{:S(2)}, u32[]{:S(2)}) collective-permute-start(bf16[224,3584]{1,0:T(8,128)(2,1)S(1)} %get-tuple-element.20.near_ref), channel_id=1, source_target_pairs={{0,256},{256,0},{1,257},{257,1},{2,258},{258,2},{3,259},{259,3},{4... | collective-permute-start | bytes 4816904 | tf_op jit(solution)/shard_map/ppermute | solution.py:253
  56.4 11.4 %collective-permute-start.1 = (bf16[4,240,256]{2,1,0:T(8,128)(2,1)S(1)}, bf16[4,240,256]{2,1,0:T(8,128)(2,1)S(1)}, u32[]{:S(2)}, u32[]{:S(2)}) collective-permute-start(bf16[4,240,256]{2,1,0:T(8,128)(2,1)S(1)} %bitcast.27), channel_id=1, source_target_pairs={{0,1},{1,2},{2,3},{3,4},{4,5},{5,6},{6,7},{7,8},{8,9},{9,10},{10,1... | collective-permute-start | bytes 1474568 | tf_op jit(solution)/shard_map/ppermute | solution.py:257
  59.3 10.0 %collective-permute-start.2 = (bf16[4,240,256]{2,1,0:T(8,128)(2,1)S(1)}, bf16[4,240,256]{2,1,0:T(8,128)(2,1)S(1)}, u32[]{:S(2)}, u32[]{:S(2)}) collective-permute-start(bf16[4,240,256]{2,1,0:T(8,128)(2,1)S(1)} %bitcast.25), channel_id=1, source_target_pairs={{0,15},{1,0},{2,1},{3,2},{4,3},{5,4},{6,5},{7,6},{8,7},{9,8},{10,9... | collective-permute-start | bytes 1474568 | tf_op jit(solution)/shard_map/ppermute | solution.py:257
  83.6 10.0 %copy-start.4 = (bf16[224,1]{1,0:T(8,128)(2,1)S(1)}, bf16[224,1]{1,0:T(8,128)(2,1)}, u32[]{:S(2)}) copy-start(bf16[224,1]{1,0:T(8,128)(2,1)} %get-tuple-element.24.gain_ref) | copy-start | bytes 1348
  86.8 6.9 %collective-permute-start.6 = (f32[232,256]{1,0:T(8,128)S(1)}, f32[232,256]{1,0:T(8,128)S(1)}, u32[]{:S(2)}, u32[]{:S(2)}) collective-permute-start(f32[232,256]{1,0:T(8,128)S(1)} %get-tuple-element.23), channel_id=1, source_target_pairs={{0,16},{16,0},{1,17},{17,1},{2,18},{18,2},{3,19},{19,3},{4,20},{20... | collective-permute-start | bytes 712712 | tf_op jit(solution)/shard_map/ppermute | solution.py:253
  93.8 51.6 %copy-start.6 = (s32[4]{0:T(128)S(1)}, s32[4]{0:T(128)}, u32[]{:S(2)}) copy-start(s32[4]{0:T(128)} %copy-done.5) | copy-start | bytes 52
  133.0 11.6 %collective-permute-start.7 = (bf16[4,240,256]{2,1,0:T(8,128)(2,1)S(1)}, bf16[4,240,256]{2,1,0:T(8,128)(2,1)S(1)}, u32[]{:S(2)}, u32[]{:S(2)}) collective-permute-start(bf16[4,240,256]{2,1,0:T(8,128)(2,1)S(1)} %bitcast.28), channel_id=1, source_target_pairs={{0,1},{1,2},{2,3},{3,4},{4,5},{5,6},{6,7},{7,8},{8,9},{9,10},{10,1... | collective-permute-start | bytes 1474568 | tf_op jit(solution)/shard_map/ppermute | solution.py:257
  135.5 10.0 %collective-permute-start.8 = (bf16[4,240,256]{2,1,0:T(8,128)(2,1)S(1)}, bf16[4,240,256]{2,1,0:T(8,128)(2,1)S(1)}, u32[]{:S(2)}, u32[]{:S(2)}) collective-permute-start(bf16[4,240,256]{2,1,0:T(8,128)(2,1)S(1)} %bitcast.26), channel_id=1, source_target_pairs={{0,15},{1,0},{2,1},{3,2},{4,3},{5,4},{6,5},{7,6},{8,7},{9,8},{10,9... | collective-permute-start | bytes 1474568 | tf_op jit(solution)/shard_map/ppermute | solution.py:257
  145.4 10.2 %copy-start.8 = (bf16[224]{0:T(256)(128)(2,1)S(1)}, bf16[224]{0:T(256)(128)(2,1)}, u32[]{:S(2)}) copy-start(bf16[224]{0:T(256)(128)(2,1)} %param.12) | copy-start | bytes 1348
  145.4 10.2 %copy-start.9 = (bf16[224]{0:T(256)(128)(2,1)S(1)}, bf16[224]{0:T(256)(128)(2,1)}, u32[]{:S(2)}) copy-start(bf16[224]{0:T(256)(128)(2,1)} %param.11) | copy-start | bytes 1348
  149.1 0.7 copy-start.2
  149.8 9.5 %collective-permute-start.9 = (f32[232,256]{1,0:T(8,128)}, f32[232,256]{1,0:T(8,128)S(1)}, u32[]{:S(2)}, u32[]{:S(2)}) collective-permute-start(f32[232,256]{1,0:T(8,128)} %get-tuple-element.28), channel_id=1, source_target_pairs={{0,16},{16,0},{1,17},{17,1},{2,18},{18,2},{3,19},{19,3},{4,20},{20... | collective-permute-start | bytes 712712 | tf_op jit(solution)/shard_map/ppermute | solution.py:253
  159.3 0.9 copy-start.3
  160.2 0.7 copy-start.7
  162.3 20.0 %all-to-all-start = ((f32[32,2,256]{2,1,0:T(2,128)}), f32[32,2,256]{2,1,0:T(2,128)S(1)}, u32[]{:S(2)}, u32[]{:S(2)}) async-start(f32[32,2,256]{2,1,0:T(2,128)} %get-tuple-element.31), calls=%async_computation | async-start | bytes 131072 | tf_op jit(solution)/shard_map/all_to_all | solution.py:294
  169.1 31.6 %collective-permute-start.10 = (bf16[224,256]{1,0:T(8,128)(2,1)S(1)}, bf16[224,256]{1,0:T(8,128)(2,1)S(1)}, u32[]{:S(2)}, u32[]{:S(2)}) collective-permute-start(bf16[224,256]{1,0:T(8,128)(2,1)S(1)} %get-tuple-element.29), channel_id=1, source_target_pairs={{0,256},{256,0},{1,257},{257,1},{2,258},{258,2},{3,259},{259,3},{4... | collective-permute-start | bytes 344072 | tf_op jit(solution)/shard_map/ppermute | solution.py:253
  183.0 24.9 %all-to-all-start.1 = ((f32[16,2,128]{2,1,0:T(2,128)}), f32[16,2,128]{2,1,0:T(2,128)S(1)}, u32[]{:S(2)}, u32[]{:S(2)}) async-start(f32[16,2,128]{2,1,0:T(2,128)} %loss_parts.1), calls=%async_computation.1 | async-start | bytes 32768 | tf_op jit(solution)/shard_map/all_to_all | solution.py:297

commit v3 on v2

v3 whole, which is shorter than its diff:
```python
import functools

import jax
import jax.numpy as jnp
from jax import lax
from jax.experimental import pallas as pl
from jax.experimental.pallas import tpu as pltpu
from jax.sharding import Mesh
from jax.sharding import PartitionSpec as P

D = 7168
SEGS = 16
EPS = 1e-05
F = 224
T = 256
KH = D // 2
HALF = F // 2
R = 240
F32 = jnp.float32
BF16 = jnp.bfloat16
Z = ("h", "p")
SMALL = pltpu.CompilerParams(vmem_limit_bytes=4 * 1024 * 1024)
LARGE = pltpu.CompilerParams(vmem_limit_bytes=16 * 1024 * 1024)


def vmem():
    return pl.BlockSpec(memory_space=pltpu.VMEM)


def hbm():
    return pl.BlockSpec(memory_space=pltpu.HBM)


def anywhere():
    return pl.BlockSpec(memory_space=pl.ANY)


def column(row):
    down = lax.broadcasted_iota(jnp.int32, (F, F), 0)
    along = lax.broadcasted_iota(jnp.int32, (F, F), 1)
    wide = jnp.where(down == along, jnp.broadcast_to(row.astype(F32), (F, F)), 0.0)
    return jnp.sum(wide, axis=1, keepdims=True)


def picked(here_ref, away_ref, local):
    return column(jnp.where(local, here_ref[...].astype(F32), away_ref[...].astype(F32)))


def pack_block(rows, gain, block_ref):
    block_ref[0:F, :] = (rows * gain).astype(BF16)
    squares = jnp.sum(rows * rows, axis=0, keepdims=True)
    first = squares.astype(BF16)
    rest = squares - first.astype(F32)
    second = rest.astype(BF16)
    third = (rest - second.astype(F32)).astype(BF16)
    at = lax.broadcasted_iota(jnp.int32, (R - F, T), 0)
    tail = jnp.where(at == 0, first.astype(F32), 0.0)
    tail = jnp.where(at == 1, second.astype(F32), tail)
    tail = jnp.where(at == 2, third.astype(F32), tail)
    block_ref[F:R, :] = tail.astype(BF16)


def call(kernel, outs, ins, out_specs, params, name, scratch=()):
    return pl.pallas_call(
        kernel,
        out_shape=outs,
        in_specs=ins,
        out_specs=out_specs,
        scratch_shapes=scratch,
        compiler_params=params,
        name=name,
    )


def shape(dims, dtype):
    return jax.ShapeDtypeStruct(dims, dtype)


def pack_kernel(tokens_ref, here_ref, away_ref, block_ref):
    section = lax.axis_index("s")
    gain = picked(here_ref, away_ref, section == 0)
    pack_block(tokens_ref[section].astype(F32), gain, block_ref)


def pack(tokens, here, away):
    return call(
        pack_kernel, shape((R, T), BF16), [vmem()] * 3, vmem(), SMALL, "pack"
    )(tokens, here, away)


def split_kernel(weight_ref, near_ref, far_ref, sems):
    x = lax.axis_index("x")
    rows = pl.ds(pl.multiple_of(lax.axis_index("c") * HALF, 16), HALF)
    near = pl.ds(pl.multiple_of(x * KH, 128), KH)
    far = pl.ds(pl.multiple_of((1 - x) * KH, 128), KH)
    copies = [
        pltpu.make_async_copy(weight_ref.at[rows, near], near_ref, sems.at[0]),
        pltpu.make_async_copy(weight_ref.at[rows, far], far_ref, sems.at[1]),
    ]
    for copy in copies:
        copy.start()
    for copy in copies:
        copy.wait()


def split(weight):
    out = shape((HALF, KH), BF16)
    return call(
        split_kernel, (out, out), [hbm()], (anywhere(), anywhere()), SMALL, "split",
        [pltpu.SemaphoreType.DMA((2,))],
    )(weight)


def product_kernel(
    local_block, same_ref, below_ref, above_ref, weight_ref, side_ref, side2_ref, over_ref,
    over2_ref, cross_ref, cross2_ref, own_ref, send_ref, held, values, sems,
):
    local = lax.axis_index("s") == local_block
    parity = lax.axis_index("p")
    core = lax.axis_index("c")
    columns = pl.ds(pl.multiple_of(lax.axis_index("x") * KH, 128), KH)

    def rows(start, half):
        return pl.ds(pl.multiple_of(start + half * HALF, 16), HALF)

    def near_copies():
        return [
            pltpu.make_async_copy(weight_ref.at[:, columns], held.at[0:F, :], sems.at[0]),
            pltpu.make_async_copy(side_ref, held.at[rows(F, core), :], sems.at[1]),
            pltpu.make_async_copy(side2_ref, held.at[rows(F, 1 - core), :], sems.at[2]),
        ]

    def away_copies():
        return [
            pltpu.make_async_copy(over_ref, held.at[rows(0, core), :], sems.at[0]),
            pltpu.make_async_copy(over2_ref, held.at[rows(0, 1 - core), :], sems.at[1]),
            pltpu.make_async_copy(cross_ref, held.at[rows(F, core), :], sems.at[2]),
            pltpu.make_async_copy(cross2_ref, held.at[rows(F, 1 - core), :], sems.at[3]),
        ]

    @pl.when(local)
    def _():
        for copy in near_copies():
            copy.start()

    @pl.when(jnp.logical_not(local))
    def _():
        for copy in away_copies():
            copy.start()

    squares = jnp.zeros((1, T), F32)
    for i in range(8):
        got = same_ref[i]
        here = pl.ds(pl.multiple_of((2 * i + parity) * F, 16), F)
        values[here, :] = got[0:F]
        squares += jnp.sum(got[F:R].astype(F32), axis=0, keepdims=True)
        other = below_ref[i] if i < 4 else above_ref[i - 4]
        there = pl.ds(pl.multiple_of((2 * i + 1 - parity) * F, 16), F)
        values[there, :] = other[0:F]
        squares += jnp.sum(other[F:R].astype(F32), axis=0, keepdims=True)

    @pl.when(local)
    def _():
        for copy in near_copies():
            copy.wait()

    @pl.when(jnp.logical_not(local))
    def _():
        for copy in away_copies():
            copy.wait()

    product = jnp.dot(held[...], values[...], preferred_element_type=F32)
    total = jnp.broadcast_to(squares, (8, T))
    own_ref[0:F, :] = product[0:F]
    own_ref[F:F + 8, :] = total
    send_ref[0:F, :] = product[F:2 * F]
    send_ref[F:F + 8, :] = total


def product(local_block, same, below, above, blocks):
    out = shape((F + 8, T), F32)
    return call(
        functools.partial(product_kernel, local_block),
        (out, out),
        [vmem(), vmem(), vmem(), hbm()] + [anywhere()] * 6,
        (vmem(), vmem()),
        LARGE,
        "product",
        [
            pltpu.VMEM((2 * F, KH), BF16),
            pltpu.VMEM((KH, T), BF16),
            pltpu.SemaphoreType.DMA((4,)),
        ],
    )(same, below, above, *blocks)


def block_rows(own_ref, other_ref, rows):
    squares = own_ref[F:F + 1, :] + other_ref[F:F + 1, :]
    inv_root = lax.rsqrt(squares / D + EPS)
    mixed = (own_ref[0:F, :] + other_ref[0:F, :]) * inv_root
    gated = mixed / (1.0 + jnp.exp(-mixed))
    return (rows.astype(F32) + gated).astype(BF16)


def middle_kernel(own_ref, other_ref, tokens_ref, here_ref, away_ref, out_ref, block_ref):
    section = lax.axis_index("s")
    out = block_rows(own_ref, other_ref, tokens_ref[section])
    out_ref[...] = out
    gain = picked(here_ref, away_ref, section == 1)
    pack_block(out.astype(F32), gain, block_ref)


def middle(own, other, tokens, here, away):
    return call(
        middle_kernel,
        (shape((F, T), BF16), shape((R, T), BF16)),
        [vmem()] * 5,
        (vmem(), vmem()),
        SMALL,
        "middle",
    )(own, other, tokens, here, away)


def last_kernel(
    own_ref, other_ref, rows_ref, gain_ref, score_ref, out_ref, swap_ref, stats_ref
):
    out = block_rows(own_ref, other_ref, rows_ref[...])
    out_ref[...] = out
    section = lax.axis_index("s")

    @pl.when(section == 0)
    def _():
        swap_ref[...] = out

    @pl.when(section != 0)
    def _():
        swap_ref[...] = rows_ref[...]

    as_float = out.astype(F32)
    head = column(gain_ref[...].astype(F32) * score_ref[...].astype(F32))
    squares = jnp.sum(as_float * as_float, axis=0, keepdims=True)
    scores = jnp.sum(as_float * head, axis=0, keepdims=True)
    stats = jnp.concatenate([squares, scores], axis=0)
    for i in range(32):
        stats_ref[i] = stats


def last(own, other, rows, gain, score):
    out = shape((F, T), BF16)
    return call(
        last_kernel,
        (out, out, shape((32, 2, T), F32)),
        [vmem()] * 5,
        (vmem(), vmem(), vmem()),
        SMALL,
        "last",
    )(own, other, rows, gain, score)


def loss_kernel(stats_ref, label_ref, mask_ref, segment_ref, sums_ref):
    first = lax.axis_index("s") == 0

    def pick(ref):
        return jnp.where(first, ref[0:1, :], ref[1:2, :])

    total = jnp.sum(stats_ref[...], axis=0)
    inv_root = lax.rsqrt(total[0:1] / D + EPS)
    score = total[1:2] * inv_root
    target = pick(label_ref).astype(F32) - 1.0
    mask = pick(mask_ref).astype(F32)
    err = score - target
    squared = mask * err * err
    member = pick(segment_ref) == lax.broadcasted_iota(jnp.int32, (SEGS, T), 0)
    sums = jnp.sum(jnp.where(member, squared, 0.0), axis=1, keepdims=True)
    counts = jnp.sum(jnp.where(member, mask, 0.0), axis=1, keepdims=True)
    lane = lax.broadcasted_iota(jnp.int32, (SEGS, 128), 1)
    diagonal = lane == lax.broadcasted_iota(jnp.int32, (SEGS, 128), 0)
    sums = jnp.sum(jnp.where(diagonal, sums, 0.0), axis=0, keepdims=True)
    counts = jnp.sum(jnp.where(diagonal, counts, 0.0), axis=0, keepdims=True)
    both = jnp.concatenate([sums, counts], axis=0)
    for i in range(16):
        sums_ref[i] = both


def loss_parts(stats, label, mask, segment):
    return call(
        loss_kernel, shape((16, 2, 128), F32), [vmem()] * 4, vmem(), SMALL, "loss_parts"
    )(stats, label, mask, segment)


def swapped(value, *axes):
    count = 2 ** len(axes)
    name = axes if len(axes) > 1 else axes[0]
    return lax.ppermute(value, name, [(i, i ^ (count - 1)) for i in range(count)])


def shifted(value, by):
    return lax.ppermute(value, Z, [(i, (i + by) % 16) for i in range(16)])


def body(
    tokens_in, section_proj, section_gain, final_gain, score_weight, labels, loss_mask, segment_ids
):
    section = lax.axis_index("s")
    weight = section_proj[0]
    gain_away = swapped(section_gain, "s")

    near, far = split(weight)
    near, far, gain_away = lax.optimization_barrier((near, far, gain_away))
    side = swapped(far, "x")
    over = swapped(near, "s")
    cross = swapped(far, "s", "x")

    same = lax.all_gather(pack(tokens_in, section_gain, gain_away), "h", axis=0, tiled=False)
    low, high = same[0:4], same[4:8]
    low, high, side, over, cross = lax.optimization_barrier((low, high, side, over, cross))
    below, above = shifted(low, 1), shifted(high, -1)
    blocks = (
        weight, side, swapped(side, "c"), over, swapped(over, "c"), cross, swapped(cross, "c")
    )
    own, send = product(0, same, below, above, blocks)
    first, block = middle(own, swapped(send, "x"), tokens_in, section_gain, gain_away)

    same = lax.all_gather(block, "h", axis=0, tiled=False)
    below, above = shifted(same[0:4], 1), shifted(same[4:8], -1)
    own, send = product(1, same, below, above, blocks)
    second, handed, stats = last(
        own, swapped(send, "x"), first, final_gain[None], score_weight[None]
    )
    handed = swapped(handed, "s")

    stats = lax.all_to_all(stats, ("x", "h", "p"), 0, 0, tiled=True)
    parts = loss_parts(stats, labels, loss_mask, segment_ids)
    parts = lax.all_to_all(parts, ("s", "y", "c"), 0, 0, tiled=True)
    parts = jnp.sum(parts.reshape(2, 8, 2, 128), axis=1)[:, :, :SEGS]
    segment_loss = parts[:, 0] / jnp.maximum(parts[:, 1], 1.0)

    section_out = jnp.where(section == 0, jnp.stack([first, handed]), jnp.stack([handed, second]))
    return section_out[None], segment_loss


def solution(mesh):
    finer = Mesh(mesh.devices.reshape(2, 4, 2, 2, 8, 2), ("s", "y", "c", "x", "h", "p"))
    tensor = ("x", "h", "p")
    dp = ("y", "c")
    in_specs = (
        P(None, tensor, dp),
        P("s", tensor, None),
        P("s", tensor),
        P(tensor),
        P(tensor),
        P(None, dp),
        P(None, dp),
        P(None, dp),
    )
    out_specs = (P("s", None, tensor, dp), P())
    return jax.shard_map(body, mesh=finer, in_specs=in_specs, out_specs=out_specs, check_vma=False)
```

time: 209 us -> 193 us (0.923)
  starting transfers between devices: 62.5 us -> 78.9 us
  blocking collectives: 74.1 us -> 62.4 us
  waiting for transfers between devices: 51.1 us -> 40.3 us
  Pallas kernels: 11.1 us -> 5.05 us
  local copies, waits for them, and re-layouts: 6.75 us -> 3.01 us
    ppermute x7 -> x10, waiting for transfers between devices: 22.9 us -> 8.53 us  [swapped(): return lax.ppermute(value, name, [(i, i ^ count - 1) for i in range(count)])]
    ppermute x7 -> x10, starting transfers between devices: 25.2 us -> 39.1 us  [swapped(): return lax.ppermute(value, name, [(i, i ^ count - 1) for i in range(count)])]
    all_gather x2, blocking collectives: 74.1 us -> 62.4 us  [the longest x1 35.4 us: body(): lax.all_gather(pack(tokens_in, section_gain, gain_away), 'h', axis=0, til...]
    pallas_call x7, Pallas kernels: 11.1 us -> 5.05 us  [the longest x2 2.96 us: product(): call(functools.partial(product_kernel, local_block), (out, out), [vmem(),...]
    ppermute x4, waiting for transfers between devices: 12.3 us -> 16.9 us  [shifted(): return lax.ppermute(value, Z, [(i, (i + by) % 16) for i in range(16)])]
    ppermute x4, starting transfers between devices: 13 us -> 15.3 us  [shifted(): return lax.ppermute(value, Z, [(i, (i + by) % 16) for i in range(16)])]
  transfers between devices with their start and end apart: 13 -> 16, of which waited for: 9 -> 8; matrix products, arithmetic and copies ran while one was open for 1% -> 0% of each run, Pallas kernels for 1% -> 1%
where the time goes in v3:
time: 193 us; the launch traced here: 192 us
  starting transfers between devices  78.9 us (41%)
  blocking collectives  62.4 us (32%)
  waiting for transfers between devices  40.3 us (21%)
  Pallas kernels  5.05 us (3%)
  local copies, waits for them, and re-layouts  3.01 us (2%)
    ppermute x10, starting transfers between devices, swapped(): return lax.ppermute(value, name, [(i, i ^ count - 1) for i in range(count)])  39.1 us
    all_gather x1, blocking collectives, body(): lax.all_gather(pack(tokens_in, section_gain, gain_away), 'h', axis=0, til...  35.4 us
    all_gather x1, blocking collectives, body(): same = lax.all_gather(block, 'h', axis=0, tiled=False)  27 us
    ppermute x4, waiting for transfers between devices, shifted(): return lax.ppermute(value, Z, [(i, (i + by) % 16) for i in range(16)])  16.9 us
    all_to_all x1, starting transfers between devices, body(): parts = lax.all_to_all(parts, ('s', 'y', 'c'), 0, 0, tiled=True)  16.3 us
    ppermute x4, starting transfers between devices, shifted(): return lax.ppermute(value, Z, [(i, (i + by) % 16) for i in range(16)])  15.3 us
    ppermute x10, waiting for transfers between devices, swapped(): return lax.ppermute(value, name, [(i, i ^ count - 1) for i in range(count)])  8.53 us
    all_to_all x1, waiting for transfers between devices, body(): stats = lax.all_to_all(stats, ('x', 'h', 'p'), 0, 0, tiled=True)  8.31 us
  transfers between devices with their start and end apart: 16, of which 8 were waited for; matrix products, arithmetic and copies ran while one was open for 0% of the time, Pallas kernels for 1%

profile of v3, /device:TPU:1, one launch (start us, length us, event | category | flops | bytes accessed | tf_op | source)
XLA Modules:
  0.0 192.0 jit_solution(15157830688039723001)
XLA Ops:
  0.6 5.5 %collective-permute-start = (bf16[1,224]{1,0:T(2,128)(2,1)}, bf16[1,224]{1,0:T(2,128)(2,1)S(1)}, u32[]{:S(2)}, u32[]{:S(2)}) collective-permute-start(bf16[1,224]{1,0:T(2,128)(2,1)} %here_ref.3), channel_id=1, source_target_pairs={{0,256},{256,0},{1,257},{257,1},{2,258},{258,2},{3,259},{259,3},{4... | collective-permute-start | bytes 1352 | tf_op jit(solution)/shard_map/ppermute | solution.py:294
  6.1 1.9 copy-done
  8.2 2.5 %collective-permute-start.1 = (bf16[112,3584]{1,0:T(8,128)(2,1)S(1)}, bf16[112,3584]{1,0:T(8,128)(2,1)S(1)}, u32[]{:S(2)}, u32[]{:S(2)}) collective-permute-start(bf16[112,3584]{1,0:T(8,128)(2,1)S(1)} %get-tuple-element.24), channel_id=1, source_target_pairs={{0,16},{16,0},{1,17},{17,1},{2,18},{18,2},{3,19},{19,3},{4,20},{20... | collective-permute-start | bytes 2408456 | tf_op jit(solution)/shard_map/ppermute | solution.py:294
  10.7 3.6 %collective-permute-start.3 = (bf16[112,3584]{1,0:T(8,128)(2,1)S(1)}, bf16[112,3584]{1,0:T(8,128)(2,1)S(1)}, u32[]{:S(2)}, u32[]{:S(2)}) collective-permute-start(bf16[112,3584]{1,0:T(8,128)(2,1)S(1)} %get-tuple-element.24), channel_id=1, source_target_pairs={{0,272},{16,256},{256,16},{272,0},{1,273},{17,257},{257,17},{273,1... | collective-permute-start | bytes 2408456 | tf_op jit(solution)/shard_map/ppermute | solution.py:294
  14.3 3.0 %collective-permute-start.2 = (bf16[112,3584]{1,0:T(8,128)(2,1)S(1)}, bf16[112,3584]{1,0:T(8,128)(2,1)S(1)}, u32[]{:S(2)}, u32[]{:S(2)}) collective-permute-start(bf16[112,3584]{1,0:T(8,128)(2,1)S(1)} %get-tuple-element.25), channel_id=1, source_target_pairs={{0,256},{256,0},{1,257},{257,1},{2,258},{258,2},{3,259},{259,3},{4... | collective-permute-start | bytes 2408456 | tf_op jit(solution)/shard_map/ppermute | solution.py:294
  17.4 0.9 copy-done.2
  18.4 35.4 %all-gather = bf16[1920,256]{1,0:T(8,128)(2,1)S(1)} all-gather(bf16[240,256]{1,0:T(8,128)(2,1)S(1)} %pack.1), channel_id=2, replica_groups=mesh['s'=2,'y'=4,'c'=2,'x'=2,'h'=8,'p'=2] {'h'}, dimensions={0}, use_global_device_ids=true | all-gather | bytes 1105920 | tf_op jit(solution)/shard_map/all_gather | solution.py:314
  54.0 8.6 %collective-permute-start.6 = (bf16[112,3584]{1,0:T(8,128)(2,1)S(1)}, bf16[112,3584]{1,0:T(8,128)(2,1)S(1)}, u32[]{:S(2)}, u32[]{:S(2)}) collective-permute-start(bf16[112,3584]{1,0:T(8,128)(2,1)S(1)} %collective-permute-done.1.side_ref), channel_id=1, source_target_pairs={{0,32},{32,0},{1,33},{33,1},{2,34},{34,2},{3,35},{35,3},{4,36},{36... | collective-permute-start | bytes 2408456 | tf_op jit(solution)/shard_map/ppermute | solution.py:294
  62.6 1.9 %collective-permute-start.7 = (bf16[112,3584]{1,0:T(8,128)(2,1)S(1)}, bf16[112,3584]{1,0:T(8,128)(2,1)S(1)}, u32[]{:S(2)}, u32[]{:S(2)}) collective-permute-start(bf16[112,3584]{1,0:T(8,128)(2,1)S(1)} %collective-permute-done.2.over_ref), channel_id=1, source_target_pairs={{0,32},{32,0},{1,33},{33,1},{2,34},{34,2},{3,35},{35,3},{4,36},{36... | collective-permute-start | bytes 2408456 | tf_op jit(solution)/shard_map/ppermute | solution.py:294
  64.5 2.4 %collective-permute-start.8 = (bf16[112,3584]{1,0:T(8,128)(2,1)S(1)}, bf16[112,3584]{1,0:T(8,128)(2,1)S(1)}, u32[]{:S(2)}, u32[]{:S(2)}) collective-permute-start(bf16[112,3584]{1,0:T(8,128)(2,1)S(1)} %collective-permute-done.3.cross_ref), channel_id=1, source_target_pairs={{0,32},{32,0},{1,33},{33,1},{2,34},{34,2},{3,35},{35,3},{4,36},{36... | collective-permute-start | bytes 2408456 | tf_op jit(solution)/shard_map/ppermute | solution.py:294
  66.9 3.2 %collective-permute-start.4 = (bf16[4,240,256]{2,1,0:T(8,128)(2,1)S(1)}, bf16[4,240,256]{2,1,0:T(8,128)(2,1)S(1)}, u32[]{:S(2)}, u32[]{:S(2)}) collective-permute-start(bf16[4,240,256]{2,1,0:T(8,128)(2,1)S(1)} %bitcast.21), channel_id=1, source_target_pairs={{0,1},{1,2},{2,3},{3,4},{4,5},{5,6},{6,7},{7,8},{8,9},{9,10},{10,1... | collective-permute-start | bytes 1474568 | tf_op jit(solution)/shard_map/ppermute | solution.py:298
  70.2 3.2 %collective-permute-start.5 = (bf16[4,240,256]{2,1,0:T(8,128)(2,1)S(1)}, bf16[4,240,256]{2,1,0:T(8,128)(2,1)S(1)}, u32[]{:S(2)}, u32[]{:S(2)}) collective-permute-start(bf16[4,240,256]{2,1,0:T(8,128)(2,1)S(1)} %bitcast.20), channel_id=1, source_target_pairs={{0,15},{1,0},{2,1},{3,2},{4,3},{5,4},{6,5},{7,6},{8,7},{9,8},{10,9... | collective-permute-start | bytes 1474568 | tf_op jit(solution)/shard_map/ppermute | solution.py:298
  73.4 9.4 %collective-permute-done.4.below_ref = bf16[4,240,256]{2,1,0:T(8,128)(2,1)S(1)} collective-permute-done((bf16[4,240,256]{2,1,0:T(8,128)(2,1)S(1)}, bf16[4,240,256]{2,1,0:T(8,128)(2,1)S(1)}, u32[]{:S(2)}, u32[]{:S(2)}) %collective-permute-start.4) | collective-permute-done | bytes 491552 | tf_op jit(solution)/shard_map/ppermute | solution.py:298
  82.9 1.7 collective-permute-done.5.above_ref
  84.6 1.5 product.2
  86.1 3.0 %collective-permute-start.9 = (f32[232,256]{1,0:T(8,128)S(1)}, f32[232,256]{1,0:T(8,128)S(1)}, u32[]{:S(2)}, u32[]{:S(2)}) collective-permute-start(f32[232,256]{1,0:T(8,128)S(1)} %get-tuple-element.32), channel_id=1, source_target_pairs={{0,16},{16,0},{1,17},{17,1},{2,18},{18,2},{3,19},{19,3},{4,20},{20... | collective-permute-start | bytes 712712 | tf_op jit(solution)/shard_map/ppermute | solution.py:294
  89.1 5.1 %collective-permute-done.9.other_ref = f32[232,256]{1,0:T(8,128)S(1)} collective-permute-done((f32[232,256]{1,0:T(8,128)S(1)}, f32[232,256]{1,0:T(8,128)S(1)}, u32[]{:S(2)}, u32[]{:S(2)}) %collective-permute-start.9) | collective-permute-done | bytes 237600 | tf_op jit(solution)/shard_map/ppermute | solution.py:294
  94.3 27.0 %all-gather.1 = bf16[1920,256]{1,0:T(8,128)(2,1)S(1)} all-gather(bf16[240,256]{1,0:T(8,128)(2,1)S(1)} %get-tuple-element.34), channel_id=3, replica_groups=mesh['s'=2,'y'=4,'c'=2,'x'=2,'h'=8,'p'=2] {'h'}, dimensions={0}, use_global_device_ids=true | all-gather | bytes 1105920 | tf_op jit(solution)/shard_map/all_gather | solution.py:324
  121.4 4.3 %collective-permute-start.10 = (bf16[4,240,256]{2,1,0:T(8,128)(2,1)S(1)}, bf16[4,240,256]{2,1,0:T(8,128)(2,1)S(1)}, u32[]{:S(2)}, u32[]{:S(2)}) collective-permute-start(bf16[4,240,256]{2,1,0:T(8,128)(2,1)S(1)} %bitcast.23), channel_id=1, source_target_pairs={{0,1},{1,2},{2,3},{3,4},{4,5},{5,6},{6,7},{7,8},{8,9},{9,10},{10,1... | collective-permute-start | bytes 1474568 | tf_op jit(solution)/shard_map/ppermute | solution.py:298
  125.7 4.5 %collective-permute-start.11 = (bf16[4,240,256]{2,1,0:T(8,128)(2,1)S(1)}, bf16[4,240,256]{2,1,0:T(8,128)(2,1)S(1)}, u32[]{:S(2)}, u32[]{:S(2)}) collective-permute-start(bf16[4,240,256]{2,1,0:T(8,128)(2,1)S(1)} %bitcast.22), channel_id=1, source_target_pairs={{0,15},{1,0},{2,1},{3,2},{4,3},{5,4},{6,5},{7,6},{8,7},{9,8},{10,9... | collective-permute-start | bytes 1474568 | tf_op jit(solution)/shard_map/ppermute | solution.py:298
  130.2 4.3 %collective-permute-done.10.below_ref = bf16[4,240,256]{2,1,0:T(8,128)(2,1)S(1)} collective-permute-done((bf16[4,240,256]{2,1,0:T(8,128)(2,1)S(1)}, bf16[4,240,256]{2,1,0:T(8,128)(2,1)S(1)}, u32[]{:S(2)}, u32[]{:S(2)}) %collective-permute-start.10) | collective-permute-done | bytes 491552 | tf_op jit(solution)/shard_map/ppermute | solution.py:298
  134.5 1.5 collective-permute-done.11.above_ref
  136.0 1.5 product.3
  137.5 3.7 %collective-permute-start.12 = (f32[232,256]{1,0:T(8,128)S(1)}, f32[232,256]{1,0:T(8,128)S(1)}, u32[]{:S(2)}, u32[]{:S(2)}) collective-permute-start(f32[232,256]{1,0:T(8,128)S(1)} %get-tuple-element.36), channel_id=1, source_target_pairs={{0,16},{16,0},{1,17},{17,1},{2,18},{18,2},{3,19},{19,3},{4,20},{20... | collective-permute-start | bytes 712712 | tf_op jit(solution)/shard_map/ppermute | solution.py:294
  141.2 3.4 %collective-permute-done.12.other_ref = f32[232,256]{1,0:T(8,128)S(1)} collective-permute-done((f32[232,256]{1,0:T(8,128)S(1)}, f32[232,256]{1,0:T(8,128)S(1)}, u32[]{:S(2)}, u32[]{:S(2)}) %collective-permute-start.12) | collective-permute-done | bytes 237600 | tf_op jit(solution)/shard_map/ppermute | solution.py:294
  144.6 0.9 last.1
  145.5 8.3 %all-to-all-start = ((f32[32,2,256]{2,1,0:T(2,128)}), f32[32,2,256]{2,1,0:T(2,128)S(1)}, u32[]{:S(2)}, u32[]{:S(2)}) async-start(f32[32,2,256]{2,1,0:T(2,128)} %get-tuple-element.39), calls=%async_computation | async-start | bytes 131072 | tf_op jit(solution)/shard_map/all_to_all | solution.py:332
  153.8 4.9 %collective-permute-start.13 = (bf16[224,256]{1,0:T(8,128)(2,1)S(1)}, bf16[224,256]{1,0:T(8,128)(2,1)S(1)}, u32[]{:S(2)}, u32[]{:S(2)}) collective-permute-start(bf16[224,256]{1,0:T(8,128)(2,1)S(1)} %get-tuple-element.37), channel_id=1, source_target_pairs={{0,256},{256,0},{1,257},{257,1},{2,258},{258,2},{3,259},{259,3},{4... | collective-permute-start | bytes 344072 | tf_op jit(solution)/shard_map/ppermute | solution.py:294
  158.7 8.3 %all-to-all-done.stats_ref = f32[32,2,256]{2,1,0:T(2,128)S(1)} async-done(((f32[32,2,256]{2,1,0:T(2,128)}), f32[32,2,256]{2,1,0:T(2,128)S(1)}, u32[]{:S(2)}, u32[]{:S(2)}) %all-to-all-start) | async-done | bytes 65568 | tf_op jit(solution)/shard_map/all_to_all | solution.py:332
  167.0 0.8 loss_parts.1
  167.8 16.3 %all-to-all-start.1 = ((f32[16,2,128]{2,1,0:T(2,128)}), f32[16,2,128]{2,1,0:T(2,128)S(1)}, u32[]{:S(2)}, u32[]{:S(2)}) async-start(f32[16,2,128]{2,1,0:T(2,128)} %loss_parts.1), calls=%async_computation.1 | async-start | bytes 32768 | tf_op jit(solution)/shard_map/all_to_all | solution.py:334
  184.8 6.6 %all-to-all-done.1 = f32[16,2,128]{2,1,0:T(2,128)S(1)} async-done(((f32[16,2,128]{2,1,0:T(2,128)}), f32[16,2,128]{2,1,0:T(2,128)S(1)}, u32[]{:S(2)}, u32[]{:S(2)}) %all-to-all-start.1) | async-done | bytes 16416 | tf_op jit(solution)/shard_map/all_to_all | solution.py:334
  (36 shorter events, 2.0 us)
Async XLA Ops:
  0.6 16.7 %copy-start.4 = (bf16[1,224]{1,0:T(2,128)(2,1)S(1)}, bf16[1,224]{1,0:T(2,128)(2,1)}, u32[]{:S(2)}) copy-start(bf16[1,224]{1,0:T(2,128)(2,1)} %here_ref.3) | copy-start | bytes 1348
  0.6 7.6 %collective-permute-start = (bf16[1,224]{1,0:T(2,128)(2,1)}, bf16[1,224]{1,0:T(2,128)(2,1)S(1)}, u32[]{:S(2)}, u32[]{:S(2)}) collective-permute-start(bf16[1,224]{1,0:T(2,128)(2,1)} %here_ref.3), channel_id=1, source_target_pairs={{0,256},{256,0},{1,257},{257,1},{2,258},{258,2},{3,259},{259,3},{4... | collective-permute-start | bytes 1352 | tf_op jit(solution)/shard_map/ppermute | solution.py:294
  6.1 1.9 copy-start
  8.0 76.6 %copy-start.1 = (bf16[1,224,7168]{2,1,0:T(8,128)(2,1)S(1)}, bf16[1,224,7168]{2,1,0:T(8,128)(2,1)}, u32[]{:S(2)}) copy-start(bf16[1,224,7168]{2,1,0:T(8,128)(2,1)} %param.9) | copy-start | bytes 9633796
  8.2 45.7 %collective-permute-start.1 = (bf16[112,3584]{1,0:T(8,128)(2,1)S(1)}, bf16[112,3584]{1,0:T(8,128)(2,1)S(1)}, u32[]{:S(2)}, u32[]{:S(2)}) collective-permute-start(bf16[112,3584]{1,0:T(8,128)(2,1)S(1)} %get-tuple-element.24), channel_id=1, source_target_pairs={{0,16},{16,0},{1,17},{17,1},{2,18},{18,2},{3,19},{19,3},{4,20},{20... | collective-permute-start | bytes 2408456 | tf_op jit(solution)/shard_map/ppermute | solution.py:294
  10.7 43.2 %collective-permute-start.3 = (bf16[112,3584]{1,0:T(8,128)(2,1)S(1)}, bf16[112,3584]{1,0:T(8,128)(2,1)S(1)}, u32[]{:S(2)}, u32[]{:S(2)}) collective-permute-start(bf16[112,3584]{1,0:T(8,128)(2,1)S(1)} %get-tuple-element.24), channel_id=1, source_target_pairs={{0,272},{16,256},{256,16},{272,0},{1,273},{17,257},{257,17},{273,1... | collective-permute-start | bytes 2408456 | tf_op jit(solution)/shard_map/ppermute | solution.py:294
  14.3 39.6 %collective-permute-start.2 = (bf16[112,3584]{1,0:T(8,128)(2,1)S(1)}, bf16[112,3584]{1,0:T(8,128)(2,1)S(1)}, u32[]{:S(2)}, u32[]{:S(2)}) collective-permute-start(bf16[112,3584]{1,0:T(8,128)(2,1)S(1)} %get-tuple-element.25), channel_id=1, source_target_pairs={{0,256},{256,0},{1,257},{257,1},{2,258},{258,2},{3,259},{259,3},{4... | collective-permute-start | bytes 2408456 | tf_op jit(solution)/shard_map/ppermute | solution.py:294
  17.4 0.9 copy-start.2
  54.0 30.7 %collective-permute-start.6 = (bf16[112,3584]{1,0:T(8,128)(2,1)S(1)}, bf16[112,3584]{1,0:T(8,128)(2,1)S(1)}, u32[]{:S(2)}, u32[]{:S(2)}) collective-permute-start(bf16[112,3584]{1,0:T(8,128)(2,1)S(1)} %collective-permute-done.1.side_ref), channel_id=1, source_target_pairs={{0,32},{32,0},{1,33},{33,1},{2,34},{34,2},{3,35},{35,3},{4,36},{36... | collective-permute-start | bytes 2408456 | tf_op jit(solution)/shard_map/ppermute | solution.py:294
  62.6 22.0 %collective-permute-start.7 = (bf16[112,3584]{1,0:T(8,128)(2,1)S(1)}, bf16[112,3584]{1,0:T(8,128)(2,1)S(1)}, u32[]{:S(2)}, u32[]{:S(2)}) collective-permute-start(bf16[112,3584]{1,0:T(8,128)(2,1)S(1)} %collective-permute-done.2.over_ref), channel_id=1, source_target_pairs={{0,32},{32,0},{1,33},{33,1},{2,34},{34,2},{3,35},{35,3},{4,36},{36... | collective-permute-start | bytes 2408456 | tf_op jit(solution)/shard_map/ppermute | solution.py:294
  64.5 20.1 %collective-permute-start.8 = (bf16[112,3584]{1,0:T(8,128)(2,1)S(1)}, bf16[112,3584]{1,0:T(8,128)(2,1)S(1)}, u32[]{:S(2)}, u32[]{:S(2)}) collective-permute-start(bf16[112,3584]{1,0:T(8,128)(2,1)S(1)} %collective-permute-done.3.cross_ref), channel_id=1, source_target_pairs={{0,32},{32,0},{1,33},{33,1},{2,34},{34,2},{3,35},{35,3},{4,36},{36... | collective-permute-start | bytes 2408456 | tf_op jit(solution)/shard_map/ppermute | solution.py:294
  66.9 15.9 %collective-permute-start.4 = (bf16[4,240,256]{2,1,0:T(8,128)(2,1)S(1)}, bf16[4,240,256]{2,1,0:T(8,128)(2,1)S(1)}, u32[]{:S(2)}, u32[]{:S(2)}) collective-permute-start(bf16[4,240,256]{2,1,0:T(8,128)(2,1)S(1)} %bitcast.21), channel_id=1, source_target_pairs={{0,1},{1,2},{2,3},{3,4},{4,5},{5,6},{6,7},{7,8},{8,9},{9,10},{10,1... | collective-permute-start | bytes 1474568 | tf_op jit(solution)/shard_map/ppermute | solution.py:298
  70.2 14.4 %collective-permute-start.5 = (bf16[4,240,256]{2,1,0:T(8,128)(2,1)S(1)}, bf16[4,240,256]{2,1,0:T(8,128)(2,1)S(1)}, u32[]{:S(2)}, u32[]{:S(2)}) collective-permute-start(bf16[4,240,256]{2,1,0:T(8,128)(2,1)S(1)} %bitcast.20), channel_id=1, source_target_pairs={{0,15},{1,0},{2,1},{3,2},{4,3},{5,4},{6,5},{7,6},{8,7},{9,8},{10,9... | collective-permute-start | bytes 1474568 | tf_op jit(solution)/shard_map/ppermute | solution.py:298
  84.6 9.5 %copy-start.3 = (bf16[2,224,256]{2,1,0:T(8,128)(2,1)S(1)}, bf16[2,224,256]{2,1,0:T(8,128)(2,1)}, u32[]{:S(2)}) copy-start(bf16[2,224,256]{2,1,0:T(8,128)(2,1)} %tokens_ref.3) | copy-start | bytes 688132
  86.1 8.1 %collective-permute-start.9 = (f32[232,256]{1,0:T(8,128)S(1)}, f32[232,256]{1,0:T(8,128)S(1)}, u32[]{:S(2)}, u32[]{:S(2)}) collective-permute-start(f32[232,256]{1,0:T(8,128)S(1)} %get-tuple-element.32), channel_id=1, source_target_pairs={{0,16},{16,0},{1,17},{17,1},{2,18},{18,2},{3,19},{19,3},{4,20},{20... | collective-permute-start | bytes 712712 | tf_op jit(solution)/shard_map/ppermute | solution.py:294
  121.4 13.1 %collective-permute-start.10 = (bf16[4,240,256]{2,1,0:T(8,128)(2,1)S(1)}, bf16[4,240,256]{2,1,0:T(8,128)(2,1)S(1)}, u32[]{:S(2)}, u32[]{:S(2)}) collective-permute-start(bf16[4,240,256]{2,1,0:T(8,128)(2,1)S(1)} %bitcast.23), channel_id=1, source_target_pairs={{0,1},{1,2},{2,3},{3,4},{4,5},{5,6},{6,7},{7,8},{8,9},{9,10},{10,1... | collective-permute-start | bytes 1474568 | tf_op jit(solution)/shard_map/ppermute | solution.py:298
  125.7 10.2 %collective-permute-start.11 = (bf16[4,240,256]{2,1,0:T(8,128)(2,1)S(1)}, bf16[4,240,256]{2,1,0:T(8,128)(2,1)S(1)}, u32[]{:S(2)}, u32[]{:S(2)}) collective-permute-start(bf16[4,240,256]{2,1,0:T(8,128)(2,1)S(1)} %bitcast.22), channel_id=1, source_target_pairs={{0,15},{1,0},{2,1},{3,2},{4,3},{5,4},{6,5},{7,6},{8,7},{9,8},{10,9... | collective-permute-start | bytes 1474568 | tf_op jit(solution)/shard_map/ppermute | solution.py:298
  136.0 5.2 %copy-start.8 = (bf16[224]{0:T(256)(128)(2,1)S(1)}, bf16[224]{0:T(256)(128)(2,1)}, u32[]{:S(2)}) copy-start(bf16[224]{0:T(256)(128)(2,1)} %param.11) | copy-start | bytes 1348
  136.0 5.2 %copy-start.9 = (bf16[224]{0:T(256)(128)(2,1)S(1)}, bf16[224]{0:T(256)(128)(2,1)}, u32[]{:S(2)}) copy-start(bf16[224]{0:T(256)(128)(2,1)} %param.12) | copy-start | bytes 1348
  136.0 31.1 %copy-start.5 = (s32[2,256]{1,0:T(2,128)S(1)}, s32[2,256]{1,0:T(2,128)}, u32[]{:S(2)}) copy-start(s32[2,256]{1,0:T(2,128)} %label_ref.1) | copy-start | bytes 6148
  136.0 31.1 %copy-start.6 = (s32[2,256]{1,0:T(2,128)S(1)}, s32[2,256]{1,0:T(2,128)}, u32[]{:S(2)}) copy-start(s32[2,256]{1,0:T(2,128)} %mask_ref.1) | copy-start | bytes 6148
  136.0 31.1 %copy-start.7 = (s32[2,256]{1,0:T(2,128)S(1)}, s32[2,256]{1,0:T(2,128)}, u32[]{:S(2)}) copy-start(s32[2,256]{1,0:T(2,128)} %segment_ref.1) | copy-start | bytes 6148
  137.5 7.2 %collective-permute-start.12 = (f32[232,256]{1,0:T(8,128)S(1)}, f32[232,256]{1,0:T(8,128)S(1)}, u32[]{:S(2)}, u32[]{:S(2)}) collective-permute-start(f32[232,256]{1,0:T(8,128)S(1)} %get-tuple-element.36), channel_id=1, source_target_pairs={{0,16},{16,0},{1,17},{17,1},{2,18},{18,2},{3,19},{19,3},{4,20},{20... | collective-permute-start | bytes 712712 | tf_op jit(solution)/shard_map/ppermute | solution.py:294
  145.5 21.5 %all-to-all-start = ((f32[32,2,256]{2,1,0:T(2,128)}), f32[32,2,256]{2,1,0:T(2,128)S(1)}, u32[]{:S(2)}, u32[]{:S(2)}) async-start(f32[32,2,256]{2,1,0:T(2,128)} %get-tuple-element.39), calls=%async_computation | async-start | bytes 131072 | tf_op jit(solution)/shard_map/all_to_all | solution.py:332
  153.8 30.3 %collective-permute-start.13 = (bf16[224,256]{1,0:T(8,128)(2,1)S(1)}, bf16[224,256]{1,0:T(8,128)(2,1)S(1)}, u32[]{:S(2)}, u32[]{:S(2)}) collective-permute-start(bf16[224,256]{1,0:T(8,128)(2,1)S(1)} %get-tuple-element.37), channel_id=1, source_target_pairs={{0,256},{256,0},{1,257},{257,1},{2,258},{258,2},{3,259},{259,3},{4... | collective-permute-start | bytes 344072 | tf_op jit(solution)/shard_map/ppermute | solution.py:294
  167.8 23.6 %all-to-all-start.1 = ((f32[16,2,128]{2,1,0:T(2,128)}), f32[16,2,128]{2,1,0:T(2,128)S(1)}, u32[]{:S(2)}, u32[]{:S(2)}) async-start(f32[16,2,128]{2,1,0:T(2,128)} %loss_parts.1), calls=%async_computation.1 | async-start | bytes 32768 | tf_op jit(solution)/shard_map/all_to_all | solution.py:334

commit v4 on v3

v4 whole, which is shorter than its diff:
```python
import jax
import jax.numpy as jnp
from jax import lax
from jax.experimental import pallas as pl
from jax.experimental.pallas import tpu as pltpu
from jax.sharding import Mesh
from jax.sharding import PartitionSpec as P

D = 7168
SEGS = 16
EPS = 1e-05
F = 224
T = 256
KH = D // 2
HALF = F // 2
R = 240
F32 = jnp.float32
BF16 = jnp.bfloat16
SCALE = 32.0
SMALL = pltpu.CompilerParams(vmem_limit_bytes=4 * 1024 * 1024)
MEDIUM = pltpu.CompilerParams(vmem_limit_bytes=8 * 1024 * 1024)
LARGE = pltpu.CompilerParams(vmem_limit_bytes=12 * 1024 * 1024)


def vmem():
    return pl.BlockSpec(memory_space=pltpu.VMEM)


def anywhere():
    return pl.BlockSpec(memory_space=pl.ANY)


def column(row):
    down = lax.broadcasted_iota(jnp.int32, (F, F), 0)
    along = lax.broadcasted_iota(jnp.int32, (F, F), 1)
    wide = jnp.where(down == along, jnp.broadcast_to(row.astype(F32), (F, F)), 0.0)
    return jnp.sum(wide, axis=1, keepdims=True)


def picked(here_ref, away_ref, local):
    return column(jnp.where(local, here_ref[...].astype(F32), away_ref[...].astype(F32)))


def pack_block(rows, gain, block_ref):
    block_ref[0:F, :] = ((rows * gain).astype(BF16).astype(F32) * SCALE).astype(BF16)
    block_ref[F:R, :] = three_terms(jnp.sqrt(jnp.sum(rows * rows, axis=0, keepdims=True)))


def call(kernel, outs, ins, out_specs, params, name, scratch=()):
    return pl.pallas_call(
        kernel,
        out_shape=outs,
        in_specs=ins,
        out_specs=out_specs,
        scratch_shapes=scratch,
        compiler_params=params,
        name=name,
    )


def shape(dims, dtype):
    return jax.ShapeDtypeStruct(dims, dtype)


def pack_kernel(tokens_ref, here_ref, away_ref, block_ref):
    section = lax.axis_index("s")
    gain = picked(here_ref, away_ref, section == 0)
    pack_block(tokens_ref[section].astype(F32), gain, block_ref)


def pack(tokens, here, away):
    return call(
        pack_kernel, shape((R, T), BF16), [vmem()] * 3, vmem(), SMALL, "pack"
    )(tokens, here, away)


def split_kernel(weight_ref, out_ref, sems):
    rows = pl.ds(pl.multiple_of(lax.axis_index("c") * HALF, 16), HALF)
    copies = []
    for i in range(4):
        columns = pl.ds(i % 2 * KH, KH)
        copies.append(
            pltpu.make_async_copy(weight_ref.at[rows, columns], out_ref.at[i], sems.at[i])
        )
    for copy in copies:
        copy.start()
    for copy in copies:
        copy.wait()


def split(weight):
    return call(
        split_kernel, shape((4, HALF, KH), BF16), [anywhere()], vmem(), MEDIUM, "split",
        [pltpu.SemaphoreType.DMA((4,))],
    )(weight)


def three_terms(row):
    first = row.astype(BF16)
    rest = row - first.astype(F32)
    second = rest.astype(BF16)
    third = (rest - second.astype(F32)).astype(BF16)
    at = lax.broadcasted_iota(jnp.int32, (R - F, T), 0)
    tail = jnp.where(at == 0, first.astype(F32), 0.0)
    tail = jnp.where(at == 1, second.astype(F32), tail)
    tail = jnp.where(at == 2, third.astype(F32), tail)
    return tail.astype(BF16)


def product_kernel(
    same_ref, half_ref, half2_ref, own_ref, send_ref, held, values, sems
):
    core = lax.axis_index("c")
    x = lax.axis_index("x")
    copies = []
    for i in range(4):
        ref, half = (half_ref, core) if i % 2 == 0 else (half2_ref, 1 - core)
        index, start = (x, 0) if i < 2 else (1 - x, F)
        rows = pl.ds(pl.multiple_of(start + half * HALF, 16), HALF)
        copies.append(pltpu.make_async_copy(ref.at[index], held.at[rows, :], sems.at[i]))
    for copy in copies:
        copy.start()

    squares = jnp.zeros((1, T), F32)
    for i in range(16):
        got = same_ref[i]
        values[i * F:(i + 1) * F, :] = got[0:F]
        root = jnp.sum(got[F:R].astype(F32), axis=0, keepdims=True)
        squares += root * root

    for copy in copies:
        copy.wait()

    product = jnp.dot(held[...], values[...], preferred_element_type=F32)
    own_ref[0:F, :] = product[0:F]
    own_ref[F:F + 8, :] = jnp.broadcast_to(squares, (8, T))
    send_ref[0:F, :] = product[F:2 * F].astype(BF16)
    send_ref[F:R, :] = three_terms(squares)


def product(same, halves):
    return call(
        product_kernel,
        (shape((F + 8, T), F32), shape((R, T), BF16)),
        [vmem(), anywhere(), anywhere()],
        (vmem(), vmem()),
        LARGE,
        "product",
        [
            pltpu.VMEM((2 * F, KH), BF16),
            pltpu.VMEM((KH, T), BF16),
            pltpu.SemaphoreType.DMA((4,)),
        ],
    )(same, *halves)


def block_rows(own_ref, other_ref, rows):
    other = jnp.sum(other_ref[F:R, :].astype(F32), axis=0, keepdims=True)
    inv_root = lax.rsqrt((own_ref[F:F + 1, :] + other) / D + EPS) / SCALE
    mixed = (own_ref[0:F, :] + other_ref[0:F, :].astype(F32)) * inv_root
    gated = mixed / (1.0 + jnp.exp(-mixed))
    return (rows.astype(F32) + gated).astype(BF16)


def middle_kernel(own_ref, other_ref, tokens_ref, here_ref, away_ref, out_ref, block_ref):
    section = lax.axis_index("s")
    out = block_rows(own_ref, other_ref, tokens_ref[section])
    out_ref[...] = out
    gain = picked(here_ref, away_ref, section == 1)
    pack_block(out.astype(F32), gain, block_ref)


def middle(own, other, tokens, here, away):
    return call(
        middle_kernel,
        (shape((F, T), BF16), shape((R, T), BF16)),
        [vmem()] * 5,
        (vmem(), vmem()),
        SMALL,
        "middle",
    )(own, other, tokens, here, away)


def last_kernel(
    own_ref, other_ref, rows_ref, gain_ref, score_ref, out_ref, swap_ref, stats_ref
):
    out = block_rows(own_ref, other_ref, rows_ref[...])
    out_ref[...] = out
    section = lax.axis_index("s")

    @pl.when(section == 0)
    def _():
        swap_ref[...] = out

    @pl.when(section != 0)
    def _():
        swap_ref[...] = rows_ref[...]

    as_float = out.astype(F32)
    head = column(gain_ref[...].astype(F32) * score_ref[...].astype(F32))
    squares = jnp.sum(as_float * as_float, axis=0, keepdims=True)
    scores = jnp.sum(as_float * head, axis=0, keepdims=True)
    stats = jnp.concatenate([squares, scores], axis=0)
    for i in range(32):
        stats_ref[i] = stats


def last(own, other, rows, gain, score):
    out = shape((F, T), BF16)
    return call(
        last_kernel,
        (out, out, shape((32, 2, T), F32)),
        [vmem()] * 5,
        (vmem(), vmem(), vmem()),
        SMALL,
        "last",
    )(own, other, rows, gain, score)


def loss_kernel(stats_ref, label_ref, mask_ref, segment_ref, sums_ref):
    first = lax.axis_index("s") == 0

    def pick(ref):
        return jnp.where(first, ref[0:1, :], ref[1:2, :])

    total = jnp.sum(stats_ref[...], axis=0)
    inv_root = lax.rsqrt(total[0:1] / D + EPS)
    score = total[1:2] * inv_root
    target = pick(label_ref).astype(F32) - 1.0
    mask = pick(mask_ref).astype(F32)
    err = score - target
    squared = mask * err * err
    member = pick(segment_ref) == lax.broadcasted_iota(jnp.int32, (SEGS, T), 0)
    sums = jnp.sum(jnp.where(member, squared, 0.0), axis=1, keepdims=True)
    counts = jnp.sum(jnp.where(member, mask, 0.0), axis=1, keepdims=True)
    lane = lax.broadcasted_iota(jnp.int32, (SEGS, 128), 1)
    diagonal = lane == lax.broadcasted_iota(jnp.int32, (SEGS, 128), 0)
    sums = jnp.sum(jnp.where(diagonal, sums, 0.0), axis=0, keepdims=True)
    counts = jnp.sum(jnp.where(diagonal, counts, 0.0), axis=0, keepdims=True)
    both = jnp.concatenate([sums, counts], axis=0)
    for i in range(16):
        sums_ref[i] = both


def loss_parts(stats, label, mask, segment):
    return call(
        loss_kernel, shape((16, 2, 128), F32), [vmem()] * 4, vmem(), SMALL, "loss_parts"
    )(stats, label, mask, segment)


def swapped(value, *axes):
    count = 2 ** len(axes)
    name = axes if len(axes) > 1 else axes[0]
    return lax.ppermute(value, name, [(i, i ^ (count - 1)) for i in range(count)])


def gathered(block):
    return lax.all_gather(block.astype(jnp.float16), "z", axis=0, tiled=False).astype(BF16)


def body(
    tokens_in, section_proj, section_gain, final_gain, score_weight, labels, loss_mask, segment_ids
):
    section = lax.axis_index("s")
    gain_away = swapped(section_gain, "s")

    pieces, gain_away = lax.optimization_barrier((split(section_proj[0]), gain_away))
    half = lax.all_to_all(pieces, ("s", "x"), 0, 0, tiled=True)

    same = gathered(pack(tokens_in, section_gain, gain_away))
    same, half = lax.optimization_barrier((same, half))
    near = half[0:2]
    own, send = product(same, (near, swapped(near, "c")))
    send, half = lax.optimization_barrier((send, half))
    away = half[2:4]
    away2 = swapped(away, "c")
    first, block = middle(own, swapped(send, "x"), tokens_in, section_gain, gain_away)

    own, send = product(gathered(block), (away, away2))
    second, handed, stats = last(
        own, swapped(send, "x"), first, final_gain[None], score_weight[None]
    )
    handed = swapped(handed, "s")

    stats = lax.all_to_all(stats, ("x", "z"), 0, 0, tiled=True)
    parts = loss_parts(stats, labels, loss_mask, segment_ids)
    parts = lax.all_to_all(parts, ("s", "y", "c"), 0, 0, tiled=True)
    parts = jnp.sum(parts.reshape(2, 8, 2, 128), axis=1)[:, :, :SEGS]
    segment_loss = parts[:, 0] / jnp.maximum(parts[:, 1], 1.0)

    section_out = jnp.where(section == 0, jnp.stack([first, handed]), jnp.stack([handed, second]))
    return section_out[None], segment_loss


def solution(mesh):
    finer = Mesh(mesh.devices.reshape(2, 4, 2, 2, 16), ("s", "y", "c", "x", "z"))
    tensor = ("x", "z")
    dp = ("y", "c")
    in_specs = (
        P(None, tensor, dp),
        P("s", tensor, None),
        P("s", tensor),
        P(tensor),
        P(tensor),
        P(None, dp),
        P(None, dp),
        P(None, dp),
    )
    out_specs = (P("s", None, tensor, dp), P())
    return jax.shard_map(body, mesh=finer, in_specs=in_specs, out_specs=out_specs, check_vma=False)
```

time: 193 us -> 175 us (0.907)
  starting transfers between devices: 78.9 us -> 59.2 us
  waiting for transfers between devices: 40.3 us -> 24.3 us
  blocking collectives: 62.4 us -> 75.8 us
  local copies, waits for them, and re-layouts: 3.01 us -> 5 us
    ppermute x4 -> x0, waiting for transfers between devices: 16.9 us -> none  [shifted(): return lax.ppermute(value, Z, [(i, (i + by) % 16) for i in range(16)])]
    ppermute x4 -> x0, starting transfers between devices: 15.3 us -> none  [shifted(): return lax.ppermute(value, Z, [(i, (i + by) % 16) for i in range(16)])]
    all_gather x2, blocking collectives: 62.4 us -> 75.8 us  [gathered(): lax.all_gather(block.astype(jnp.float16), 'z', axis=0, tiled=False)]
    ppermute x10 -> x6, starting transfers between devices: 39.1 us -> 27.4 us  [swapped(): return lax.ppermute(value, name, [(i, i ^ count - 1) for i in range(count)])]
    all_to_all x1 -> x2, starting transfers between devices: 8.28 us -> 12.5 us  [the longest x1 7.65 us: body(): stats = lax.all_to_all(stats, ('x', 'z'), 0, 0, tiled=True)]
    all_to_all x1, starting transfers between devices: 16.3 us -> 19.4 us  [body(): parts = lax.all_to_all(parts, ('s', 'y', 'c'), 0, 0, tiled=True)]
    slice x2, local copies, waits for them, and re-layouts: 0.13 us -> 3.05 us  [the longest x1 1.52 us: body(): away = half[2:4]]
    ppermute x10 -> x6, waiting for transfers between devices: 8.53 us -> 10 us  [swapped(): return lax.ppermute(value, name, [(i, i ^ count - 1) for i in range(count)])]
  transfers between devices with their start and end apart: 16 -> 9, of which waited for: 8 -> 5; matrix products, arithmetic and copies ran while one was open for 0% -> 1% of each run, Pallas kernels for 1% -> 2%
where the time goes in v4:
time: 175 us; the launch traced here: 174 us
  blocking collectives  75.8 us (43%)
  starting transfers between devices  59.2 us (34%)
  waiting for transfers between devices  24.3 us (14%)
  Pallas kernels  6.97 us (4%)
  local copies, waits for them, and re-layouts  5 us (3%)
  other arithmetic  2.29 us (1%)
    all_gather x2, blocking collectives, gathered(): lax.all_gather(block.astype(jnp.float16), 'z', axis=0, tiled=False)  75.8 us
    ppermute x6, starting transfers between devices, swapped(): return lax.ppermute(value, name, [(i, i ^ count - 1) for i in range(count)])  27.4 us
    all_to_all x1, starting transfers between devices, body(): parts = lax.all_to_all(parts, ('s', 'y', 'c'), 0, 0, tiled=True)  19.4 us
    ppermute x6, waiting for transfers between devices, swapped(): return lax.ppermute(value, name, [(i, i ^ count - 1) for i in range(count)])  10 us
    all_to_all x1, waiting for transfers between devices, body(): stats = lax.all_to_all(stats, ('x', 'z'), 0, 0, tiled=True)  7.75 us
    all_to_all x1, starting transfers between devices, body(): stats = lax.all_to_all(stats, ('x', 'z'), 0, 0, tiled=True)  7.65 us
    all_to_all x1, waiting for transfers between devices, body(): parts = lax.all_to_all(parts, ('s', 'y', 'c'), 0, 0, tiled=True)  6.56 us
    all_to_all x1, starting transfers between devices, body(): half = lax.all_to_all(pieces, ('s', 'x'), 0, 0, tiled=True)  4.81 us
  transfers between devices with their start and end apart: 9, of which 5 were waited for; matrix products, arithmetic and copies ran while one was open for 1% of the time, Pallas kernels for 2%

profile of v4, /device:TPU:1, one launch (start us, length us, event | category | flops | bytes accessed | tf_op | source)
XLA Modules:
  0.0 174.5 jit_solution(18421461321132142816)
XLA Ops:
  0.6 5.5 %collective-permute-start = (bf16[1,224]{1,0:T(2,128)(2,1)}, bf16[1,224]{1,0:T(2,128)(2,1)S(1)}, u32[]{:S(2)}, u32[]{:S(2)}) collective-permute-start(bf16[1,224]{1,0:T(2,128)(2,1)} %here_ref.3), channel_id=1, source_target_pairs={{0,256},{256,0},{1,257},{257,1},{2,258},{258,2},{3,259},{259,3},{4... | collective-permute-start | bytes 1352 | tf_op jit(solution)/shard_map/ppermute | solution.py:254
  6.1 1.9 %copy-done = bf16[1,224,7168]{2,1,0:T(8,128)(2,1)S(1)} copy-done((bf16[1,224,7168]{2,1,0:T(8,128)(2,1)S(1)}, bf16[1,224,7168]{2,1,0:T(8,128)(2,1)}, u32[]{:S(2)}) %copy-start) | copy-done | bytes 3211288
  8.0 2.0 %split.1 = bf16[4,112,3584]{2,1,0:T(8,128)(2,1)} custom-call(bf16[224,7168]{1,0:T(8,128)(2,1)S(1)} %bitcast.11), custom_call_target="tpu_custom_call" | custom-call | tf_op jit(solution)/shard_map/split/pallas_call | solution.py:92
  10.1 0.0 copy-start.1
  10.1 0.0 copy-start.2
  10.1 4.8 %all-to-all-start = ((bf16[4,112,3584]{2,1,0:T(8,128)(2,1)}), bf16[4,112,3584]{2,1,0:T(8,128)(2,1)}, u32[]{:S(2)}, u32[]{:S(2)}) async-start(bf16[4,112,3584]{2,1,0:T(8,128)(2,1)} %split.1), calls=%async_computation | async-start | bytes 6422528 | tf_op jit(solution)/shard_map/all_to_all | solution.py:268
  15.0 0.1 pack.1
  15.1 43.2 %all-gather.4 = f16[3840,256]{1,0:T(8,128)(2,1)S(1)} all-gather(f16[240,256]{1,0:T(8,128)(2,1)S(1)} %convert_element_type.12), channel_id=2, replica_groups=mesh['s'=2,'y'=4,'c'=2,'x'=2,'z'=16] {'z'}, dimensions={0}, use_global_device_ids=true | all-gather | bytes 2088960 | tf_op jit(solution)/shard_map/all_gather | solution.py:258
  58.3 0.5 convert_element_type.16
  58.8 1.5 slice.15.half_ref
  60.3 8.8 %collective-permute-start.1 = (bf16[2,112,3584]{2,1,0:T(8,128)(2,1)S(1)}, bf16[2,112,3584]{2,1,0:T(8,128)(2,1)S(1)}, u32[]{:S(2)}, u32[]{:S(2)}) collective-permute-start(bf16[2,112,3584]{2,1,0:T(8,128)(2,1)S(1)} %slice.15.half_ref), channel_id=1, source_target_pairs={{0,32},{32,0},{1,33},{33,1},{2,34},{34,2},{3,35},{35,3},{4,36},{36... | collective-permute-start | bytes 4816904 | tf_op jit(solution)/shard_map/ppermute | solution.py:254
  69.1 3.1 %collective-permute-done.1.half2_ref = bf16[2,112,3584]{2,1,0:T(8,128)(2,1)S(1)} collective-permute-done((bf16[2,112,3584]{2,1,0:T(8,128)(2,1)S(1)}, bf16[2,112,3584]{2,1,0:T(8,128)(2,1)S(1)}, u32[]{:S(2)}, u32[]{:S(2)}) %collective-permute-start.1) | collective-permute-done | bytes 1605664 | tf_op jit(solution)/shard_map/ppermute | solution.py:254
  72.2 1.5 product.2
  73.7 1.5 slice.16.half_ref
  75.2 2.3 %collective-permute-start.3 = (bf16[2,112,3584]{2,1,0:T(8,128)(2,1)S(1)}, bf16[2,112,3584]{2,1,0:T(8,128)(2,1)S(1)}, u32[]{:S(2)}, u32[]{:S(2)}) collective-permute-start(bf16[2,112,3584]{2,1,0:T(8,128)(2,1)S(1)} %slice.16.half_ref), channel_id=1, source_target_pairs={{0,32},{32,0},{1,33},{33,1},{2,34},{34,2},{3,35},{35,3},{4,36},{36... | collective-permute-start | bytes 4816904 | tf_op jit(solution)/shard_map/ppermute | solution.py:254
  77.5 2.4 %collective-permute-start.2 = (bf16[240,256]{1,0:T(8,128)(2,1)S(1)}, bf16[240,256]{1,0:T(8,128)(2,1)S(1)}, u32[]{:S(2)}, u32[]{:S(2)}) collective-permute-start(bf16[240,256]{1,0:T(8,128)(2,1)S(1)} %get-tuple-element.23), channel_id=1, source_target_pairs={{0,16},{16,0},{1,17},{17,1},{2,18},{18,2},{3,19},{19,3},{4,20},{20... | collective-permute-start | bytes 368648 | tf_op jit(solution)/shard_map/ppermute | solution.py:254
  79.9 4.2 %collective-permute-done.2.other_ref = bf16[240,256]{1,0:T(8,128)(2,1)S(1)} collective-permute-done((bf16[240,256]{1,0:T(8,128)(2,1)S(1)}, bf16[240,256]{1,0:T(8,128)(2,1)S(1)}, u32[]{:S(2)}, u32[]{:S(2)}) %collective-permute-start.2) | collective-permute-done | bytes 122912 | tf_op jit(solution)/shard_map/ppermute | solution.py:254
  84.2 0.2 middle.1
  84.4 32.6 %all-gather.5 = f16[3840,256]{1,0:T(8,128)(2,1)S(1)} all-gather(f16[240,256]{1,0:T(8,128)(2,1)S(1)} %convert_element_type.14), channel_id=3, replica_groups=mesh['s'=2,'y'=4,'c'=2,'x'=2,'z'=16] {'z'}, dimensions={0}, use_global_device_ids=true | all-gather | bytes 2088960 | tf_op jit(solution)/shard_map/all_gather | solution.py:258
  117.0 0.5 convert_element_type.17
  117.6 1.5 product.3
  119.1 2.9 %collective-permute-start.4 = (bf16[240,256]{1,0:T(8,128)(2,1)S(1)}, bf16[240,256]{1,0:T(8,128)(2,1)S(1)}, u32[]{:S(2)}, u32[]{:S(2)}) collective-permute-start(bf16[240,256]{1,0:T(8,128)(2,1)S(1)} %get-tuple-element.28), channel_id=1, source_target_pairs={{0,16},{16,0},{1,17},{17,1},{2,18},{18,2},{3,19},{19,3},{4,20},{20... | collective-permute-start | bytes 368648 | tf_op jit(solution)/shard_map/ppermute | solution.py:254
  122.0 2.7 %collective-permute-done.4.other_ref = bf16[240,256]{1,0:T(8,128)(2,1)S(1)} collective-permute-done((bf16[240,256]{1,0:T(8,128)(2,1)S(1)}, bf16[240,256]{1,0:T(8,128)(2,1)S(1)}, u32[]{:S(2)}, u32[]{:S(2)}) %collective-permute-start.4) | collective-permute-done | bytes 122912 | tf_op jit(solution)/shard_map/ppermute | solution.py:254
  124.7 0.9 last.1
  125.6 7.7 %all-to-all-start.1 = ((f32[32,2,256]{2,1,0:T(2,128)}), f32[32,2,256]{2,1,0:T(2,128)S(1)}, u32[]{:S(2)}, u32[]{:S(2)}) async-start(f32[32,2,256]{2,1,0:T(2,128)} %get-tuple-element.31), calls=%async_computation.1 | async-start | bytes 131072 | tf_op jit(solution)/shard_map/all_to_all | solution.py:285
  133.2 5.5 %collective-permute-start.5 = (bf16[224,256]{1,0:T(8,128)(2,1)S(1)}, bf16[224,256]{1,0:T(8,128)(2,1)S(1)}, u32[]{:S(2)}, u32[]{:S(2)}) collective-permute-start(bf16[224,256]{1,0:T(8,128)(2,1)S(1)} %get-tuple-element.29), channel_id=1, source_target_pairs={{0,256},{256,0},{1,257},{257,1},{2,258},{258,2},{3,259},{259,3},{4... | collective-permute-start | bytes 344072 | tf_op jit(solution)/shard_map/ppermute | solution.py:254
  138.7 7.7 %all-to-all-done.1.stats_ref = f32[32,2,256]{2,1,0:T(2,128)S(1)} async-done(((f32[32,2,256]{2,1,0:T(2,128)}), f32[32,2,256]{2,1,0:T(2,128)S(1)}, u32[]{:S(2)}, u32[]{:S(2)}) %all-to-all-start.1) | async-done | bytes 65568 | tf_op jit(solution)/shard_map/all_to_all | solution.py:285
  146.5 0.8 loss_parts.1
  147.2 19.4 %all-to-all-start.2 = ((f32[16,2,128]{2,1,0:T(2,128)}), f32[16,2,128]{2,1,0:T(2,128)S(1)}, u32[]{:S(2)}, u32[]{:S(2)}) async-start(f32[16,2,128]{2,1,0:T(2,128)} %loss_parts.1), calls=%async_computation.2 | async-start | bytes 32768 | tf_op jit(solution)/shard_map/all_to_all | solution.py:287
  166.6 0.7 maximum_select_fusion
  167.3 6.6 %all-to-all-done.2 = f32[16,2,128]{2,1,0:T(2,128)S(1)} async-done(((f32[16,2,128]{2,1,0:T(2,128)}), f32[16,2,128]{2,1,0:T(2,128)S(1)}, u32[]{:S(2)}, u32[]{:S(2)}) %all-to-all-start.2) | async-done | bytes 16416 | tf_op jit(solution)/shard_map/all_to_all | solution.py:287
  173.9 0.6 fusion
  (22 shorter events, 0.1 us)
Async XLA Ops:
  0.6 9.5 %collective-permute-start = (bf16[1,224]{1,0:T(2,128)(2,1)}, bf16[1,224]{1,0:T(2,128)(2,1)S(1)}, u32[]{:S(2)}, u32[]{:S(2)}) collective-permute-start(bf16[1,224]{1,0:T(2,128)(2,1)} %here_ref.3), channel_id=1, source_target_pairs={{0,256},{256,0},{1,257},{257,1},{2,258},{258,2},{3,259},{259,3},{4... | collective-permute-start | bytes 1352 | tf_op jit(solution)/shard_map/ppermute | solution.py:254
  6.1 1.9 %copy-start = (bf16[1,224,7168]{2,1,0:T(8,128)(2,1)S(1)}, bf16[1,224,7168]{2,1,0:T(8,128)(2,1)}, u32[]{:S(2)}) copy-start(bf16[1,224,7168]{2,1,0:T(8,128)(2,1)} %param.9) | copy-start | bytes 9633796
  10.1 4.8 %copy-start.1 = (bf16[2,224,256]{2,1,0:T(8,128)(2,1)S(1)}, bf16[2,224,256]{2,1,0:T(8,128)(2,1)}, u32[]{:S(2)}) copy-start(bf16[2,224,256]{2,1,0:T(8,128)(2,1)} %tokens_ref.3) | copy-start | bytes 688132
  10.1 4.8 %copy-start.2 = (bf16[1,224]{1,0:T(2,128)(2,1)S(1)}, bf16[1,224]{1,0:T(2,128)(2,1)}, u32[]{:S(2)}) copy-start(bf16[1,224]{1,0:T(2,128)(2,1)} %here_ref.3) | copy-start | bytes 1348
  10.1 48.6 %all-to-all-start = ((bf16[4,112,3584]{2,1,0:T(8,128)(2,1)}), bf16[4,112,3584]{2,1,0:T(8,128)(2,1)}, u32[]{:S(2)}, u32[]{:S(2)}) async-start(bf16[4,112,3584]{2,1,0:T(8,128)(2,1)} %split.1), calls=%async_computation | async-start | bytes 6422528 | tf_op jit(solution)/shard_map/all_to_all | solution.py:268
  60.3 11.9 %collective-permute-start.1 = (bf16[2,112,3584]{2,1,0:T(8,128)(2,1)S(1)}, bf16[2,112,3584]{2,1,0:T(8,128)(2,1)S(1)}, u32[]{:S(2)}, u32[]{:S(2)}) collective-permute-start(bf16[2,112,3584]{2,1,0:T(8,128)(2,1)S(1)} %slice.15.half_ref), channel_id=1, source_target_pairs={{0,32},{32,0},{1,33},{33,1},{2,34},{34,2},{3,35},{35,3},{4,36},{36... | collective-permute-start | bytes 4816904 | tf_op jit(solution)/shard_map/ppermute | solution.py:254
  75.2 42.3 %collective-permute-start.3 = (bf16[2,112,3584]{2,1,0:T(8,128)(2,1)S(1)}, bf16[2,112,3584]{2,1,0:T(8,128)(2,1)S(1)}, u32[]{:S(2)}, u32[]{:S(2)}) collective-permute-start(bf16[2,112,3584]{2,1,0:T(8,128)(2,1)S(1)} %slice.16.half_ref), channel_id=1, source_target_pairs={{0,32},{32,0},{1,33},{33,1},{2,34},{34,2},{3,35},{35,3},{4,36},{36... | collective-permute-start | bytes 4816904 | tf_op jit(solution)/shard_map/ppermute | solution.py:254
  77.5 6.7 %collective-permute-start.2 = (bf16[240,256]{1,0:T(8,128)(2,1)S(1)}, bf16[240,256]{1,0:T(8,128)(2,1)S(1)}, u32[]{:S(2)}, u32[]{:S(2)}) collective-permute-start(bf16[240,256]{1,0:T(8,128)(2,1)S(1)} %get-tuple-element.23), channel_id=1, source_target_pairs={{0,16},{16,0},{1,17},{17,1},{2,18},{18,2},{3,19},{19,3},{4,20},{20... | collective-permute-start | bytes 368648 | tf_op jit(solution)/shard_map/ppermute | solution.py:254
  117.5 4.4 %copy-start.6 = (bf16[224]{0:T(256)(128)(2,1)S(1)}, bf16[224]{0:T(256)(128)(2,1)}, u32[]{:S(2)}) copy-start(bf16[224]{0:T(256)(128)(2,1)} %param.11) | copy-start | bytes 1348
  117.5 4.5 %copy-start.7 = (bf16[224]{0:T(256)(128)(2,1)S(1)}, bf16[224]{0:T(256)(128)(2,1)}, u32[]{:S(2)}) copy-start(bf16[224]{0:T(256)(128)(2,1)} %param.12) | copy-start | bytes 1348
  117.6 28.9 %copy-start.3 = (s32[2,256]{1,0:T(2,128)S(1)}, s32[2,256]{1,0:T(2,128)}, u32[]{:S(2)}) copy-start(s32[2,256]{1,0:T(2,128)} %label_ref.1) | copy-start | bytes 6148
  117.6 28.9 %copy-start.4 = (s32[2,256]{1,0:T(2,128)S(1)}, s32[2,256]{1,0:T(2,128)}, u32[]{:S(2)}) copy-start(s32[2,256]{1,0:T(2,128)} %mask_ref.1) | copy-start | bytes 6148
  117.6 28.9 %copy-start.5 = (s32[2,256]{1,0:T(2,128)S(1)}, s32[2,256]{1,0:T(2,128)}, u32[]{:S(2)}) copy-start(s32[2,256]{1,0:T(2,128)} %segment_ref.1) | copy-start | bytes 6148
  119.1 5.6 %collective-permute-start.4 = (bf16[240,256]{1,0:T(8,128)(2,1)S(1)}, bf16[240,256]{1,0:T(8,128)(2,1)S(1)}, u32[]{:S(2)}, u32[]{:S(2)}) collective-permute-start(bf16[240,256]{1,0:T(8,128)(2,1)S(1)} %get-tuple-element.28), channel_id=1, source_target_pairs={{0,16},{16,0},{1,17},{17,1},{2,18},{18,2},{3,19},{19,3},{4,20},{20... | collective-permute-start | bytes 368648 | tf_op jit(solution)/shard_map/ppermute | solution.py:254
  125.6 20.9 %all-to-all-start.1 = ((f32[32,2,256]{2,1,0:T(2,128)}), f32[32,2,256]{2,1,0:T(2,128)S(1)}, u32[]{:S(2)}, u32[]{:S(2)}) async-start(f32[32,2,256]{2,1,0:T(2,128)} %get-tuple-element.31), calls=%async_computation.1 | async-start | bytes 131072 | tf_op jit(solution)/shard_map/all_to_all | solution.py:285
  133.2 33.4 %collective-permute-start.5 = (bf16[224,256]{1,0:T(8,128)(2,1)S(1)}, bf16[224,256]{1,0:T(8,128)(2,1)S(1)}, u32[]{:S(2)}, u32[]{:S(2)}) collective-permute-start(bf16[224,256]{1,0:T(8,128)(2,1)S(1)} %get-tuple-element.29), channel_id=1, source_target_pairs={{0,256},{256,0},{1,257},{257,1},{2,258},{258,2},{3,259},{259,3},{4... | collective-permute-start | bytes 344072 | tf_op jit(solution)/shard_map/ppermute | solution.py:254
  147.2 26.7 %all-to-all-start.2 = ((f32[16,2,128]{2,1,0:T(2,128)}), f32[16,2,128]{2,1,0:T(2,128)S(1)}, u32[]{:S(2)}, u32[]{:S(2)}) async-start(f32[16,2,128]{2,1,0:T(2,128)} %loss_parts.1), calls=%async_computation.2 | async-start | bytes 32768 | tf_op jit(solution)/shard_map/all_to_all | solution.py:287

commit v5 on v4

--- a/solution.py
+++ b/solution.py
@@ -1,3 +1,5 @@
+import functools
+
 import jax
 import jax.numpy as jnp
 from jax import lax
@@ -13,12 +15,12 @@
 T = 256
 KH = D // 2
 HALF = F // 2
-R = 240
+R = 232
 F32 = jnp.float32
 BF16 = jnp.bfloat16
 SCALE = 32.0
 SMALL = pltpu.CompilerParams(vmem_limit_bytes=4 * 1024 * 1024)
-MEDIUM = pltpu.CompilerParams(vmem_limit_bytes=8 * 1024 * 1024)
+WHOLE = pltpu.CompilerParams(vmem_limit_bytes=60 * 1024 * 1024)
 LARGE = pltpu.CompilerParams(vmem_limit_bytes=12 * 1024 * 1024)
 
 
@@ -74,24 +76,29 @@
     )(tokens, here, away)
 
 
-def split_kernel(weight_ref, out_ref, sems):
+def split_kernel(weight_ref, out_ref, held, sems):
     rows = pl.ds(pl.multiple_of(lax.axis_index("c") * HALF, 16), HALF)
-    copies = []
-    for i in range(4):
-        columns = pl.ds(i % 2 * KH, KH)
-        copies.append(
-            pltpu.make_async_copy(weight_ref.at[rows, columns], out_ref.at[i], sems.at[i])
+    loads = []
+    for i in range(2):
+        columns = pl.ds(i * KH, KH)
+        loads.append(
+            pltpu.make_async_copy(weight_ref.at[rows, columns], held.at[i], sems.at[4 + i])
         )
-    for copy in copies:
-        copy.start()
-    for copy in copies:
-        copy.wait()
+    stores = [pltpu.make_async_copy(held.at[i % 2], out_ref.at[i], sems.at[i]) for i in range(4)]
+    for load in loads:
+        load.start()
+    for i in range(2):
+        loads[i].wait()
+        stores[i].start()
+        stores[i + 2].start()
+    for store in stores:
+        store.wait()
 
 
 def split(weight):
     return call(
-        split_kernel, shape((4, HALF, KH), BF16), [anywhere()], vmem(), MEDIUM, "split",
-        [pltpu.SemaphoreType.DMA((4,))],
+        split_kernel, shape((4, HALF, KH), BF16), [anywhere()], anywhere(), WHOLE, "split",
+        [pltpu.VMEM((2, HALF, KH), BF16), pltpu.SemaphoreType.DMA((6,))],
     )(weight)
 
 
@@ -108,14 +115,14 @@
 
 
 def product_kernel(
-    same_ref, half_ref, half2_ref, own_ref, send_ref, held, values, sems
+    block, same_ref, half_ref, half2_ref, own_ref, send_ref, held, values, sems
 ):
     core = lax.axis_index("c")
     x = lax.axis_index("x")
     copies = []
     for i in range(4):
         ref, half = (half_ref, core) if i % 2 == 0 else (half2_ref, 1 - core)
-        index, start = (x, 0) if i < 2 else (1 - x, F)
+        index, start = (2 * block + x, 0) if i < 2 else (2 * block + 1 - x, F)
         rows = pl.ds(pl.multiple_of(start + half * HALF, 16), HALF)
         copies.append(pltpu.make_async_copy(ref.at[index], held.at[rows, :], sems.at[i]))
     for copy in copies:
@@ -138,9 +145,9 @@
     send_ref[F:R, :] = three_terms(squares)
 
 
-def product(same, halves):
-    return call(
-        product_kernel,
+def product(block, same, halves):
+    return call(
+        functools.partial(product_kernel, block),
         (shape((F + 8, T), F32), shape((R, T), BF16)),
         [vmem(), anywhere(), anywhere()],
         (vmem(), vmem()),
@@ -255,7 +262,7 @@
 
 
 def gathered(block):
-    return lax.all_gather(block.astype(jnp.float16), "z", axis=0, tiled=False).astype(BF16)
+    return lax.all_gather(block.astype(jnp.float16), "z", axis=0, tiled=False)
 
 
 def body(
@@ -269,14 +276,11 @@
 
     same = gathered(pack(tokens_in, section_gain, gain_away))
     same, half = lax.optimization_barrier((same, half))
-    near = half[0:2]
-    own, send = product(same, (near, swapped(near, "c")))
-    send, half = lax.optimization_barrier((send, half))
-    away = half[2:4]
-    away2 = swapped(away, "c")
+    halves = half, swapped(half, "c")
+    own, send = product(0, same.astype(BF16), halves)
     first, block = middle(own, swapped(send, "x"), tokens_in, section_gain, gain_away)
 
-    own, send = product(gathered(block), (away, away2))
+    own, send = product(1, gathered(block).astype(BF16), halves)
     second, handed, stats = last(
         own, swapped(send, "x"), first, final_gain[None], score_weight[None]
     )

time: 175 us -> 168 us (0.960)
  local copies, waits for them, and re-layouts: 5 us -> 0.07 us
  starting transfers between devices: 59.2 us -> 54.3 us
    slice x2 -> x0, local copies, waits for them, and re-layouts: 3.05 us -> none  [the longest x1 1.52 us: body(): away = half[2:4]]
    ppermute x6 -> x5, starting transfers between devices: 27.4 us -> 24.9 us  [swapped(): return lax.ppermute(value, name, [(i, i ^ count - 1) for i in range(count)])]
    all_to_all x1, starting transfers between devices: 19.4 us -> 17.2 us  [body(): parts = lax.all_to_all(parts, ('s', 'y', 'c'), 0, 0, tiled=True)]
    unnamed x16 -> x20, local copies, waits for them, and re-layouts: 1.95 us -> 0.06 us
    ppermute x6 -> x5, waiting for transfers between devices: 10 us -> 9.13 us  [swapped(): return lax.ppermute(value, name, [(i, i ^ count - 1) for i in range(count)])]
  transfers between devices with their start and end apart: 9 -> 8, of which waited for: 5 -> 5; matrix products, arithmetic and copies ran while one was open for 1% -> 2% of each run, Pallas kernels for 2% -> 2%
where the time goes in v5:
time: 168 us
  blocking collectives  76.7 us (46%)
  starting transfers between devices  54.3 us (32%)
  waiting for transfers between devices  24.3 us (14%)
  Pallas kernels  7.74 us (5%)
  other arithmetic  3.63 us (2%)
    all_gather x2, blocking collectives, gathered(): return lax.all_gather(block.astype(jnp.float16), 'z', axis=0, tiled=False)  76.7 us
    ppermute x5, starting transfers between devices, swapped(): return lax.ppermute(value, name, [(i, i ^ count - 1) for i in range(count)])  24.9 us
    all_to_all x1, starting transfers between devices, body(): parts = lax.all_to_all(parts, ('s', 'y', 'c'), 0, 0, tiled=True)  17.2 us
    ppermute x5, waiting for transfers between devices, swapped(): return lax.ppermute(value, name, [(i, i ^ count - 1) for i in range(count)])  9.13 us
    all_to_all x1, waiting for transfers between devices, body(): stats = lax.all_to_all(stats, ('x', 'z'), 0, 0, tiled=True)  8.6 us
    all_to_all x1, starting transfers between devices, body(): stats = lax.all_to_all(stats, ('x', 'z'), 0, 0, tiled=True)  8.31 us
    all_to_all x1, waiting for transfers between devices, body(): parts = lax.all_to_all(parts, ('s', 'y', 'c'), 0, 0, tiled=True)  6.56 us
    all_to_all x1, starting transfers between devices, body(): half = lax.all_to_all(pieces, ('s', 'x'), 0, 0, tiled=True)  3.85 us
  transfers between devices with their start and end apart: 8, of which 5 were waited for; matrix products, arithmetic and copies ran while one was open for 2% of the time, Pallas kernels for 2%

profile of v5, /device:TPU:1, one launch (start us, length us, event | category | flops | bytes accessed | tf_op | source)
XLA Modules:
  0.0 167.6 jit_solution(6103670686305739297)
XLA Ops:
  0.6 5.5 %collective-permute-start = (bf16[1,224]{1,0:T(2,128)(2,1)}, bf16[1,224]{1,0:T(2,128)(2,1)S(1)}, u32[]{:S(2)}, u32[]{:S(2)}) collective-permute-start(bf16[1,224]{1,0:T(2,128)(2,1)} %here_ref.3), channel_id=1, source_target_pairs={{0,256},{256,0},{1,257},{257,1},{2,258},{258,2},{3,259},{259,3},{4... | collective-permute-start | bytes 1352 | tf_op jit(solution)/shard_map/ppermute | solution.py:261
  6.1 2.8 %split.1 = bf16[4,112,3584]{2,1,0:T(8,128)(2,1)} custom-call(bf16[224,7168]{1,0:T(8,128)(2,1)} %bitcast.13), custom_call_target="tpu_custom_call" | custom-call | tf_op jit(solution)/shard_map/split/pallas_call | solution.py:99
  9.0 0.0 copy-start
  9.0 0.0 copy-start.1
  9.0 0.0 copy-start.3
  9.0 3.8 %all-to-all-start = ((bf16[4,112,3584]{2,1,0:T(8,128)(2,1)}), bf16[4,112,3584]{2,1,0:T(8,128)(2,1)S(1)}, u32[]{:S(2)}, u32[]{:S(2)}) async-start(bf16[4,112,3584]{2,1,0:T(8,128)(2,1)} %split.1), calls=%async_computation | async-start | bytes 6422528 | tf_op jit(solution)/shard_map/all_to_all | solution.py:275
  12.9 0.1 pack.1
  13.1 44.8 %all-gather.4 = f16[3712,256]{1,0:T(8,128)(2,1)} all-gather(f16[232,256]{1,0:T(8,128)(2,1)S(1)} %convert_element_type.12), channel_id=2, replica_groups=mesh['s'=2,'y'=4,'c'=2,'x'=2,'z'=16] {'z'}, dimensions={0}, use_global_device_ids=true | all-gather | bytes 2019328 | tf_op jit(solution)/shard_map/all_gather | solution.py:265
  57.9 8.6 %collective-permute-start.1 = (bf16[4,112,3584]{2,1,0:T(8,128)(2,1)S(1)}, bf16[4,112,3584]{2,1,0:T(8,128)(2,1)S(1)}, u32[]{:S(2)}, u32[]{:S(2)}) collective-permute-start(bf16[4,112,3584]{2,1,0:T(8,128)(2,1)S(1)} %all-to-all-done.half_ref), channel_id=1, source_target_pairs={{0,32},{32,0},{1,33},{33,1},{2,34},{34,2},{3,35},{35,3},{4,36},{36... | collective-permute-start | bytes 9633800 | tf_op jit(solution)/shard_map/ppermute | solution.py:261
  66.5 1.8 %convert_element_type.13.same_ref = bf16[16,232,256]{2,1,0:T(8,128)(2,1)S(1)} convert(f16[16,232,256]{2,1,0:T(8,128)(2,1)} %bitcast.12) | non-fusion elementwise | flops 950272 | bytes 3801088 | tf_op jit(solution)/shard_map/convert_element_type | solution.py:280
  68.3 3.5 %collective-permute-done.1.half2_ref = bf16[4,112,3584]{2,1,0:T(8,128)(2,1)S(1)} collective-permute-done((bf16[4,112,3584]{2,1,0:T(8,128)(2,1)S(1)}, bf16[4,112,3584]{2,1,0:T(8,128)(2,1)S(1)}, u32[]{:S(2)}, u32[]{:S(2)}) %collective-permute-start.1) | collective-permute-done | bytes 3211296 | tf_op jit(solution)/shard_map/ppermute | solution.py:261
  71.8 1.5 product.2
  73.3 3.1 %collective-permute-start.2 = (bf16[232,256]{1,0:T(8,128)(2,1)S(1)}, bf16[232,256]{1,0:T(8,128)(2,1)S(1)}, u32[]{:S(2)}, u32[]{:S(2)}) collective-permute-start(bf16[232,256]{1,0:T(8,128)(2,1)S(1)} %get-tuple-element.20), channel_id=1, source_target_pairs={{0,16},{16,0},{1,17},{17,1},{2,18},{18,2},{3,19},{19,3},{4,20},{20... | collective-permute-start | bytes 356360 | tf_op jit(solution)/shard_map/ppermute | solution.py:261
  76.4 3.2 %collective-permute-done.2.other_ref = bf16[232,256]{1,0:T(8,128)(2,1)S(1)} collective-permute-done((bf16[232,256]{1,0:T(8,128)(2,1)S(1)}, bf16[232,256]{1,0:T(8,128)(2,1)S(1)}, u32[]{:S(2)}, u32[]{:S(2)}) %collective-permute-start.2) | collective-permute-done | bytes 118816 | tf_op jit(solution)/shard_map/ppermute | solution.py:261
  79.6 0.2 middle.1
  79.9 31.9 %all-gather.5 = f16[3712,256]{1,0:T(8,128)(2,1)S(1)} all-gather(f16[232,256]{1,0:T(8,128)(2,1)S(1)} %convert_element_type.14), channel_id=3, replica_groups=mesh['s'=2,'y'=4,'c'=2,'x'=2,'z'=16] {'z'}, dimensions={0}, use_global_device_ids=true | all-gather | bytes 2019328 | tf_op jit(solution)/shard_map/all_gather | solution.py:265
  111.8 0.4 convert_element_type.16
  112.2 0.0 copy-start.8
  112.2 0.0 copy-start.6
  112.3 0.0 copy-start.7
  112.3 1.5 product.3
  113.8 3.1 %collective-permute-start.3 = (bf16[232,256]{1,0:T(8,128)(2,1)S(1)}, bf16[232,256]{1,0:T(8,128)(2,1)S(1)}, u32[]{:S(2)}, u32[]{:S(2)}) collective-permute-start(bf16[232,256]{1,0:T(8,128)(2,1)S(1)} %get-tuple-element.24), channel_id=1, source_target_pairs={{0,16},{16,0},{1,17},{17,1},{2,18},{18,2},{3,19},{19,3},{4,20},{20... | collective-permute-start | bytes 356360 | tf_op jit(solution)/shard_map/ppermute | solution.py:261
  116.9 2.4 %collective-permute-done.3.other_ref = bf16[232,256]{1,0:T(8,128)(2,1)S(1)} collective-permute-done((bf16[232,256]{1,0:T(8,128)(2,1)S(1)}, bf16[232,256]{1,0:T(8,128)(2,1)S(1)}, u32[]{:S(2)}, u32[]{:S(2)}) %collective-permute-start.3) | collective-permute-done | bytes 118816 | tf_op jit(solution)/shard_map/ppermute | solution.py:261
  119.3 0.9 last.1
  120.2 8.3 %all-to-all-start.1 = ((f32[32,2,256]{2,1,0:T(2,128)}), f32[32,2,256]{2,1,0:T(2,128)S(1)}, u32[]{:S(2)}, u32[]{:S(2)}) async-start(f32[32,2,256]{2,1,0:T(2,128)} %get-tuple-element.27), calls=%async_computation.1 | async-start | bytes 131072 | tf_op jit(solution)/shard_map/all_to_all | solution.py:289
  128.5 4.6 %collective-permute-start.4 = (bf16[224,256]{1,0:T(8,128)(2,1)S(1)}, bf16[224,256]{1,0:T(8,128)(2,1)S(1)}, u32[]{:S(2)}, u32[]{:S(2)}) collective-permute-start(bf16[224,256]{1,0:T(8,128)(2,1)S(1)} %get-tuple-element.25), channel_id=1, source_target_pairs={{0,256},{256,0},{1,257},{257,1},{2,258},{258,2},{3,259},{259,3},{4... | collective-permute-start | bytes 344072 | tf_op jit(solution)/shard_map/ppermute | solution.py:261
  133.2 8.6 %all-to-all-done.1.stats_ref = f32[32,2,256]{2,1,0:T(2,128)S(1)} async-done(((f32[32,2,256]{2,1,0:T(2,128)}), f32[32,2,256]{2,1,0:T(2,128)S(1)}, u32[]{:S(2)}, u32[]{:S(2)}) %all-to-all-start.1) | async-done | bytes 65568 | tf_op jit(solution)/shard_map/all_to_all | solution.py:289
  141.8 0.7 loss_parts.1
  142.5 17.2 %all-to-all-start.2 = ((f32[16,2,128]{2,1,0:T(2,128)}), f32[16,2,128]{2,1,0:T(2,128)S(1)}, u32[]{:S(2)}, u32[]{:S(2)}) async-start(f32[16,2,128]{2,1,0:T(2,128)} %loss_parts.1), calls=%async_computation.2 | async-start | bytes 32768 | tf_op jit(solution)/shard_map/all_to_all | solution.py:291
  159.7 0.7 maximum_select_fusion
  160.5 6.6 %all-to-all-done.2 = f32[16,2,128]{2,1,0:T(2,128)S(1)} async-done(((f32[16,2,128]{2,1,0:T(2,128)}), f32[16,2,128]{2,1,0:T(2,128)S(1)}, u32[]{:S(2)}, u32[]{:S(2)}) %all-to-all-start.2) | async-done | bytes 16416 | tf_op jit(solution)/shard_map/all_to_all | solution.py:291
  167.0 0.6 fusion
  (22 shorter events, 0.1 us)
Async XLA Ops:
  0.6 8.4 %collective-permute-start = (bf16[1,224]{1,0:T(2,128)(2,1)}, bf16[1,224]{1,0:T(2,128)(2,1)S(1)}, u32[]{:S(2)}, u32[]{:S(2)}) collective-permute-start(bf16[1,224]{1,0:T(2,128)(2,1)} %here_ref.3), channel_id=1, source_target_pairs={{0,256},{256,0},{1,257},{257,1},{2,258},{258,2},{3,259},{259,3},{4... | collective-permute-start | bytes 1352 | tf_op jit(solution)/shard_map/ppermute | solution.py:261
  9.0 3.9 %copy-start = (bf16[2,224,256]{2,1,0:T(8,128)(2,1)S(1)}, bf16[2,224,256]{2,1,0:T(8,128)(2,1)}, u32[]{:S(2)}) copy-start(bf16[2,224,256]{2,1,0:T(8,128)(2,1)} %tokens_ref.3) | copy-start | bytes 688132
  9.0 3.9 %copy-start.1 = (bf16[1,224]{1,0:T(2,128)(2,1)S(1)}, bf16[1,224]{1,0:T(2,128)(2,1)}, u32[]{:S(2)}) copy-start(bf16[1,224]{1,0:T(2,128)(2,1)} %here_ref.3) | copy-start | bytes 1348
  9.0 3.9 %copy-start.3 = (bf16[1,224]{1,0:T(2,128)(2,1)}, bf16[1,224]{1,0:T(2,128)(2,1)S(1)}, u32[]{:S(2)}) copy-start(bf16[1,224]{1,0:T(2,128)(2,1)S(1)} %collective-permute-done.away_ref) | copy-start | bytes 1348
  9.0 48.9 %all-to-all-start = ((bf16[4,112,3584]{2,1,0:T(8,128)(2,1)}), bf16[4,112,3584]{2,1,0:T(8,128)(2,1)S(1)}, u32[]{:S(2)}, u32[]{:S(2)}) async-start(bf16[4,112,3584]{2,1,0:T(8,128)(2,1)} %split.1), calls=%async_computation | async-start | bytes 6422528 | tf_op jit(solution)/shard_map/all_to_all | solution.py:275
  57.9 13.9 %collective-permute-start.1 = (bf16[4,112,3584]{2,1,0:T(8,128)(2,1)S(1)}, bf16[4,112,3584]{2,1,0:T(8,128)(2,1)S(1)}, u32[]{:S(2)}, u32[]{:S(2)}) collective-permute-start(bf16[4,112,3584]{2,1,0:T(8,128)(2,1)S(1)} %all-to-all-done.half_ref), channel_id=1, source_target_pairs={{0,32},{32,0},{1,33},{33,1},{2,34},{34,2},{3,35},{35,3},{4,36},{36... | collective-permute-start | bytes 9633800 | tf_op jit(solution)/shard_map/ppermute | solution.py:261
  68.3 11.3 %copy-start.2 = (bf16[1,224]{1,0:T(2,128)(2,1)S(1)}, bf16[1,224]{1,0:T(2,128)(2,1)}, u32[]{:S(2)}) copy-start(bf16[1,224]{1,0:T(2,128)(2,1)} %here_ref.3) | copy-start | bytes 1348
  68.3 11.3 %copy-start.4 = (bf16[1,224]{1,0:T(2,128)(2,1)S(1)}, bf16[1,224]{1,0:T(2,128)(2,1)}, u32[]{:S(2)}) copy-start(bf16[1,224]{1,0:T(2,128)(2,1)} %copy-done.3) | copy-start | bytes 1348
  73.3 6.3 %collective-permute-start.2 = (bf16[232,256]{1,0:T(8,128)(2,1)S(1)}, bf16[232,256]{1,0:T(8,128)(2,1)S(1)}, u32[]{:S(2)}, u32[]{:S(2)}) collective-permute-start(bf16[232,256]{1,0:T(8,128)(2,1)S(1)} %get-tuple-element.20), channel_id=1, source_target_pairs={{0,16},{16,0},{1,17},{17,1},{2,18},{18,2},{3,19},{19,3},{4,20},{20... | collective-permute-start | bytes 356360 | tf_op jit(solution)/shard_map/ppermute | solution.py:261
  112.2 4.7 %copy-start.8 = (bf16[224]{0:T(256)(128)(2,1)S(1)}, bf16[224]{0:T(256)(128)(2,1)}, u32[]{:S(2)}) copy-start(bf16[224]{0:T(256)(128)(2,1)} %param.11) | copy-start | bytes 1348
  112.2 4.7 %copy-start.9 = (bf16[224]{0:T(256)(128)(2,1)S(1)}, bf16[224]{0:T(256)(128)(2,1)}, u32[]{:S(2)}) copy-start(bf16[224]{0:T(256)(128)(2,1)} %param.12) | copy-start | bytes 1348
  112.2 29.5 %copy-start.5 = (s32[2,256]{1,0:T(2,128)S(1)}, s32[2,256]{1,0:T(2,128)}, u32[]{:S(2)}) copy-start(s32[2,256]{1,0:T(2,128)} %label_ref.1) | copy-start | bytes 6148
  112.2 29.5 %copy-start.6 = (s32[2,256]{1,0:T(2,128)S(1)}, s32[2,256]{1,0:T(2,128)}, u32[]{:S(2)}) copy-start(s32[2,256]{1,0:T(2,128)} %mask_ref.1) | copy-start | bytes 6148
  112.3 29.5 %copy-start.7 = (s32[2,256]{1,0:T(2,128)S(1)}, s32[2,256]{1,0:T(2,128)}, u32[]{:S(2)}) copy-start(s32[2,256]{1,0:T(2,128)} %segment_ref.1) | copy-start | bytes 6148
  113.8 5.6 %collective-permute-start.3 = (bf16[232,256]{1,0:T(8,128)(2,1)S(1)}, bf16[232,256]{1,0:T(8,128)(2,1)S(1)}, u32[]{:S(2)}, u32[]{:S(2)}) collective-permute-start(bf16[232,256]{1,0:T(8,128)(2,1)S(1)} %get-tuple-element.24), channel_id=1, source_target_pairs={{0,16},{16,0},{1,17},{17,1},{2,18},{18,2},{3,19},{19,3},{4,20},{20... | collective-permute-start | bytes 356360 | tf_op jit(solution)/shard_map/ppermute | solution.py:261
  120.2 21.5 %all-to-all-start.1 = ((f32[32,2,256]{2,1,0:T(2,128)}), f32[32,2,256]{2,1,0:T(2,128)S(1)}, u32[]{:S(2)}, u32[]{:S(2)}) async-start(f32[32,2,256]{2,1,0:T(2,128)} %get-tuple-element.27), calls=%async_computation.1 | async-start | bytes 131072 | tf_op jit(solution)/shard_map/all_to_all | solution.py:289
  128.5 31.2 %collective-permute-start.4 = (bf16[224,256]{1,0:T(8,128)(2,1)S(1)}, bf16[224,256]{1,0:T(8,128)(2,1)S(1)}, u32[]{:S(2)}, u32[]{:S(2)}) collective-permute-start(bf16[224,256]{1,0:T(8,128)(2,1)S(1)} %get-tuple-element.25), channel_id=1, source_target_pairs={{0,256},{256,0},{1,257},{257,1},{2,258},{258,2},{3,259},{259,3},{4... | collective-permute-start | bytes 344072 | tf_op jit(solution)/shard_map/ppermute | solution.py:261
  142.5 24.5 %all-to-all-start.2 = ((f32[16,2,128]{2,1,0:T(2,128)}), f32[16,2,128]{2,1,0:T(2,128)S(1)}, u32[]{:S(2)}, u32[]{:S(2)}) async-start(f32[16,2,128]{2,1,0:T(2,128)} %loss_parts.1), calls=%async_computation.2 | async-start | bytes 32768 | tf_op jit(solution)/shard_map/all_to_all | solution.py:291

commit v6 on v5

--- a/solution.py
+++ b/solution.py
@@ -161,23 +161,24 @@
     )(same, *halves)
 
 
-def block_rows(own_ref, other_ref, rows):
-    other = jnp.sum(other_ref[F:R, :].astype(F32), axis=0, keepdims=True)
+def block_rows(own_ref, pair_ref, rows):
+    sent = pair_ref[1 - lax.axis_index("x")].astype(F32)
+    other = jnp.sum(sent[F:R], axis=0, keepdims=True)
     inv_root = lax.rsqrt((own_ref[F:F + 1, :] + other) / D + EPS) / SCALE
-    mixed = (own_ref[0:F, :] + other_ref[0:F, :].astype(F32)) * inv_root
+    mixed = (own_ref[0:F, :] + sent[0:F]) * inv_root
     gated = mixed / (1.0 + jnp.exp(-mixed))
     return (rows.astype(F32) + gated).astype(BF16)
 
 
-def middle_kernel(own_ref, other_ref, tokens_ref, here_ref, away_ref, out_ref, block_ref):
+def middle_kernel(own_ref, pair_ref, tokens_ref, here_ref, away_ref, out_ref, block_ref):
     section = lax.axis_index("s")
-    out = block_rows(own_ref, other_ref, tokens_ref[section])
+    out = block_rows(own_ref, pair_ref, tokens_ref[section])
     out_ref[...] = out
     gain = picked(here_ref, away_ref, section == 1)
     pack_block(out.astype(F32), gain, block_ref)
 
 
-def middle(own, other, tokens, here, away):
+def middle(own, pair, tokens, here, away):
     return call(
         middle_kernel,
         (shape((F, T), BF16), shape((R, T), BF16)),
@@ -185,13 +186,13 @@
         (vmem(), vmem()),
         SMALL,
         "middle",
-    )(own, other, tokens, here, away)
+    )(own, pair, tokens, here, away)
 
 
 def last_kernel(
-    own_ref, other_ref, rows_ref, gain_ref, score_ref, out_ref, swap_ref, stats_ref
+    own_ref, pair_ref, rows_ref, gain_ref, score_ref, out_ref, swap_ref, stats_ref
 ):
-    out = block_rows(own_ref, other_ref, rows_ref[...])
+    out = block_rows(own_ref, pair_ref, rows_ref[...])
     out_ref[...] = out
     section = lax.axis_index("s")
 
@@ -212,7 +213,7 @@
         stats_ref[i] = stats
 
 
-def last(own, other, rows, gain, score):
+def last(own, pair, rows, gain, score):
     out = shape((F, T), BF16)
     return call(
         last_kernel,
@@ -221,7 +222,7 @@
         (vmem(), vmem(), vmem()),
         SMALL,
         "last",
-    )(own, other, rows, gain, score)
+    )(own, pair, rows, gain, score)
 
 
 def loss_kernel(stats_ref, label_ref, mask_ref, segment_ref, sums_ref):
@@ -261,6 +262,10 @@
     return lax.ppermute(value, name, [(i, i ^ (count - 1)) for i in range(count)])
 
 
+def both(sent):
+    return lax.all_gather(sent, "x", axis=0, tiled=False)
+
+
 def gathered(block):
     return lax.all_gather(block.astype(jnp.float16), "z", axis=0, tiled=False)
 
@@ -278,11 +283,11 @@
     same, half = lax.optimization_barrier((same, half))
     halves = half, swapped(half, "c")
     own, send = product(0, same.astype(BF16), halves)
-    first, block = middle(own, swapped(send, "x"), tokens_in, section_gain, gain_away)
+    first, block = middle(own, both(send), tokens_in, section_gain, gain_away)
 
     own, send = product(1, gathered(block).astype(BF16), halves)
     second, handed, stats = last(
-        own, swapped(send, "x"), first, final_gain[None], score_weight[None]
+        own, both(send), first, final_gain[None], score_weight[None]
     )
     handed = swapped(handed, "s")
 

time: 168 us -> 166 us (0.988)
  blocking collectives: 76.7 us -> 86.5 us
  starting transfers between devices: 54.3 us -> 48.1 us
  waiting for transfers between devices: 24.3 us -> 18.3 us
    all_gather x0 -> x2, blocking collectives: none -> 9.78 us  [both(): return lax.all_gather(sent, 'x', axis=0, tiled=False)]
    ppermute x5 -> x3, starting transfers between devices: 24.9 us -> 19 us  [swapped(): return lax.ppermute(value, name, [(i, i ^ count - 1) for i in range(count)])]
    ppermute x5 -> x3, waiting for transfers between devices: 9.13 us -> 3.47 us  [swapped(): return lax.ppermute(value, name, [(i, i ^ count - 1) for i in range(count)])]
  transfers between devices with their start and end apart: 8 -> 6, of which waited for: 5 -> 3; matrix products, arithmetic and copies ran while one was open for 2% -> 2% of each run, Pallas kernels for 2% -> 2%
where the time goes in v6:
time: 166 us; the launch traced here: 165 us
  blocking collectives  86.5 us (52%)
  starting transfers between devices  48.1 us (29%)
  waiting for transfers between devices  18.3 us (11%)
  Pallas kernels  7.77 us (5%)
  other arithmetic  3.49 us (2%)
    all_gather x2, blocking collectives, gathered(): return lax.all_gather(block.astype(jnp.float16), 'z', axis=0, tiled=False)  76.7 us
    ppermute x3, starting transfers between devices, swapped(): return lax.ppermute(value, name, [(i, i ^ count - 1) for i in range(count)])  19 us
    all_to_all x1, starting transfers between devices, body(): parts = lax.all_to_all(parts, ('s', 'y', 'c'), 0, 0, tiled=True)  17.3 us
    all_gather x2, blocking collectives, both(): return lax.all_gather(sent, 'x', axis=0, tiled=False)  9.78 us
    all_to_all x1, waiting for transfers between devices, body(): stats = lax.all_to_all(stats, ('x', 'z'), 0, 0, tiled=True)  8.26 us
    all_to_all x1, starting transfers between devices, body(): stats = lax.all_to_all(stats, ('x', 'z'), 0, 0, tiled=True)  7.96 us
    all_to_all x1, waiting for transfers between devices, body(): parts = lax.all_to_all(parts, ('s', 'y', 'c'), 0, 0, tiled=True)  6.56 us
    all_to_all x1, starting transfers between devices, body(): half = lax.all_to_all(pieces, ('s', 'x'), 0, 0, tiled=True)  3.85 us
  transfers between devices with their start and end apart: 6, of which 3 were waited for; matrix products, arithmetic and copies ran while one was open for 2% of the time, Pallas kernels for 2%

profile of v6, /device:TPU:1, one launch (start us, length us, event | category | flops | bytes accessed | tf_op | source)
XLA Modules:
  0.0 165.1 jit_solution(768341016221130396)
XLA Ops:
  0.6 5.5 %collective-permute-start = (bf16[1,224]{1,0:T(2,128)(2,1)}, bf16[1,224]{1,0:T(2,128)(2,1)S(1)}, u32[]{:S(2)}, u32[]{:S(2)}) collective-permute-start(bf16[1,224]{1,0:T(2,128)(2,1)} %here_ref.3), channel_id=1, source_target_pairs={{0,256},{256,0},{1,257},{257,1},{2,258},{258,2},{3,259},{259,3},{4... | collective-permute-start | bytes 1352 | tf_op jit(solution)/shard_map/ppermute | solution.py:262
  6.1 2.9 %split.1 = bf16[4,112,3584]{2,1,0:T(8,128)(2,1)} custom-call(bf16[224,7168]{1,0:T(8,128)(2,1)} %bitcast.17), custom_call_target="tpu_custom_call" | custom-call | tf_op jit(solution)/shard_map/split/pallas_call | solution.py:99
  9.0 0.0 copy-start
  9.0 0.0 copy-start.1
  9.0 0.0 copy-start.8
  9.0 0.0 copy-start.9
  9.1 3.8 %all-to-all-start = ((bf16[4,112,3584]{2,1,0:T(8,128)(2,1)}), bf16[4,112,3584]{2,1,0:T(8,128)(2,1)S(1)}, u32[]{:S(2)}, u32[]{:S(2)}) async-start(bf16[4,112,3584]{2,1,0:T(8,128)(2,1)} %split.1), calls=%async_computation | async-start | bytes 6422528 | tf_op jit(solution)/shard_map/all_to_all | solution.py:280
  13.0 0.1 pack.1
  13.1 44.8 %all-gather.6 = f16[3712,256]{1,0:T(8,128)(2,1)} all-gather(f16[232,256]{1,0:T(8,128)(2,1)S(1)} %convert_element_type.12), channel_id=2, replica_groups=mesh['s'=2,'y'=4,'c'=2,'x'=2,'z'=16] {'z'}, dimensions={0}, use_global_device_ids=true | all-gather | bytes 2019328 | tf_op jit(solution)/shard_map/all_gather | solution.py:270
  57.9 8.6 %collective-permute-start.1 = (bf16[4,112,3584]{2,1,0:T(8,128)(2,1)S(1)}, bf16[4,112,3584]{2,1,0:T(8,128)(2,1)S(1)}, u32[]{:S(2)}, u32[]{:S(2)}) collective-permute-start(bf16[4,112,3584]{2,1,0:T(8,128)(2,1)S(1)} %all-to-all-done.half_ref), channel_id=1, source_target_pairs={{0,32},{32,0},{1,33},{33,1},{2,34},{34,2},{3,35},{35,3},{4,36},{36... | collective-permute-start | bytes 9633800 | tf_op jit(solution)/shard_map/ppermute | solution.py:262
  66.6 1.8 %convert_element_type.13.same_ref = bf16[16,232,256]{2,1,0:T(8,128)(2,1)S(1)} convert(f16[16,232,256]{2,1,0:T(8,128)(2,1)} %bitcast.16) | non-fusion elementwise | flops 950272 | bytes 3801088 | tf_op jit(solution)/shard_map/convert_element_type | solution.py:285
  68.4 0.0 copy-start.2
  68.4 0.0 copy-start.4
  68.4 3.5 %collective-permute-done.1.half2_ref = bf16[4,112,3584]{2,1,0:T(8,128)(2,1)S(1)} collective-permute-done((bf16[4,112,3584]{2,1,0:T(8,128)(2,1)S(1)}, bf16[4,112,3584]{2,1,0:T(8,128)(2,1)S(1)}, u32[]{:S(2)}, u32[]{:S(2)}) %collective-permute-start.1) | collective-permute-done | bytes 3211296 | tf_op jit(solution)/shard_map/ppermute | solution.py:262
  71.9 1.5 product.2
  73.3 5.1 %all-gather.1 = bf16[464,256]{1,0:T(8,128)(2,1)S(1)} all-gather(bf16[232,256]{1,0:T(8,128)(2,1)S(1)} %get-tuple-element.20), channel_id=3, replica_groups=mesh['s'=2,'y'=4,'c'=2,'x'=2,'z'=16] {'x'}, dimensions={0}, use_global_device_ids=true | all-gather | bytes 356352 | tf_op jit(solution)/shard_map/all_gather | solution.py:266
  78.5 0.2 middle.1
  78.7 31.9 %all-gather.7 = f16[3712,256]{1,0:T(8,128)(2,1)S(1)} all-gather(f16[232,256]{1,0:T(8,128)(2,1)S(1)} %convert_element_type.14), channel_id=4, replica_groups=mesh['s'=2,'y'=4,'c'=2,'x'=2,'z'=16] {'z'}, dimensions={0}, use_global_device_ids=true | all-gather | bytes 2019328 | tf_op jit(solution)/shard_map/all_gather | solution.py:270
  110.6 0.3 convert_element_type.16
  110.9 0.0 copy-start.6
  110.9 0.0 copy-start.7
  110.9 1.5 product.3
  112.4 4.7 %all-gather.3 = bf16[464,256]{1,0:T(8,128)(2,1)S(1)} all-gather(bf16[232,256]{1,0:T(8,128)(2,1)S(1)} %get-tuple-element.24), channel_id=5, replica_groups=mesh['s'=2,'y'=4,'c'=2,'x'=2,'z'=16] {'x'}, dimensions={0}, use_global_device_ids=true | all-gather | bytes 356352 | tf_op jit(solution)/shard_map/all_gather | solution.py:266
  117.1 0.9 last.1
  118.0 8.0 %all-to-all-start.1 = ((f32[32,2,256]{2,1,0:T(2,128)}), f32[32,2,256]{2,1,0:T(2,128)S(1)}, u32[]{:S(2)}, u32[]{:S(2)}) async-start(f32[32,2,256]{2,1,0:T(2,128)} %get-tuple-element.27), calls=%async_computation.1 | async-start | bytes 131072 | tf_op jit(solution)/shard_map/all_to_all | solution.py:294
  125.9 4.9 %collective-permute-start.2 = (bf16[224,256]{1,0:T(8,128)(2,1)S(1)}, bf16[224,256]{1,0:T(8,128)(2,1)S(1)}, u32[]{:S(2)}, u32[]{:S(2)}) collective-permute-start(bf16[224,256]{1,0:T(8,128)(2,1)S(1)} %get-tuple-element.25), channel_id=1, source_target_pairs={{0,256},{256,0},{1,257},{257,1},{2,258},{258,2},{3,259},{259,3},{4... | collective-permute-start | bytes 344072 | tf_op jit(solution)/shard_map/ppermute | solution.py:262
  130.9 8.3 %all-to-all-done.1.stats_ref = f32[32,2,256]{2,1,0:T(2,128)S(1)} async-done(((f32[32,2,256]{2,1,0:T(2,128)}), f32[32,2,256]{2,1,0:T(2,128)S(1)}, u32[]{:S(2)}, u32[]{:S(2)}) %all-to-all-start.1) | async-done | bytes 65568 | tf_op jit(solution)/shard_map/all_to_all | solution.py:294
  139.2 0.7 loss_parts.1
  139.9 17.3 %all-to-all-start.2 = ((f32[16,2,128]{2,1,0:T(2,128)}), f32[16,2,128]{2,1,0:T(2,128)S(1)}, u32[]{:S(2)}, u32[]{:S(2)}) async-start(f32[16,2,128]{2,1,0:T(2,128)} %loss_parts.1), calls=%async_computation.2 | async-start | bytes 32768 | tf_op jit(solution)/shard_map/all_to_all | solution.py:296
  157.2 0.7 maximum_select_fusion
  157.9 6.6 %all-to-all-done.2 = f32[16,2,128]{2,1,0:T(2,128)S(1)} async-done(((f32[16,2,128]{2,1,0:T(2,128)}), f32[16,2,128]{2,1,0:T(2,128)S(1)}, u32[]{:S(2)}, u32[]{:S(2)}) %all-to-all-start.2) | async-done | bytes 16416 | tf_op jit(solution)/shard_map/all_to_all | solution.py:296
  164.5 0.6 fusion
  (20 shorter events, 0.1 us)
Async XLA Ops:
  0.6 8.4 %collective-permute-start = (bf16[1,224]{1,0:T(2,128)(2,1)}, bf16[1,224]{1,0:T(2,128)(2,1)S(1)}, u32[]{:S(2)}, u32[]{:S(2)}) collective-permute-start(bf16[1,224]{1,0:T(2,128)(2,1)} %here_ref.3), channel_id=1, source_target_pairs={{0,256},{256,0},{1,257},{257,1},{2,258},{258,2},{3,259},{259,3},{4... | collective-permute-start | bytes 1352 | tf_op jit(solution)/shard_map/ppermute | solution.py:262
  9.0 3.9 %copy-start = (bf16[2,224,256]{2,1,0:T(8,128)(2,1)S(1)}, bf16[2,224,256]{2,1,0:T(8,128)(2,1)}, u32[]{:S(2)}) copy-start(bf16[2,224,256]{2,1,0:T(8,128)(2,1)} %tokens_ref.3) | copy-start | bytes 688132
  9.0 3.9 %copy-start.1 = (bf16[1,224]{1,0:T(2,128)(2,1)S(1)}, bf16[1,224]{1,0:T(2,128)(2,1)}, u32[]{:S(2)}) copy-start(bf16[1,224]{1,0:T(2,128)(2,1)} %here_ref.3) | copy-start | bytes 1348
  9.0 57.5 %copy-start.8 = (bf16[224]{0:T(256)(128)(2,1)S(1)}, bf16[224]{0:T(256)(128)(2,1)}, u32[]{:S(2)}) copy-start(bf16[224]{0:T(256)(128)(2,1)} %param.11) | copy-start | bytes 1348
  9.0 57.5 %copy-start.9 = (bf16[224]{0:T(256)(128)(2,1)S(1)}, bf16[224]{0:T(256)(128)(2,1)}, u32[]{:S(2)}) copy-start(bf16[224]{0:T(256)(128)(2,1)} %param.12) | copy-start | bytes 1348
  9.1 3.9 %copy-start.3 = (bf16[1,224]{1,0:T(2,128)(2,1)}, bf16[1,224]{1,0:T(2,128)(2,1)S(1)}, u32[]{:S(2)}) copy-start(bf16[1,224]{1,0:T(2,128)(2,1)S(1)} %collective-permute-done.away_ref) | copy-start | bytes 1348
  9.1 48.9 %all-to-all-start = ((bf16[4,112,3584]{2,1,0:T(8,128)(2,1)}), bf16[4,112,3584]{2,1,0:T(8,128)(2,1)S(1)}, u32[]{:S(2)}, u32[]{:S(2)}) async-start(bf16[4,112,3584]{2,1,0:T(8,128)(2,1)} %split.1), calls=%async_computation | async-start | bytes 6422528 | tf_op jit(solution)/shard_map/all_to_all | solution.py:280
  57.9 13.9 %collective-permute-start.1 = (bf16[4,112,3584]{2,1,0:T(8,128)(2,1)S(1)}, bf16[4,112,3584]{2,1,0:T(8,128)(2,1)S(1)}, u32[]{:S(2)}, u32[]{:S(2)}) collective-permute-start(bf16[4,112,3584]{2,1,0:T(8,128)(2,1)S(1)} %all-to-all-done.half_ref), channel_id=1, source_target_pairs={{0,32},{32,0},{1,33},{33,1},{2,34},{34,2},{3,35},{35,3},{4,36},{36... | collective-permute-start | bytes 9633800 | tf_op jit(solution)/shard_map/ppermute | solution.py:262
  68.4 10.1 %copy-start.2 = (bf16[1,224]{1,0:T(2,128)(2,1)S(1)}, bf16[1,224]{1,0:T(2,128)(2,1)}, u32[]{:S(2)}) copy-start(bf16[1,224]{1,0:T(2,128)(2,1)} %here_ref.3) | copy-start | bytes 1348
  68.4 10.1 %copy-start.4 = (bf16[1,224]{1,0:T(2,128)(2,1)S(1)}, bf16[1,224]{1,0:T(2,128)(2,1)}, u32[]{:S(2)}) copy-start(bf16[1,224]{1,0:T(2,128)(2,1)} %copy-done.3) | copy-start | bytes 1348
  110.9 28.2 %copy-start.5 = (s32[2,256]{1,0:T(2,128)S(1)}, s32[2,256]{1,0:T(2,128)}, u32[]{:S(2)}) copy-start(s32[2,256]{1,0:T(2,128)} %label_ref.1) | copy-start | bytes 6148
  110.9 28.2 %copy-start.6 = (s32[2,256]{1,0:T(2,128)S(1)}, s32[2,256]{1,0:T(2,128)}, u32[]{:S(2)}) copy-start(s32[2,256]{1,0:T(2,128)} %mask_ref.1) | copy-start | bytes 6148
  110.9 28.2 %copy-start.7 = (s32[2,256]{1,0:T(2,128)S(1)}, s32[2,256]{1,0:T(2,128)}, u32[]{:S(2)}) copy-start(s32[2,256]{1,0:T(2,128)} %segment_ref.1) | copy-start | bytes 6148
  118.0 21.2 %all-to-all-start.1 = ((f32[32,2,256]{2,1,0:T(2,128)}), f32[32,2,256]{2,1,0:T(2,128)S(1)}, u32[]{:S(2)}, u32[]{:S(2)}) async-start(f32[32,2,256]{2,1,0:T(2,128)} %get-tuple-element.27), calls=%async_computation.1 | async-start | bytes 131072 | tf_op jit(solution)/shard_map/all_to_all | solution.py:294
  125.9 31.2 %collective-permute-start.2 = (bf16[224,256]{1,0:T(8,128)(2,1)S(1)}, bf16[224,256]{1,0:T(8,128)(2,1)S(1)}, u32[]{:S(2)}, u32[]{:S(2)}) collective-permute-start(bf16[224,256]{1,0:T(8,128)(2,1)S(1)} %get-tuple-element.25), channel_id=1, source_target_pairs={{0,256},{256,0},{1,257},{257,1},{2,258},{258,2},{3,259},{259,3},{4... | collective-permute-start | bytes 344072 | tf_op jit(solution)/shard_map/ppermute | solution.py:262
  139.9 24.6 %all-to-all-start.2 = ((f32[16,2,128]{2,1,0:T(2,128)}), f32[16,2,128]{2,1,0:T(2,128)S(1)}, u32[]{:S(2)}, u32[]{:S(2)}) async-start(f32[16,2,128]{2,1,0:T(2,128)} %loss_parts.1), calls=%async_computation.2 | async-start | bytes 32768 | tf_op jit(solution)/shard_map/all_to_all | solution.py:296

commit v7 on v6

--- a/solution.py
+++ b/solution.py
@@ -115,7 +115,7 @@
 
 
 def product_kernel(
-    block, same_ref, half_ref, half2_ref, own_ref, send_ref, held, values, sems
+    block, same_ref, terms_ref, half_ref, half2_ref, own_ref, send_ref, held, values, sems
 ):
     core = lax.axis_index("c")
     x = lax.axis_index("x")
@@ -132,7 +132,8 @@
     for i in range(16):
         got = same_ref[i]
         values[i * F:(i + 1) * F, :] = got[0:F]
-        root = jnp.sum(got[F:R].astype(F32), axis=0, keepdims=True)
+        terms = terms_ref[...] if i == 0 else got[F:R]
+        root = jnp.sum(terms.astype(F32), axis=0, keepdims=True)
         squares += root * root
 
     for copy in copies:
@@ -145,11 +146,11 @@
     send_ref[F:R, :] = three_terms(squares)
 
 
-def product(block, same, halves):
+def product(block, same, terms, halves):
     return call(
         functools.partial(product_kernel, block),
         (shape((F + 8, T), F32), shape((R, T), BF16)),
-        [vmem(), anywhere(), anywhere()],
+        [vmem(), vmem(), anywhere(), anywhere()],
         (vmem(), vmem()),
         LARGE,
         "product",
@@ -158,7 +159,7 @@
             pltpu.VMEM((KH, T), BF16),
             pltpu.SemaphoreType.DMA((4,)),
         ],
-    )(same, *halves)
+    )(same.astype(BF16), terms.astype(BF16), *halves)
 
 
 def block_rows(own_ref, pair_ref, rows):
@@ -280,12 +281,13 @@
     half = lax.all_to_all(pieces, ("s", "x"), 0, 0, tiled=True)
 
     same = gathered(pack(tokens_in, section_gain, gain_away))
-    same, half = lax.optimization_barrier((same, half))
+    terms, half = lax.optimization_barrier((same[0, F:R], half))
     halves = half, swapped(half, "c")
-    own, send = product(0, same.astype(BF16), halves)
+    own, send = product(0, same, terms, halves)
     first, block = middle(own, both(send), tokens_in, section_gain, gain_away)
 
-    own, send = product(1, gathered(block).astype(BF16), halves)
+    same = gathered(block)
+    own, send = product(1, same, same[0, F:R], halves)
     second, handed, stats = last(
         own, both(send), first, final_gain[None], score_weight[None]
     )

time: 166 us -> 165 us (level)
  no operation moved by 1% of the time
where the time goes in v7:
time: 165 us; the launch traced here: 164 us
  blocking collectives  85 us (52%)
  starting transfers between devices  47.3 us (29%)
  waiting for transfers between devices  18.4 us (11%)
  Pallas kernels  7.76 us (5%)
  other arithmetic  3.5 us (2%)
    all_gather x2, blocking collectives, gathered(): return lax.all_gather(block.astype(jnp.float16), 'z', axis=0, tiled=False)  75.2 us
    ppermute x3, starting transfers between devices, swapped(): return lax.ppermute(value, name, [(i, i ^ count - 1) for i in range(count)])  18.3 us
    all_to_all x1, starting transfers between devices, body(): parts = lax.all_to_all(parts, ('s', 'y', 'c'), 0, 0, tiled=True)  16.9 us
    all_gather x2, blocking collectives, both(): return lax.all_gather(sent, 'x', axis=0, tiled=False)  9.78 us
    all_to_all x1, waiting for transfers between devices, body(): stats = lax.all_to_all(stats, ('x', 'z'), 0, 0, tiled=True)  8.4 us
    all_to_all x1, starting transfers between devices, body(): stats = lax.all_to_all(stats, ('x', 'z'), 0, 0, tiled=True)  8.25 us
    all_to_all x1, waiting for transfers between devices, body(): parts = lax.all_to_all(parts, ('s', 'y', 'c'), 0, 0, tiled=True)  6.56 us
    all_to_all x1, starting transfers between devices, body(): half = lax.all_to_all(pieces, ('s', 'x'), 0, 0, tiled=True)  3.85 us
  transfers between devices with their start and end apart: 6, of which 3 were waited for; matrix products, arithmetic and copies ran while one was open for 2% of the time, Pallas kernels for 2%

profile of v7, /device:TPU:1, one launch (start us, length us, event | category | flops | bytes accessed | tf_op | source)
XLA Modules:
  0.0 164.2 jit_solution(16889087123762128135)
XLA Ops:
  0.6 5.5 %collective-permute-start = (bf16[1,224]{1,0:T(2,128)(2,1)}, bf16[1,224]{1,0:T(2,128)(2,1)S(1)}, u32[]{:S(2)}, u32[]{:S(2)}) collective-permute-start(bf16[1,224]{1,0:T(2,128)(2,1)} %here_ref.3), channel_id=1, source_target_pairs={{0,256},{256,0},{1,257},{257,1},{2,258},{258,2},{3,259},{259,3},{4... | collective-permute-start | bytes 1352 | tf_op jit(solution)/shard_map/ppermute | solution.py:263
  6.1 2.9 %split.1 = bf16[4,112,3584]{2,1,0:T(8,128)(2,1)} custom-call(bf16[224,7168]{1,0:T(8,128)(2,1)} %bitcast.23), custom_call_target="tpu_custom_call" | custom-call | tf_op jit(solution)/shard_map/split/pallas_call | solution.py:99
  9.0 0.0 copy-start
  9.0 0.0 copy-start.3
  9.0 3.8 %all-to-all-start = ((bf16[4,112,3584]{2,1,0:T(8,128)(2,1)}), bf16[4,112,3584]{2,1,0:T(8,128)(2,1)S(1)}, u32[]{:S(2)}, u32[]{:S(2)}) async-start(bf16[4,112,3584]{2,1,0:T(8,128)(2,1)} %split.1), calls=%async_computation | async-start | bytes 6422528 | tf_op jit(solution)/shard_map/all_to_all | solution.py:281
  12.9 0.0 copy-start.9
  12.9 0.0 copy-start.10
  12.9 0.1 pack.1
  13.1 43.3 %all-gather.6 = f16[3712,256]{1,0:T(8,128)(2,1)S(1)} all-gather(f16[232,256]{1,0:T(8,128)(2,1)S(1)} %convert_element_type.20), channel_id=2, replica_groups=mesh['s'=2,'y'=4,'c'=2,'x'=2,'z'=16] {'z'}, dimensions={0}, use_global_device_ids=true | all-gather | bytes 2019328 | tf_op jit(solution)/shard_map/all_gather | solution.py:271
  56.4 1.3 copy-done.8
  57.7 8.0 %collective-permute-start.1 = (bf16[4,112,3584]{2,1,0:T(8,128)(2,1)S(1)}, bf16[4,112,3584]{2,1,0:T(8,128)(2,1)S(1)}, u32[]{:S(2)}, u32[]{:S(2)}) collective-permute-start(bf16[4,112,3584]{2,1,0:T(8,128)(2,1)S(1)} %all-to-all-done.half_ref), channel_id=1, source_target_pairs={{0,32},{32,0},{1,33},{33,1},{2,34},{34,2},{3,35},{35,3},{4,36},{36... | collective-permute-start | bytes 9633800 | tf_op jit(solution)/shard_map/ppermute | solution.py:263
  65.7 1.8 %convert_element_type.21.same_ref = bf16[16,232,256]{2,1,0:T(8,128)(2,1)S(1)} convert(f16[16,232,256]{2,1,0:T(8,128)(2,1)} %bitcast.20) | non-fusion elementwise | flops 950272 | bytes 3801088 | tf_op jit(solution)/shard_map/convert_element_type | solution.py:162
  67.6 0.0 copy-start.2
  67.6 0.0 copy-start.4
  67.6 3.4 %collective-permute-done.1.half2_ref = bf16[4,112,3584]{2,1,0:T(8,128)(2,1)S(1)} collective-permute-done((bf16[4,112,3584]{2,1,0:T(8,128)(2,1)S(1)}, bf16[4,112,3584]{2,1,0:T(8,128)(2,1)S(1)}, u32[]{:S(2)}, u32[]{:S(2)}) %collective-permute-start.1) | collective-permute-done | bytes 3211296 | tf_op jit(solution)/shard_map/ppermute | solution.py:263
  71.0 1.5 product.2
  72.5 5.1 %all-gather.1 = bf16[464,256]{1,0:T(8,128)(2,1)S(1)} all-gather(bf16[232,256]{1,0:T(8,128)(2,1)S(1)} %get-tuple-element.20), channel_id=3, replica_groups=mesh['s'=2,'y'=4,'c'=2,'x'=2,'z'=16] {'x'}, dimensions={0}, use_global_device_ids=true | all-gather | bytes 356352 | tf_op jit(solution)/shard_map/all_gather | solution.py:267
  77.6 0.2 middle.1
  77.9 31.9 %all-gather.7 = f16[3712,256]{1,0:T(8,128)(2,1)S(1)} all-gather(f16[232,256]{1,0:T(8,128)(2,1)S(1)} %convert_element_type.23), channel_id=4, replica_groups=mesh['s'=2,'y'=4,'c'=2,'x'=2,'z'=16] {'z'}, dimensions={0}, use_global_device_ids=true | all-gather | bytes 2019328 | tf_op jit(solution)/shard_map/all_gather | solution.py:271
  109.8 0.3 convert_element_type.24.same_ref
  110.1 0.0 copy-start.6
  110.1 1.5 product.3
  111.6 4.7 %all-gather.3 = bf16[464,256]{1,0:T(8,128)(2,1)S(1)} all-gather(bf16[232,256]{1,0:T(8,128)(2,1)S(1)} %get-tuple-element.24), channel_id=5, replica_groups=mesh['s'=2,'y'=4,'c'=2,'x'=2,'z'=16] {'x'}, dimensions={0}, use_global_device_ids=true | all-gather | bytes 356352 | tf_op jit(solution)/shard_map/all_gather | solution.py:267
  116.3 0.9 last.1
  117.2 8.3 %all-to-all-start.1 = ((f32[32,2,256]{2,1,0:T(2,128)}), f32[32,2,256]{2,1,0:T(2,128)S(1)}, u32[]{:S(2)}, u32[]{:S(2)}) async-start(f32[32,2,256]{2,1,0:T(2,128)} %get-tuple-element.27), calls=%async_computation.1 | async-start | bytes 131072 | tf_op jit(solution)/shard_map/all_to_all | solution.py:296
  125.4 4.8 %collective-permute-start.2 = (bf16[224,256]{1,0:T(8,128)(2,1)S(1)}, bf16[224,256]{1,0:T(8,128)(2,1)S(1)}, u32[]{:S(2)}, u32[]{:S(2)}) collective-permute-start(bf16[224,256]{1,0:T(8,128)(2,1)S(1)} %get-tuple-element.25), channel_id=1, source_target_pairs={{0,256},{256,0},{1,257},{257,1},{2,258},{258,2},{3,259},{259,3},{4... | collective-permute-start | bytes 344072 | tf_op jit(solution)/shard_map/ppermute | solution.py:263
  130.2 8.4 %all-to-all-done.1.stats_ref = f32[32,2,256]{2,1,0:T(2,128)S(1)} async-done(((f32[32,2,256]{2,1,0:T(2,128)}), f32[32,2,256]{2,1,0:T(2,128)S(1)}, u32[]{:S(2)}, u32[]{:S(2)}) %all-to-all-start.1) | async-done | bytes 65568 | tf_op jit(solution)/shard_map/all_to_all | solution.py:296
  138.7 0.8 loss_parts.1
  139.4 16.9 %all-to-all-start.2 = ((f32[16,2,128]{2,1,0:T(2,128)}), f32[16,2,128]{2,1,0:T(2,128)S(1)}, u32[]{:S(2)}, u32[]{:S(2)}) async-start(f32[16,2,128]{2,1,0:T(2,128)} %loss_parts.1), calls=%async_computation.2 | async-start | bytes 32768 | tf_op jit(solution)/shard_map/all_to_all | solution.py:298
  156.3 0.7 maximum_select_fusion
  157.0 6.6 %all-to-all-done.2 = f32[16,2,128]{2,1,0:T(2,128)S(1)} async-done(((f32[16,2,128]{2,1,0:T(2,128)}), f32[16,2,128]{2,1,0:T(2,128)S(1)}, u32[]{:S(2)}, u32[]{:S(2)}) %all-to-all-start.2) | async-done | bytes 16416 | tf_op jit(solution)/shard_map/all_to_all | solution.py:298
  163.6 0.6 fusion.1
  (25 shorter events, 0.1 us)
Async XLA Ops:
  0.6 8.4 %collective-permute-start = (bf16[1,224]{1,0:T(2,128)(2,1)}, bf16[1,224]{1,0:T(2,128)(2,1)S(1)}, u32[]{:S(2)}, u32[]{:S(2)}) collective-permute-start(bf16[1,224]{1,0:T(2,128)(2,1)} %here_ref.3), channel_id=1, source_target_pairs={{0,256},{256,0},{1,257},{257,1},{2,258},{258,2},{3,259},{259,3},{4... | collective-permute-start | bytes 1352 | tf_op jit(solution)/shard_map/ppermute | solution.py:263
  9.0 3.9 %copy-start = (bf16[2,224,256]{2,1,0:T(8,128)(2,1)S(1)}, bf16[2,224,256]{2,1,0:T(8,128)(2,1)}, u32[]{:S(2)}) copy-start(bf16[2,224,256]{2,1,0:T(8,128)(2,1)} %tokens_ref.3) | copy-start | bytes 688132
  9.0 3.9 %copy-start.1 = (bf16[1,224]{1,0:T(2,128)(2,1)S(1)}, bf16[1,224]{1,0:T(2,128)(2,1)}, u32[]{:S(2)}) copy-start(bf16[1,224]{1,0:T(2,128)(2,1)} %here_ref.3) | copy-start | bytes 1348
  9.0 3.9 %copy-start.3 = (bf16[1,224]{1,0:T(2,128)(2,1)}, bf16[1,224]{1,0:T(2,128)(2,1)S(1)}, u32[]{:S(2)}) copy-start(bf16[1,224]{1,0:T(2,128)(2,1)S(1)} %collective-permute-done.away_ref) | copy-start | bytes 1348
  9.0 48.6 %all-to-all-start = ((bf16[4,112,3584]{2,1,0:T(8,128)(2,1)}), bf16[4,112,3584]{2,1,0:T(8,128)(2,1)S(1)}, u32[]{:S(2)}, u32[]{:S(2)}) async-start(bf16[4,112,3584]{2,1,0:T(8,128)(2,1)} %split.1), calls=%async_computation | async-start | bytes 6422528 | tf_op jit(solution)/shard_map/all_to_all | solution.py:281
  12.9 52.8 %copy-start.9 = (bf16[224]{0:T(256)(128)(2,1)S(1)}, bf16[224]{0:T(256)(128)(2,1)}, u32[]{:S(2)}) copy-start(bf16[224]{0:T(256)(128)(2,1)} %param.11) | copy-start | bytes 1348
  12.9 52.8 %copy-start.10 = (bf16[224]{0:T(256)(128)(2,1)S(1)}, bf16[224]{0:T(256)(128)(2,1)}, u32[]{:S(2)}) copy-start(bf16[224]{0:T(256)(128)(2,1)} %param.12) | copy-start | bytes 1348
  56.4 1.3 copy-start.8
  57.7 13.4 %collective-permute-start.1 = (bf16[4,112,3584]{2,1,0:T(8,128)(2,1)S(1)}, bf16[4,112,3584]{2,1,0:T(8,128)(2,1)S(1)}, u32[]{:S(2)}, u32[]{:S(2)}) collective-permute-start(bf16[4,112,3584]{2,1,0:T(8,128)(2,1)S(1)} %all-to-all-done.half_ref), channel_id=1, source_target_pairs={{0,32},{32,0},{1,33},{33,1},{2,34},{34,2},{3,35},{35,3},{4,36},{36... | collective-permute-start | bytes 9633800 | tf_op jit(solution)/shard_map/ppermute | solution.py:263
  67.6 10.1 %copy-start.2 = (bf16[1,224]{1,0:T(2,128)(2,1)S(1)}, bf16[1,224]{1,0:T(2,128)(2,1)}, u32[]{:S(2)}) copy-start(bf16[1,224]{1,0:T(2,128)(2,1)} %here_ref.3) | copy-start | bytes 1348
  67.6 10.1 %copy-start.4 = (bf16[1,224]{1,0:T(2,128)(2,1)S(1)}, bf16[1,224]{1,0:T(2,128)(2,1)}, u32[]{:S(2)}) copy-start(bf16[1,224]{1,0:T(2,128)(2,1)} %copy-done.3) | copy-start | bytes 1348
  110.1 28.5 %copy-start.5 = (s32[2,256]{1,0:T(2,128)S(1)}, s32[2,256]{1,0:T(2,128)}, u32[]{:S(2)}) copy-start(s32[2,256]{1,0:T(2,128)} %label_ref.1) | copy-start | bytes 6148
  110.1 28.5 %copy-start.6 = (s32[2,256]{1,0:T(2,128)S(1)}, s32[2,256]{1,0:T(2,128)}, u32[]{:S(2)}) copy-start(s32[2,256]{1,0:T(2,128)} %mask_ref.1) | copy-start | bytes 6148
  110.1 28.5 %copy-start.7 = (s32[2,256]{1,0:T(2,128)S(1)}, s32[2,256]{1,0:T(2,128)}, u32[]{:S(2)}) copy-start(s32[2,256]{1,0:T(2,128)} %segment_ref.1) | copy-start | bytes 6148
  117.2 21.5 %all-to-all-start.1 = ((f32[32,2,256]{2,1,0:T(2,128)}), f32[32,2,256]{2,1,0:T(2,128)S(1)}, u32[]{:S(2)}, u32[]{:S(2)}) async-start(f32[32,2,256]{2,1,0:T(2,128)} %get-tuple-element.27), calls=%async_computation.1 | async-start | bytes 131072 | tf_op jit(solution)/shard_map/all_to_all | solution.py:296
  125.4 30.9 %collective-permute-start.2 = (bf16[224,256]{1,0:T(8,128)(2,1)S(1)}, bf16[224,256]{1,0:T(8,128)(2,1)S(1)}, u32[]{:S(2)}, u32[]{:S(2)}) collective-permute-start(bf16[224,256]{1,0:T(8,128)(2,1)S(1)} %get-tuple-element.25), channel_id=1, source_target_pairs={{0,256},{256,0},{1,257},{257,1},{2,258},{258,2},{3,259},{259,3},{4... | collective-permute-start | bytes 344072 | tf_op jit(solution)/shard_map/ppermute | solution.py:263
  139.4 24.2 %all-to-all-start.2 = ((f32[16,2,128]{2,1,0:T(2,128)}), f32[16,2,128]{2,1,0:T(2,128)S(1)}, u32[]{:S(2)}, u32[]{:S(2)}) async-start(f32[16,2,128]{2,1,0:T(2,128)} %loss_parts.1), calls=%async_computation.2 | async-start | bytes 32768 | tf_op jit(solution)/shard_map/all_to_all | solution.py:298

commit v8 on v7

--- a/solution.py
+++ b/solution.py
@@ -1,5 +1,3 @@
-import functools
-
 import jax
 import jax.numpy as jnp
 from jax import lax
@@ -115,14 +113,14 @@
 
 
 def product_kernel(
-    block, same_ref, terms_ref, half_ref, half2_ref, own_ref, send_ref, held, values, sems
+    same_ref, terms_ref, half_ref, half2_ref, own_ref, send_ref, held, values, sems
 ):
     core = lax.axis_index("c")
     x = lax.axis_index("x")
     copies = []
     for i in range(4):
         ref, half = (half_ref, core) if i % 2 == 0 else (half2_ref, 1 - core)
-        index, start = (2 * block + x, 0) if i < 2 else (2 * block + 1 - x, F)
+        index, start = (x, 0) if i < 2 else (1 - x, F)
         rows = pl.ds(pl.multiple_of(start + half * HALF, 16), HALF)
         copies.append(pltpu.make_async_copy(ref.at[index], held.at[rows, :], sems.at[i]))
     for copy in copies:
@@ -146,9 +144,28 @@
     send_ref[F:R, :] = three_terms(squares)
 
 
-def product(block, same, terms, halves):
-    return call(
-        functools.partial(product_kernel, block),
+def parted_kernel(both_ref, first_ref, second_ref, sems):
+    copies = [
+        pltpu.make_async_copy(both_ref.at[0:2], first_ref, sems.at[0]),
+        pltpu.make_async_copy(both_ref.at[2:4], second_ref, sems.at[1]),
+    ]
+    for copy in copies:
+        copy.start()
+    for copy in copies:
+        copy.wait()
+
+
+def parted(both):
+    out = shape((2, HALF, KH), BF16)
+    return call(
+        parted_kernel, (out, out), [anywhere()], (vmem(), vmem()), SMALL, "parted",
+        [pltpu.SemaphoreType.DMA((2,))],
+    )(both)
+
+
+def product(same, terms, halves):
+    return call(
+        product_kernel,
         (shape((F + 8, T), F32), shape((R, T), BF16)),
         [vmem(), vmem(), anywhere(), anywhere()],
         (vmem(), vmem()),
@@ -282,12 +299,13 @@
 
     same = gathered(pack(tokens_in, section_gain, gain_away))
     terms, half = lax.optimization_barrier((same[0, F:R], half))
-    halves = half, swapped(half, "c")
-    own, send = product(0, same, terms, halves)
+    near, away = parted(half)
+    near2, away2 = swapped(near, "c"), swapped(away, "c")
+    own, send = product(same, terms, (near, near2))
     first, block = middle(own, both(send), tokens_in, section_gain, gain_away)
 
     same = gathered(block)
-    own, send = product(1, same, same[0, F:R], halves)
+    own, send = product(same, same[0, F:R], (away, away2))
     second, handed, stats = last(
         own, both(send), first, final_gain[None], score_weight[None]
     )

time: 165 us -> 163 us (0.988)
  waiting for transfers between devices: 18.4 us -> 15.6 us
  starting transfers between devices: 47.3 us -> 49.4 us
    ppermute x3 -> x4, waiting for transfers between devices: 3.45 us -> 0.69 us  [swapped(): return lax.ppermute(value, name, [(i, i ^ count - 1) for i in range(count)])]
    ppermute x3 -> x4, starting transfers between devices: 18.3 us -> 20.4 us  [swapped(): return lax.ppermute(value, name, [(i, i ^ count - 1) for i in range(count)])]
  transfers between devices with their start and end apart: 6 -> 7, of which waited for: 3 -> 3; matrix products, arithmetic and copies ran while one was open for 2% -> 1% of each run, Pallas kernels for 2% -> 3%
where the time goes in v8:
time: 163 us; the launch traced here: 162 us
  blocking collectives  85 us (52%)
  starting transfers between devices  49.4 us (30%)
  waiting for transfers between devices  15.6 us (10%)
  Pallas kernels  8.08 us (5%)
  other arithmetic  2.15 us (1%)
    all_gather x2, blocking collectives, gathered(): return lax.all_gather(block.astype(jnp.float16), 'z', axis=0, tiled=False)  75.2 us
    ppermute x4, starting transfers between devices, swapped(): return lax.ppermute(value, name, [(i, i ^ count - 1) for i in range(count)])  20.4 us
    all_to_all x1, starting transfers between devices, body(): parts = lax.all_to_all(parts, ('s', 'y', 'c'), 0, 0, tiled=True)  16.9 us
    all_gather x2, blocking collectives, both(): return lax.all_gather(sent, 'x', axis=0, tiled=False)  9.78 us
    all_to_all x1, waiting for transfers between devices, body(): stats = lax.all_to_all(stats, ('x', 'z'), 0, 0, tiled=True)  8.38 us
    all_to_all x1, starting transfers between devices, body(): stats = lax.all_to_all(stats, ('x', 'z'), 0, 0, tiled=True)  8.25 us
    all_to_all x1, waiting for transfers between devices, body(): parts = lax.all_to_all(parts, ('s', 'y', 'c'), 0, 0, tiled=True)  6.56 us
    all_to_all x1, starting transfers between devices, body(): half = lax.all_to_all(pieces, ('s', 'x'), 0, 0, tiled=True)  3.85 us
  transfers between devices with their start and end apart: 7, of which 3 were waited for; matrix products, arithmetic and copies ran while one was open for 1% of the time, Pallas kernels for 3%

profile of v8, /device:TPU:1, one launch (start us, length us, event | category | flops | bytes accessed | tf_op | source)
XLA Modules:
  0.0 162.4 jit_solution(6046759403520503849)
XLA Ops:
  0.6 5.5 %collective-permute-start = (bf16[1,224]{1,0:T(2,128)(2,1)}, bf16[1,224]{1,0:T(2,128)(2,1)S(1)}, u32[]{:S(2)}, u32[]{:S(2)}) collective-permute-start(bf16[1,224]{1,0:T(2,128)(2,1)} %here_ref.3), channel_id=1, source_target_pairs={{0,256},{256,0},{1,257},{257,1},{2,258},{258,2},{3,259},{259,3},{4... | collective-permute-start | bytes 1352 | tf_op jit(solution)/shard_map/ppermute | solution.py:280
  6.1 2.9 %split.1 = bf16[4,112,3584]{2,1,0:T(8,128)(2,1)} custom-call(bf16[224,7168]{1,0:T(8,128)(2,1)} %bitcast.23), custom_call_target="tpu_custom_call" | custom-call | tf_op jit(solution)/shard_map/split/pallas_call | solution.py:97
  9.0 0.0 copy-start
  9.0 0.0 copy-start.1
  9.0 3.8 %all-to-all-start = ((bf16[4,112,3584]{2,1,0:T(8,128)(2,1)}), bf16[4,112,3584]{2,1,0:T(8,128)(2,1)S(1)}, u32[]{:S(2)}, u32[]{:S(2)}) async-start(bf16[4,112,3584]{2,1,0:T(8,128)(2,1)} %split.1), calls=%async_computation | async-start | bytes 6422528 | tf_op jit(solution)/shard_map/all_to_all | solution.py:298
  12.9 0.1 pack.1
  13.1 43.3 %all-gather.6 = f16[3712,256]{1,0:T(8,128)(2,1)S(1)} all-gather(f16[232,256]{1,0:T(8,128)(2,1)S(1)} %convert_element_type.20), channel_id=2, replica_groups=mesh['s'=2,'y'=4,'c'=2,'x'=2,'z'=16] {'z'}, dimensions={0}, use_global_device_ids=true | all-gather | bytes 2019328 | tf_op jit(solution)/shard_map/all_gather | solution.py:288
  56.3 1.3 copy-done.5
  57.6 0.3 parted.1
  57.9 8.2 %collective-permute-start.1 = (bf16[2,112,3584]{2,1,0:T(8,128)(2,1)S(1)}, bf16[2,112,3584]{2,1,0:T(8,128)(2,1)S(1)}, u32[]{:S(2)}, u32[]{:S(2)}) collective-permute-start(bf16[2,112,3584]{2,1,0:T(8,128)(2,1)S(1)} %get-tuple-element.21.half_ref), channel_id=1, source_target_pairs={{0,32},{32,0},{1,33},{33,1},{2,34},{34,2},{3,35},{35,3},{4,36},{36... | collective-permute-start | bytes 4816904 | tf_op jit(solution)/shard_map/ppermute | solution.py:280
  66.1 1.9 %collective-permute-start.2 = (bf16[2,112,3584]{2,1,0:T(8,128)(2,1)S(1)}, bf16[2,112,3584]{2,1,0:T(8,128)(2,1)S(1)}, u32[]{:S(2)}, u32[]{:S(2)}) collective-permute-start(bf16[2,112,3584]{2,1,0:T(8,128)(2,1)S(1)} %get-tuple-element.26.half_ref), channel_id=1, source_target_pairs={{0,32},{32,0},{1,33},{33,1},{2,34},{34,2},{3,35},{35,3},{4,36},{36... | collective-permute-start | bytes 4816904 | tf_op jit(solution)/shard_map/ppermute | solution.py:280
  68.1 0.4 convert_element_type.21.same_ref
  68.5 0.7 collective-permute-done.1.half2_ref
  69.2 1.5 product.2
  70.7 5.1 %all-gather.1 = bf16[464,256]{1,0:T(8,128)(2,1)S(1)} all-gather(bf16[232,256]{1,0:T(8,128)(2,1)S(1)} %get-tuple-element.23), channel_id=3, replica_groups=mesh['s'=2,'y'=4,'c'=2,'x'=2,'z'=16] {'x'}, dimensions={0}, use_global_device_ids=true | all-gather | bytes 356352 | tf_op jit(solution)/shard_map/all_gather | solution.py:284
  75.8 0.2 middle.1
  76.0 31.9 %all-gather.7 = f16[3712,256]{1,0:T(8,128)(2,1)S(1)} all-gather(f16[232,256]{1,0:T(8,128)(2,1)S(1)} %convert_element_type.23), channel_id=4, replica_groups=mesh['s'=2,'y'=4,'c'=2,'x'=2,'z'=16] {'z'}, dimensions={0}, use_global_device_ids=true | all-gather | bytes 2019328 | tf_op jit(solution)/shard_map/all_gather | solution.py:288
  107.9 0.4 convert_element_type.24.same_ref
  108.3 0.0 copy-start.2
  108.3 0.0 copy-start.3
  108.3 0.0 copy-start.4
  108.4 1.5 product.3
  109.9 4.7 %all-gather.3 = bf16[464,256]{1,0:T(8,128)(2,1)S(1)} all-gather(bf16[232,256]{1,0:T(8,128)(2,1)S(1)} %get-tuple-element.28), channel_id=5, replica_groups=mesh['s'=2,'y'=4,'c'=2,'x'=2,'z'=16] {'x'}, dimensions={0}, use_global_device_ids=true | all-gather | bytes 356352 | tf_op jit(solution)/shard_map/all_gather | solution.py:284
  114.5 0.9 last.1
  115.4 8.2 %all-to-all-start.1 = ((f32[32,2,256]{2,1,0:T(2,128)}), f32[32,2,256]{2,1,0:T(2,128)S(1)}, u32[]{:S(2)}, u32[]{:S(2)}) async-start(f32[32,2,256]{2,1,0:T(2,128)} %get-tuple-element.31), calls=%async_computation.1 | async-start | bytes 131072 | tf_op jit(solution)/shard_map/all_to_all | solution.py:314
  123.6 4.8 %collective-permute-start.3 = (bf16[224,256]{1,0:T(8,128)(2,1)S(1)}, bf16[224,256]{1,0:T(8,128)(2,1)S(1)}, u32[]{:S(2)}, u32[]{:S(2)}) collective-permute-start(bf16[224,256]{1,0:T(8,128)(2,1)S(1)} %get-tuple-element.29), channel_id=1, source_target_pairs={{0,256},{256,0},{1,257},{257,1},{2,258},{258,2},{3,259},{259,3},{4... | collective-permute-start | bytes 344072 | tf_op jit(solution)/shard_map/ppermute | solution.py:280
  128.5 8.4 %all-to-all-done.1.stats_ref = f32[32,2,256]{2,1,0:T(2,128)S(1)} async-done(((f32[32,2,256]{2,1,0:T(2,128)}), f32[32,2,256]{2,1,0:T(2,128)S(1)}, u32[]{:S(2)}, u32[]{:S(2)}) %all-to-all-start.1) | async-done | bytes 65568 | tf_op jit(solution)/shard_map/all_to_all | solution.py:314
  136.9 0.8 loss_parts.1
  137.6 16.9 %all-to-all-start.2 = ((f32[16,2,128]{2,1,0:T(2,128)}), f32[16,2,128]{2,1,0:T(2,128)S(1)}, u32[]{:S(2)}, u32[]{:S(2)}) async-start(f32[16,2,128]{2,1,0:T(2,128)} %loss_parts.1), calls=%async_computation.2 | async-start | bytes 32768 | tf_op jit(solution)/shard_map/all_to_all | solution.py:316
  154.5 0.7 maximum_select_fusion
  155.3 6.6 %all-to-all-done.2 = f32[16,2,128]{2,1,0:T(2,128)S(1)} async-done(((f32[16,2,128]{2,1,0:T(2,128)}), f32[16,2,128]{2,1,0:T(2,128)S(1)}, u32[]{:S(2)}, u32[]{:S(2)}) %all-to-all-start.2) | async-done | bytes 16416 | tf_op jit(solution)/shard_map/all_to_all | solution.py:316
  161.8 0.6 fusion.1
  (24 shorter events, 0.1 us)
Async XLA Ops:
  0.6 8.4 %collective-permute-start = (bf16[1,224]{1,0:T(2,128)(2,1)}, bf16[1,224]{1,0:T(2,128)(2,1)S(1)}, u32[]{:S(2)}, u32[]{:S(2)}) collective-permute-start(bf16[1,224]{1,0:T(2,128)(2,1)} %here_ref.3), channel_id=1, source_target_pairs={{0,256},{256,0},{1,257},{257,1},{2,258},{258,2},{3,259},{259,3},{4... | collective-permute-start | bytes 1352 | tf_op jit(solution)/shard_map/ppermute | solution.py:280
  9.0 3.9 %copy-start = (bf16[2,224,256]{2,1,0:T(8,128)(2,1)S(1)}, bf16[2,224,256]{2,1,0:T(8,128)(2,1)}, u32[]{:S(2)}) copy-start(bf16[2,224,256]{2,1,0:T(8,128)(2,1)} %tokens_ref.3) | copy-start | bytes 688132
  9.0 3.9 %copy-start.1 = (bf16[1,224]{1,0:T(2,128)(2,1)S(1)}, bf16[1,224]{1,0:T(2,128)(2,1)}, u32[]{:S(2)}) copy-start(bf16[1,224]{1,0:T(2,128)(2,1)} %here_ref.3) | copy-start | bytes 1348
  9.0 48.6 %all-to-all-start = ((bf16[4,112,3584]{2,1,0:T(8,128)(2,1)}), bf16[4,112,3584]{2,1,0:T(8,128)(2,1)S(1)}, u32[]{:S(2)}, u32[]{:S(2)}) async-start(bf16[4,112,3584]{2,1,0:T(8,128)(2,1)} %split.1), calls=%async_computation | async-start | bytes 6422528 | tf_op jit(solution)/shard_map/all_to_all | solution.py:298
  56.3 1.3 copy-start.5
  56.3 11.7 %copy-start.7 = (bf16[224]{0:T(256)(128)(2,1)S(1)}, bf16[224]{0:T(256)(128)(2,1)}, u32[]{:S(2)}) copy-start(bf16[224]{0:T(256)(128)(2,1)} %param.11) | copy-start | bytes 1348
  56.3 11.7 %copy-start.8 = (bf16[224]{0:T(256)(128)(2,1)S(1)}, bf16[224]{0:T(256)(128)(2,1)}, u32[]{:S(2)}) copy-start(bf16[224]{0:T(256)(128)(2,1)} %param.12) | copy-start | bytes 1348
  57.6 10.5 %copy-start.6 = (f16[3712,256]{1,0:T(8,128)(2,1)S(1)}, f16[3712,256]{1,0:T(8,128)(2,1)}, u32[]{:S(2)}) copy-start(f16[3712,256]{1,0:T(8,128)(2,1)} %copy-done.5) | copy-start | bytes 5701636
  57.9 11.2 %collective-permute-start.1 = (bf16[2,112,3584]{2,1,0:T(8,128)(2,1)S(1)}, bf16[2,112,3584]{2,1,0:T(8,128)(2,1)S(1)}, u32[]{:S(2)}, u32[]{:S(2)}) collective-permute-start(bf16[2,112,3584]{2,1,0:T(8,128)(2,1)S(1)} %get-tuple-element.21.half_ref), channel_id=1, source_target_pairs={{0,32},{32,0},{1,33},{33,1},{2,34},{34,2},{3,35},{35,3},{4,36},{36... | collective-permute-start | bytes 4816904 | tf_op jit(solution)/shard_map/ppermute | solution.py:280
  66.1 42.2 %collective-permute-start.2 = (bf16[2,112,3584]{2,1,0:T(8,128)(2,1)S(1)}, bf16[2,112,3584]{2,1,0:T(8,128)(2,1)S(1)}, u32[]{:S(2)}, u32[]{:S(2)}) collective-permute-start(bf16[2,112,3584]{2,1,0:T(8,128)(2,1)S(1)} %get-tuple-element.26.half_ref), channel_id=1, source_target_pairs={{0,32},{32,0},{1,33},{33,1},{2,34},{34,2},{3,35},{35,3},{4,36},{36... | collective-permute-start | bytes 4816904 | tf_op jit(solution)/shard_map/ppermute | solution.py:280
  108.3 28.5 %copy-start.2 = (s32[2,256]{1,0:T(2,128)S(1)}, s32[2,256]{1,0:T(2,128)}, u32[]{:S(2)}) copy-start(s32[2,256]{1,0:T(2,128)} %label_ref.1) | copy-start | bytes 6148
  108.3 28.5 %copy-start.3 = (s32[2,256]{1,0:T(2,128)S(1)}, s32[2,256]{1,0:T(2,128)}, u32[]{:S(2)}) copy-start(s32[2,256]{1,0:T(2,128)} %mask_ref.1) | copy-start | bytes 6148
  108.3 28.5 %copy-start.4 = (s32[2,256]{1,0:T(2,128)S(1)}, s32[2,256]{1,0:T(2,128)}, u32[]{:S(2)}) copy-start(s32[2,256]{1,0:T(2,128)} %segment_ref.1) | copy-start | bytes 6148
  115.4 21.5 %all-to-all-start.1 = ((f32[32,2,256]{2,1,0:T(2,128)}), f32[32,2,256]{2,1,0:T(2,128)S(1)}, u32[]{:S(2)}, u32[]{:S(2)}) async-start(f32[32,2,256]{2,1,0:T(2,128)} %get-tuple-element.31), calls=%async_computation.1 | async-start | bytes 131072 | tf_op jit(solution)/shard_map/all_to_all | solution.py:314
  123.6 30.9 %collective-permute-start.3 = (bf16[224,256]{1,0:T(8,128)(2,1)S(1)}, bf16[224,256]{1,0:T(8,128)(2,1)S(1)}, u32[]{:S(2)}, u32[]{:S(2)}) collective-permute-start(bf16[224,256]{1,0:T(8,128)(2,1)S(1)} %get-tuple-element.29), channel_id=1, source_target_pairs={{0,256},{256,0},{1,257},{257,1},{2,258},{258,2},{3,259},{259,3},{4... | collective-permute-start | bytes 344072 | tf_op jit(solution)/shard_map/ppermute | solution.py:280
  137.6 24.2 %all-to-all-start.2 = ((f32[16,2,128]{2,1,0:T(2,128)}), f32[16,2,128]{2,1,0:T(2,128)S(1)}, u32[]{:S(2)}, u32[]{:S(2)}) async-start(f32[16,2,128]{2,1,0:T(2,128)} %loss_parts.1), calls=%async_computation.2 | async-start | bytes 32768 | tf_op jit(solution)/shard_map/all_to_all | solution.py:316
